TPU v7x, 128 devices: a whole 4x4x4 slice. The times are simulated.
128 devices in a mesh: segment: 2 (over core), seq: 32 (over z_lo, y, x), mp: 2 (over z_hi).
Axes of the slice: x: 4, y: 4, z: 4 (z_hi: 2, z_lo: 2; z = z_hi * 2 + z_lo), core: 2. Of those that a mesh axis runs over, the one named last changes fastest.
Arguments:
- inputs: bfloat16 [65536, 512], P('seq', 'mp'), may hold values from -6 to 6
- cotangent: bfloat16 [65536, 512], P('seq', 'mp'), may hold values from -0.375 to 0.375
- gate_gain: float32 [2, 512], P('segment', 'mp'), may hold values from 0.3 to 3
- key_gain: float32 [2, 512], P('segment', 'mp'), may hold values from 0.3 to 3
- first_factor: bfloat16 [2, 256, 256, 256], P('segment', 'seq'), may hold values from -0.375 to 0.375
- second_factor: bfloat16 [2, 256, 256, 256], P('segment', 'seq'), may hold values from -0.375 to 0.375
- up_first: bfloat16 [2, 4, 128, 128], P('segment', 'mp'), may hold values from -0.5 to 0.5
- up_second: bfloat16 [2, 4, 128, 512], P('segment', 'mp'), may hold values from -0.5 to 0.5
- down_first: bfloat16 [2, 4, 512, 128], P('segment', 'mp'), may hold values from -0.25 to 0.25
- down_second_weight: bfloat16 [2, 4, 128, 128], P('segment', 'mp'), may hold values from -0.5 to 0.5
Outputs:
- grad_first: float32 [2, 256, 256, 256], P('segment', 'seq', 'mp')
- grad_second: float32 [2, 256, 256, 256], P('segment', 'seq', 'mp')
All inputs are finite; a program needn't handle non-finite values.
Results may differ from a plain program's by a relative error of at most 0.024.
Values may be sent and summed in bfloat16 or wider, within the bound.
No kernel may reach another device: no remote copies, remote signals or barrier semaphores. Data moves between devices by JAX's collectives and lax.ppermute only.
A program may use at most 128 MiB of HBM per device.

v0:
```python
import jax
import jax.numpy as jnp
from jax import lax
from jax.sharding import PartitionSpec as P


def shifted(value, axis, steps):
    count = lax.axis_size(axis)
    leading, last = (max(0, -steps), min(count, count - steps))
    return lax.ppermute(value, axis, [(source, source + steps) for source in range(leading, last)])


def sigmoid_slope(values):
    logistic = jax.nn.sigmoid(values)
    return logistic * (1.0 + values * (1.0 - logistic))


def sequence_mix(scaled, first_block, second_block):
    mixed_rows = jnp.einsum(
        "aoi,aic->aoc", first_block, scaled, preferred_element_type=jnp.float32
    ).astype(jnp.bfloat16)
    columns = lax.all_to_all(mixed_rows, "seq", split_axis=1, concat_axis=0, tiled=True)
    turned_cols = jnp.einsum(
        "boi,ibc->obc", second_block, columns, preferred_element_type=jnp.float32
    ).astype(jnp.bfloat16)
    return (lax.all_to_all(turned_cols, "seq", split_axis=0, concat_axis=1, tiled=True), columns)


def sequence_back(back_turned, mixed_cols, second_block):
    back_turned_cols = lax.all_to_all(back_turned, "seq", split_axis=1, concat_axis=0, tiled=True)
    second_grad = jnp.einsum(
        "obc,ibc->boi", back_turned_cols, mixed_cols, preferred_element_type=jnp.float32
    )
    back_mixed_cols = jnp.einsum(
        "boi,obc->ibc", second_block, back_turned_cols, preferred_element_type=jnp.float32
    ).astype(jnp.bfloat16)
    back_mixed = lax.all_to_all(back_mixed_cols, "seq", split_axis=0, concat_axis=1, tiled=True)
    return (back_mixed, second_grad)


def forward_pass(rows_in, weights, with_output):
    (
        gate_gain,
        key_gain,
        first_block,
        second_block,
        up_first,
        up_second,
        down_first,
        down_second_weight,
    ) = weights
    tokens = rows_in.shape[0]
    channels = rows_in.shape[1]
    row_blocks = first_block.shape[0]
    block_size = first_block.shape[1]
    local_blocks = up_first.shape[0]
    block_column_width = up_first.shape[1]
    total_blocks = local_blocks * lax.axis_size("mp")
    sub_width = block_column_width // total_blocks
    rows_grid = rows_in.reshape(row_blocks, block_size, channels).astype(jnp.float32)
    scaled = (rows_grid * key_gain).astype(jnp.bfloat16)
    turned, mixed_cols = sequence_mix(scaled, first_block, second_block)
    gate_pre = rows_grid * gate_gain
    hidden_rows = (rows_grid + jax.nn.silu(gate_pre) * turned.astype(jnp.float32)).astype(
        jnp.bfloat16
    )
    hidden_rows = hidden_rows.reshape(tokens, local_blocks, block_column_width)
    up_grid = up_first.reshape(local_blocks, block_column_width, total_blocks, sub_width)
    permuted = jnp.einsum(
        "tki,kijc->tjkc", hidden_rows, up_grid, preferred_element_type=jnp.float32
    ).astype(jnp.bfloat16)
    permuted = permuted.reshape(tokens, total_blocks, local_blocks * sub_width)
    gathered_in = lax.all_to_all(permuted, "mp", split_axis=1, concat_axis=2, tiled=True)
    preact = jnp.einsum("tjq,jqe->tje", gathered_in, up_second, preferred_element_type=jnp.float32)
    kept_state = (rows_grid, scaled, mixed_cols, turned, preact)
    if not with_output:
        return (None, kept_state)
    active = jax.nn.silu(preact).astype(jnp.bfloat16)
    down_grid = down_first.reshape(local_blocks, down_first.shape[1], total_blocks, sub_width)
    folded_rows = jnp.einsum(
        "tje,jemc->tmjc", active, down_grid, preferred_element_type=jnp.float32
    ).astype(jnp.bfloat16)
    folded_rows = folded_rows.reshape(tokens, total_blocks, local_blocks * sub_width)
    gathered_output = lax.all_to_all(folded_rows, "mp", split_axis=1, concat_axis=2, tiled=True)
    output_portion = jnp.einsum(
        "xds,dsl->xdl", gathered_output, down_second_weight, preferred_element_type=jnp.float32
    )
    result = (
        (hidden_rows.astype(jnp.float32) + output_portion)
        .reshape(tokens, channels)
        .astype(jnp.bfloat16)
    )
    return (result, kept_state)


def backward_pass(cot_rows, kept_state, weights):
    (
        gate_gain,
        key_gain,
        first_block,
        second_block,
        up_first,
        up_second,
        down_first,
        down_second_weight,
    ) = weights
    rows_grid, scaled, mixed_cols, turned, preact = kept_state
    tokens = cot_rows.shape[0]
    channels = cot_rows.shape[1]
    row_blocks = first_block.shape[0]
    block_size = first_block.shape[1]
    local_blocks = up_first.shape[0]
    block_column_width = up_first.shape[1]
    total_blocks = local_blocks * lax.axis_size("mp")
    sub_width = block_column_width // total_blocks
    up_grid = up_first.reshape(local_blocks, block_column_width, total_blocks, sub_width)
    down_grid = down_first.reshape(local_blocks, down_first.shape[1], total_blocks, sub_width)
    backward_folded_rows = jnp.einsum(
        "hsd,sad->hsa",
        cot_rows.reshape(tokens, local_blocks, block_column_width),
        down_second_weight,
        preferred_element_type=jnp.float32,
    ).astype(jnp.bfloat16)
    back_grid = lax.all_to_all(
        backward_folded_rows, "mp", split_axis=2, concat_axis=1, tiled=True
    ).reshape(tokens, total_blocks, local_blocks, sub_width)
    back_active = jnp.einsum(
        "tmjc,jemc->tje", back_grid, down_grid, preferred_element_type=jnp.float32
    )
    back_preact = (back_active * sigmoid_slope(preact)).astype(jnp.bfloat16)
    back_perm = jnp.einsum(
        "tje,jqe->tjq", back_preact, up_second, preferred_element_type=jnp.float32
    ).astype(jnp.bfloat16)
    back_perm_grid = lax.all_to_all(
        back_perm, "mp", split_axis=2, concat_axis=1, tiled=True
    ).reshape(tokens, total_blocks, local_blocks, sub_width)
    back_ffn = jnp.einsum(
        "tjkc,kijc->tki", back_perm_grid, up_grid, preferred_element_type=jnp.float32
    )
    back_hidden = cot_rows.astype(jnp.float32).reshape(
        row_blocks, block_size, channels
    ) + back_ffn.reshape(row_blocks, block_size, channels)
    gate_pre = rows_grid * gate_gain
    back_turned = (back_hidden * jax.nn.silu(gate_pre)).astype(jnp.bfloat16)
    back_mixed, second_grad = sequence_back(back_turned, mixed_cols, second_block)
    first_grad = jnp.einsum("aoc,aic->aoi", back_mixed, scaled, preferred_element_type=jnp.float32)
    back_scaled = jnp.einsum(
        "aoi,aoc->aic", first_block, back_mixed, preferred_element_type=jnp.float32
    )
    back_inputs = (
        back_hidden
        + back_hidden * turned.astype(jnp.float32) * sigmoid_slope(gate_pre) * gate_gain
        + back_scaled * key_gain
    )
    back_inputs = back_inputs.reshape(tokens, channels).astype(jnp.bfloat16)
    return (back_inputs, first_grad, second_grad)


def reduce_channels(first_grad, second_grad):
    totals_first, totals_second = (
        lax.psum(first_grad.astype(jnp.bfloat16), "mp").astype(jnp.float32),
        lax.psum(second_grad.astype(jnp.bfloat16), "mp").astype(jnp.float32),
    )
    half_rows = first_grad.shape[2] // lax.axis_size("mp")
    offset = lax.axis_index("mp") * half_rows
    share_first = lax.dynamic_slice_in_dim(totals_first, offset, half_rows, 2)
    share_second = lax.dynamic_slice_in_dim(totals_second, offset, half_rows, 2)
    return (share_first, share_second)


def on_device(
    inputs,
    cotangent,
    gate_gain,
    key_gain,
    first_factor,
    second_factor,
    up_first,
    up_second,
    down_first,
    down_second_weight,
):
    weights = (
        gate_gain[0],
        key_gain[0],
        first_factor[0],
        second_factor[0],
        up_first[0],
        up_second[0],
        down_first[0],
        down_second_weight[0],
    )
    early_out, early_state = forward_pass(inputs, weights, True)
    received = shifted(early_out, "segment", 1)
    unused_late, later_state = forward_pass(received, weights, False)
    is_first = lax.axis_index("segment") == 0

    def choose_segment(former, latter):
        return jnp.where(is_first, former, latter)

    kept_state = jax.tree.map(choose_segment, early_state, later_state)
    back_upper, first_upper, second_upper = backward_pass(cotangent, kept_state, weights)
    sent_back = shifted(back_upper, "segment", -1)
    back_lower, first_lower, second_lower = backward_pass(sent_back, kept_state, weights)
    first_grad = jnp.where(is_first, first_lower, first_upper)
    second_grad = jnp.where(is_first, second_lower, second_upper)
    return reduce_channels(first_grad[None], second_grad[None])


def solution(mesh):
    placed = (
        P("seq", "mp"),
        P("seq", "mp"),
        P("segment", "mp"),
        P("segment", "mp"),
        P("segment", "seq", None, None),
        P("segment", "seq", None, None),
        P("segment", "mp", None, None),
        P("segment", "mp", None, None),
        P("segment", "mp", None, None),
        P("segment", "mp", None, None),
    )
    return jax.shard_map(
        on_device,
        mesh=mesh,
        in_specs=placed,
        out_specs=(P("segment", "seq", "mp", None), P("segment", "seq", "mp", None)),
        check_vma=False,
    )
```

profile of v0, /device:TPU:1, one launch (start us, length us, event | category | flops | bytes accessed | tf_op | source)
XLA Modules:
  0.0 530.9 jit_solution(14439777909356738681)
XLA Ops:
  11.6 2.6 copy.178
  14.2 24.8 %all_to_all.240 = bf16[8,256,256]{2,0,1:T(8,128)(2,1)S(1)} all-to-all(bf16[8,256,256]{2,0,1:T(8,128)(2,1)} %copy.178), channel_id=1, replica_groups=mesh['segment'=2,'seq'=32,'mp'=2] {'seq'}, dimensions={1} | all-to-all | bytes 2097152 | tf_op jit(solution)/shard_map/all_to_all | solution.py:22
  41.8 2.6 copy.182
  44.5 4.7 all-to-all-start.2
  49.1 2.6 copy.176
  51.8 11.6 %all-to-all-done.2 = bf16[256,8,256]{2,1,0:T(8,128)(2,1)} async-done(((bf16[256,8,256]{2,1,0:T(8,128)(2,1)}), bf16[256,8,256]{2,1,0:T(8,128)(2,1)}, u32[]{:S(2)}, u32[]{:S(2)}) %all-to-all-start.2) | async-done | bytes 1048608 | tf_op jit(solution)/shard_map/all_to_all | solution.py:26
  66.4 3.3 reshape.116
  69.6 4.2 copy.184
  73.8 3.0 add_convert_fusion.1
  77.6 15.9 %all_to_all.241 = bf16[2048,4,64]{0,2,1:T(8,128)(2,1)S(1)} all-to-all(bf16[2048,4,64]{0,2,1:T(8,128)(2,1)S(1)} %bitcast.283), channel_id=1, replica_groups=mesh['segment'=2,'seq'=32,'mp'=2] {'mp'}, dimensions={1} | all-to-all | bytes 2097152 | tf_op jit(solution)/shard_map/all_to_all | solution.py:73
  94.9 2.8 fusion.6
  98.4 13.1 %all_to_all.242 = bf16[2048,4,64]{0,2,1:T(8,128)(2,1)S(1)} all-to-all(bf16[2048,4,64]{0,2,1:T(8,128)(2,1)S(1)} %bitcast.285), channel_id=1, replica_groups=mesh['segment'=2,'seq'=32,'mp'=2] {'mp'}, dimensions={1} | all-to-all | bytes 2097152 | tf_op jit(solution)/shard_map/all_to_all | solution.py:84
  113.4 7.8 %collective-permute-done = bf16[2048,256]{0,1:T(8,128)(2,1)} collective-permute-done((bf16[2048,256]{0,1:T(8,128)(2,1)S(1)}, bf16[2048,256]{0,1:T(8,128)(2,1)}, u32[]{:S(2)}, u32[]{:S(2)}) %collective-permute-start) | collective-permute-done | bytes 1048608 | tf_op jit(solution)/shard_map/ppermute | solution.py:10
  121.2 2.6 copy.194
  123.8 1.9 multiply_convert_fusion.2
  128.2 2.6 copy.196
  130.8 22.3 %all_to_all.243 = bf16[8,256,256]{2,0,1:T(8,128)(2,1)S(1)} all-to-all(bf16[8,256,256]{2,0,1:T(8,128)(2,1)} %copy.196), channel_id=1, replica_groups=mesh['segment'=2,'seq'=32,'mp'=2] {'seq'}, dimensions={1} | all-to-all | bytes 2097152 | tf_op jit(solution)/shard_map/all_to_all | solution.py:22
  155.9 2.6 copy.200
  158.5 4.7 all-to-all-start.6
  164.9 2.1 copy.171
  167.0 2.8 convert_element_type.273
  169.8 8.2 %all-to-all-done.6 = bf16[256,8,256]{2,1,0:T(8,128)(2,1)} async-done(((bf16[256,8,256]{2,1,0:T(8,128)(2,1)}), bf16[256,8,256]{2,1,0:T(8,128)(2,1)}, u32[]{:S(2)}, u32[]{:S(2)}) %all-to-all-start.6) | async-done | bytes 1048608 | tf_op jit(solution)/shard_map/all_to_all | solution.py:26
  177.9 4.4 all-to-all-start
  185.3 3.3 reshape.119
  188.6 4.2 copy.202
  192.8 3.2 fusion.43
  197.2 4.4 all-to-all-start.7
  201.7 1.8 copy.174
  206.1 7.5 %all-to-all-done.7 = bf16[2048,4,64]{0,2,1:T(8,128)(2,1)} async-done(((bf16[2048,4,64]{0,2,1:T(8,128)(2,1)}), bf16[2048,4,64]{0,2,1:T(8,128)(2,1)}, u32[]{:S(2)}, u32[]{:S(2)}) %all-to-all-start.7) | async-done | bytes 1048608 | tf_op jit(solution)/shard_map/all_to_all | solution.py:73
  214.9 7.5 %add_multiply_fusion = f32[2048,2,512]{2,0,1:T(8,128)} fusion(f32[2,2048,512]{2,1,0:T(8,128)} %copy-done.5, bf16[2048,2,128]{0,2,1:T(8,128)(2,1)S(1)} %bitcast.301, pred[]{:T(512)S(6)} %eq.3, bf16[1,2,128,512]{3,2,1,0:T(8,128)(2,1)S(1)} %copy-done.18), kind=kOutput, calls=%fused_computation.10 | convolution fusion | flops 553648128 | bytes 18087936 | tf_op jit(solution)/shard_map/tjq,jqe->tje/dot_general | solution.py:74
  222.4 7.1 %fusion.12 = bf16[2048,2,128]{2,0,1:T(8,128)(2,1)} fusion(f32[2048,2,512]{2,0,1:T(8,128)} %add_multiply_fusion, bf16[2048,4,2,32]{0,3,2,1:T(8,128)(2,1)} %bitcast.298, bf16[1,2,128,512]{3,2,1,0:T(8,128)(2,1)S(1)} %copy-done.18, bf16[2,512,4,32]{1,3,2,0:T(8,128)(2,1)} %bitcast.305), kind=kOutput, calls=%fused_computation.24 | convolution fusion | flops 1078460416 | bytes 11010048 | tf_op jit(solution)/shard_map/tje,jqe->tjq/dot_general | solution.py:131
  229.5 3.7 copy.207
  233.2 4.6 all-to-all-start.8
  238.8 10.1 %all-to-all-done.8 = bf16[2048,2,128]{0,1,2:T(2,128)(2,1)} async-done(((bf16[2048,2,128]{0,1,2:T(2,128)(2,1)}), bf16[2048,2,128]{0,1,2:T(2,128)(2,1)}, u32[]{:S(2)}, u32[]{:S(2)}) %all-to-all-start.8) | async-done | bytes 1048608 | tf_op jit(solution)/shard_map/all_to_all | solution.py:134
  251.0 8.6 %copy.255 = f32[2048,2,128]{2,1,0:T(2,128)} copy(f32[2048,2,128]{2,0,1:T(8,128)S(1)} %convolution_bitcast_fusion.1) | data formatting | bytes 4194304 | tf_op jit(solution)/shard_map/reshape | solution.py:142
  259.6 3.9 reshape.136
  263.5 3.3 multiply_convert_fusion.1
  267.4 20.8 %all_to_all.244 = bf16[8,256,256]{2,0,1:T(8,128)(2,1)S(1)} all-to-all(bf16[8,256,256]{2,0,1:T(8,128)(2,1)S(1)} %copy.214), channel_id=1, replica_groups=mesh['segment'=2,'seq'=32,'mp'=2] {'seq'}, dimensions={1} | all-to-all | bytes 2097152 | tf_op jit(solution)/shard_map/all_to_all | solution.py:30
  291.0 2.6 copy.218
  293.7 5.0 all-to-all-start.10
  298.6 2.3 broadcast_select_fusion.1
  301.0 10.3 %all-to-all-done.10 = bf16[256,8,256]{2,1,0:T(8,128)(2,1)} async-done(((bf16[256,8,256]{2,1,0:T(8,128)(2,1)}), bf16[256,8,256]{2,1,0:T(8,128)(2,1)}, u32[]{:S(2)}, u32[]{:S(2)}) %all-to-all-start.10) | async-done | bytes 1048608 | tf_op jit(solution)/shard_map/all_to_all | solution.py:37
  311.3 6.2 %fusion.14 = bf16[8,256,256]{2,1,0:T(8,128)(2,1)} fusion(f32[8,256,256]{2,1,0:T(8,128)} %reshape.136, bf16[8,256,256]{2,1,0:T(8,128)(2,1)} %bitcast.271, bf16[1,8,256,256]{3,2,1,0:T(8,128)(2,1)} %param.14, f32[256]{0:T(256)S(1)} %bitcast.314, f32[256]{0:T(256)S(1)} %bitcast.310, bf16[8,32,8,256]{3,2,0,1:T(8,128)(2,1)} %bitcast.76, ...), kind=kOutput, calls=%fused_computation.31 | convolution fusion | flops 278396928 | bytes 11536385 | tf_op jit(solution)/shard_map/aoi,aoc->aic/dot_general | solution.py:147
  317.5 2.3 copy.221
  319.7 6.8 %collective-permute-start.1 = (bf16[2048,256]{0,1:T(8,128)(2,1)}, bf16[2048,256]{0,1:T(8,128)(2,1)S(1)}, u32[]{:S(2)}, u32[]{:S(2)}) collective-permute-start(bf16[2048,256]{0,1:T(8,128)(2,1)} %copy.221), channel_id=1, source_target_pairs={{64,0},{65,1},{66,2},{67,3},{68,4},{69,5},{70,6},{71,7},{72,8},{73... | collective-permute-start | bytes 3145736 | tf_op jit(solution)/shard_map/ppermute | solution.py:10
  326.5 2.0 collective-permute-done.1
  331.0 3.7 copy.224
  334.7 18.4 %all_to_all.245 = bf16[2048,2,128]{0,1,2:T(2,128)(2,1)S(1)} all-to-all(bf16[2048,2,128]{0,1,2:T(2,128)(2,1)} %copy.224), channel_id=1, replica_groups=mesh['segment'=2,'seq'=32,'mp'=2] {'mp'}, dimensions={2} | all-to-all | bytes 2097152 | tf_op jit(solution)/shard_map/all_to_all | solution.py:124
  354.5 7.2 %fusion.13 = bf16[2048,2,128]{2,0,1:T(8,128)(2,1)} fusion(f32[2048,2,512]{2,0,1:T(8,128)} %add_multiply_fusion, bf16[2048,4,2,32]{0,3,2,1:T(8,128)(2,1)} %bitcast.300, bf16[1,2,128,512]{3,2,1,0:T(8,128)(2,1)S(1)} %copy-done.18, bf16[2,512,4,32]{1,3,2,0:T(8,128)(2,1)} %bitcast.306), kind=kOutput, calls=%fused_computation.25 | convolution fusion | flops 1078460416 | bytes 11010048 | tf_op jit(solution)/shard_map/tje,jqe->tjq/dot_general | solution.py:131
  361.6 3.7 copy.228
  365.3 4.4 all-to-all-start.12
  369.7 2.6 copy.222
  372.3 11.4 %all-to-all-done.12 = bf16[2048,2,128]{0,1,2:T(2,128)(2,1)} async-done(((bf16[2048,2,128]{0,1,2:T(2,128)(2,1)}), bf16[2048,2,128]{0,1,2:T(2,128)(2,1)}, u32[]{:S(2)}, u32[]{:S(2)}) %all-to-all-start.12) | async-done | bytes 1048608 | tf_op jit(solution)/shard_map/all_to_all | solution.py:134
  386.0 8.6 %copy.232 = f32[2048,2,128]{2,1,0:T(2,128)} copy(f32[2048,2,128]{2,0,1:T(8,128)S(1)} %convolution_bitcast_fusion) | data formatting | bytes 4194304 | tf_op jit(solution)/shard_map/tjkc,kijc->tki/transpose | solution.py:137
  394.6 3.9 reshape.111
  398.4 3.5 multiply_convert_fusion
  402.6 18.7 %all_to_all.246 = bf16[8,256,256]{2,0,1:T(8,128)(2,1)S(1)} all-to-all(bf16[8,256,256]{2,0,1:T(8,128)(2,1)S(1)} %copy.233), channel_id=1, replica_groups=mesh['segment'=2,'seq'=32,'mp'=2] {'seq'}, dimensions={1} | all-to-all | bytes 2097152 | tf_op jit(solution)/shard_map/all_to_all | solution.py:30
  424.1 2.8 copy.237
  426.9 4.9 all-to-all-start.14
  435.9 9.5 %all-to-all-done.14 = bf16[256,8,256]{2,1,0:T(8,128)(2,1)} async-done(((bf16[256,8,256]{2,1,0:T(8,128)(2,1)}), bf16[256,8,256]{2,1,0:T(8,128)(2,1)}, u32[]{:S(2)}, u32[]{:S(2)}) %all-to-all-start.14) | async-done | bytes 1048608 | tf_op jit(solution)/shard_map/all_to_all | solution.py:37
  445.4 1.8 fusion.29
  447.1 2.8 fusion.25
  449.9 71.2 %all-reduce.3.cloned.1.call-done = (bf16[1,8,256,256]{3,2,1,0:T(8,128)(2,1)}, bf16[1,8,256,256]{3,2,1,0:T(8,128)(2,1)}) async-done(((bf16[1,8,256,256]{3,2,1,0:T(8,128)(2,1)}, bf16[1,8,256,256]{3,2,1,0:T(8,128)(2,1)}), (bf16[1,8,256,256]{3,2,1,0:T(8,128)(2,1)}, bf16[1,8,256,256]{3,2,1,0:T(8,128)(2,1)})) %all-reduce.3.cloned.1.call-update) | async-done | bytes 2097168 | tf_op jit(solution)/shard_map/psum | solution.py:161
  521.1 2.7 dynamic-slice_convert_fusion
  (96 shorter events, 49.9 us)
Async XLA Ops:
  7.2 33.2 %copy-start = (bf16[1,8,256,256]{3,2,1,0:T(8,128)(2,1)S(1)}, bf16[1,8,256,256]{3,2,1,0:T(8,128)(2,1)}, u32[]{:S(2)}) copy-start(bf16[1,8,256,256]{3,2,1,0:T(8,128)(2,1)} %param.15) | copy-start | bytes 3145732
  7.2 1.5 copy-start.22
  8.7 1.5 copy-start.6
  8.9 1.0 copy-start.8
  39.4 1.0 copy-start.1
  44.5 18.9 %all-to-all-start.2 = ((bf16[256,8,256]{2,1,0:T(8,128)(2,1)}), bf16[256,8,256]{2,1,0:T(8,128)(2,1)}, u32[]{:S(2)}, u32[]{:S(2)}) async-start(bf16[256,8,256]{2,1,0:T(8,128)(2,1)} %copy.182), calls=%async_computation.2 | async-start | bytes 2097152 | tf_op jit(solution)/shard_map/all_to_all | solution.py:26
  69.6 4.2 copy-start.21
  73.8 3.0 copy-start.19
  77.6 16.0 %copy-start.18 = (bf16[1,2,128,512]{3,2,1,0:T(8,128)(2,1)S(1)}, bf16[1,2,128,512]{3,2,1,0:T(8,128)(2,1)}, u32[]{:S(2)}) copy-start(bf16[1,2,128,512]{3,2,1,0:T(8,128)(2,1)} %param.17) | copy-start | bytes 786436
  93.5 1.3 copy-start.20
  94.9 3.3 copy-start.5
  98.4 13.2 %copy-start.17 = (bf16[1,2,128,128]{3,2,1,0:T(8,128)(2,1)S(1)}, bf16[1,2,128,128]{3,2,1,0:T(8,128)(2,1)}, u32[]{:S(2)}) copy-start(bf16[1,2,128,128]{3,2,1,0:T(8,128)(2,1)} %param.19) | copy-start | bytes 196612
  112.1 9.1 %collective-permute-start = (bf16[2048,256]{0,1:T(8,128)(2,1)S(1)}, bf16[2048,256]{0,1:T(8,128)(2,1)}, u32[]{:S(2)}, u32[]{:S(2)}) collective-permute-start(bf16[2048,256]{0,1:T(8,128)(2,1)S(1)} %bitcast.297), channel_id=1, source_target_pairs={{0,64},{1,65},{2,66},{3,67},{4,68},{5,69},{6,70},{7,71},{8,72},{9,... | collective-permute-start | bytes 3145736 | tf_op jit(solution)/shard_map/ppermute | solution.py:10
  123.8 2.9 copy-start.7
  125.7 1.0 copy-start.10
  153.4 1.0 copy-start.3
  158.5 19.4 %all-to-all-start.6 = ((bf16[256,8,256]{2,1,0:T(8,128)(2,1)}), bf16[256,8,256]{2,1,0:T(8,128)(2,1)}, u32[]{:S(2)}, u32[]{:S(2)}) async-start(bf16[256,8,256]{2,1,0:T(8,128)(2,1)} %copy.200), calls=%async_computation.6 | async-start | bytes 2097152 | tf_op jit(solution)/shard_map/all_to_all | solution.py:26
  177.9 19.3 %all-to-all-start = ((bf16[2048,2,128]{0,1,2:T(2,128)(2,1)}), bf16[2048,2,128]{0,1,2:T(2,128)(2,1)}, u32[]{:S(2)}, u32[]{:S(2)}) async-start(bf16[2048,2,128]{0,1,2:T(2,128)(2,1)} %copy.171), calls=%async_computation | async-start | bytes 2097152 | tf_op jit(solution)/shard_map/all_to_all | solution.py:124
  197.2 16.3 %all-to-all-start.7 = ((bf16[2048,4,64]{0,2,1:T(8,128)(2,1)}), bf16[2048,4,64]{0,2,1:T(8,128)(2,1)}, u32[]{:S(2)}, u32[]{:S(2)}) async-start(bf16[2048,4,64]{0,2,1:T(8,128)(2,1)} %bitcast.281), calls=%async_computation.7 | async-start | bytes 2097152 | tf_op jit(solution)/shard_map/all_to_all | solution.py:73
  233.2 15.7 %all-to-all-start.8 = ((bf16[2048,2,128]{0,1,2:T(2,128)(2,1)}), bf16[2048,2,128]{0,1,2:T(2,128)(2,1)}, u32[]{:S(2)}, u32[]{:S(2)}) async-start(bf16[2048,2,128]{0,1,2:T(2,128)(2,1)} %copy.207), calls=%async_computation.8 | async-start | bytes 2097152 | tf_op jit(solution)/shard_map/all_to_all | solution.py:134
  288.5 1.1 copy-start.12
  293.7 17.6 %all-to-all-start.10 = ((bf16[256,8,256]{2,1,0:T(8,128)(2,1)}), bf16[256,8,256]{2,1,0:T(8,128)(2,1)}, u32[]{:S(2)}, u32[]{:S(2)}) async-start(bf16[256,8,256]{2,1,0:T(8,128)(2,1)} %copy.218), calls=%async_computation.10 | async-start | bytes 2097152 | tf_op jit(solution)/shard_map/all_to_all | solution.py:37
  319.7 8.8 %collective-permute-start.1 = (bf16[2048,256]{0,1:T(8,128)(2,1)}, bf16[2048,256]{0,1:T(8,128)(2,1)S(1)}, u32[]{:S(2)}, u32[]{:S(2)}) collective-permute-start(bf16[2048,256]{0,1:T(8,128)(2,1)} %copy.221), channel_id=1, source_target_pairs={{64,0},{65,1},{66,2},{67,3},{68,4},{69,5},{70,6},{71,7},{72,8},{73... | collective-permute-start | bytes 3145736 | tf_op jit(solution)/shard_map/ppermute | solution.py:10
  328.5 1.0 copy-start.14
  365.3 18.5 %all-to-all-start.12 = ((bf16[2048,2,128]{0,1,2:T(2,128)(2,1)}), bf16[2048,2,128]{0,1,2:T(2,128)(2,1)}, u32[]{:S(2)}, u32[]{:S(2)}) async-start(bf16[2048,2,128]{0,1,2:T(2,128)(2,1)} %copy.228), calls=%async_computation.12 | async-start | bytes 2097152 | tf_op jit(solution)/shard_map/all_to_all | solution.py:134
  421.6 1.0 copy-start.15
  424.1 7.7 %copy-start.2 = (bf16[32,8,8,256]{3,2,1,0:T(8,128)(2,1)S(1)}, bf16[32,8,8,256]{3,2,1,0:T(8,128)(2,1)}, u32[]{:S(2)}) copy-start(bf16[32,8,8,256]{3,2,1,0:T(8,128)(2,1)} %copy-done.1) | copy-start | bytes 3145732
  424.1 7.7 %copy-start.4 = (bf16[32,8,8,256]{3,2,1,0:T(8,128)(2,1)S(1)}, bf16[32,8,8,256]{3,2,1,0:T(8,128)(2,1)}, u32[]{:S(2)}) copy-start(bf16[32,8,8,256]{3,2,1,0:T(8,128)(2,1)} %copy-done.3) | copy-start | bytes 3145732
  426.9 18.5 %all-to-all-start.14 = ((bf16[256,8,256]{2,1,0:T(8,128)(2,1)}), bf16[256,8,256]{2,1,0:T(8,128)(2,1)}, u32[]{:S(2)}, u32[]{:S(2)}) async-start(bf16[256,8,256]{2,1,0:T(8,128)(2,1)} %copy.237), calls=%async_computation.14 | async-start | bytes 2097152 | tf_op jit(solution)/shard_map/all_to_all | solution.py:37
  431.8 89.4 %all-reduce.3.cloned.1.call-start = ((), (), s32[]{:S(2)}) async-start(), calls=%async_computation.15 | async-start | bytes 4194304 | tf_op jit(solution)/shard_map/psum | solution.py:161
  431.8 1.2 copy-start.16
  433.1 1.2 copy-start.13
  434.3 11.1 %copy-start.9 = (bf16[8,256,256]{2,1,0:T(8,128)(2,1)S(1)}, bf16[8,256,256]{2,1,0:T(8,128)(2,1)}, u32[]{:S(2)}) copy-start(bf16[8,256,256]{2,1,0:T(8,128)(2,1)} %copy-done.8) | copy-start | bytes 3145732
  434.3 11.1 %copy-start.11 = (bf16[8,256,256]{2,1,0:T(8,128)(2,1)S(1)}, bf16[8,256,256]{2,1,0:T(8,128)(2,1)}, u32[]{:S(2)}) copy-start(bf16[8,256,256]{2,1,0:T(8,128)(2,1)} %copy-done.10) | copy-start | bytes 3145732
Sparse Core Ops, SparseCore 0:
  450.0 71.0 all-reduce.2
where the time goes:
time: 542 us; the launch traced here: 531 us
  waiting for transfers between devices  150 us (28%)
  blocking collectives  134 us (25%)
  local copies, waits for them, and re-layouts  107 us (20%)
  matrix products  55.9 us (10%)
  starting transfers between devices  45.2 us (8%)
  other arithmetic  24.8 us (5%)
  between operations  14.8 us (3%)
    psum x1, waiting for transfers between devices, reduce_channels(): lax.psum(first_grad.astype(jnp.bfloat16), 'mp').astype(jnp.float32)  71.2 us
    all_to_all x2, blocking collectives, sequence_mix(): lax.all_to_all(mixed_rows, 'seq', split_axis=1, concat_axis=0, tiled=True)  47.1 us
    all_to_all x2, blocking collectives, sequence_back(): lax.all_to_all(back_turned, 'seq', split_axis=1, concat_axis=0, tiled=True)  39.5 us
    all_to_all x2, waiting for transfers between devices, backward_pass(): lax.all_to_all(back_perm, 'mp', split_axis=2, concat_axis=1, tiled=True)  21.5 us
    all_to_all x2, waiting for transfers between devices, sequence_back(): lax.all_to_all(back_mixed_cols, 'seq', split_axis=0, concat_axis=1, tiled...  19.8 us
    all_to_all x2, waiting for transfers between devices, sequence_mix(): lax.all_to_all(turned_cols, 'seq', split_axis=0, concat_axis=1, tiled=True)  19.8 us
    all_to_all x1, blocking collectives, backward_pass(): lax.all_to_all(backward_folded_rows, 'mp', split_axis=2, concat_axis=1, t...  18.4 us
    convert_element_type x6, local copies, waits for them, and re-layouts, forward_pass(): turned.astype(jnp.float32)  17.9 us
  transfers between devices with their start and end apart: 11, of which 10 were waited for; matrix products, arithmetic and copies ran while one was open for 7% of the time, Pallas kernels for 0%

commit v1 on v0

v1 whole, which is shorter than its diff:
```python
import functools

import jax
import jax.numpy as jnp
from jax import lax
from jax.experimental import pallas as pl
from jax.experimental.pallas import tpu as pltpu
from jax.sharding import PartitionSpec as P

ROWS_ORDER = ("seq", "segment", "mp")
QUARTER_ORDER = ("mp", "seq", "segment")
BF = jnp.bfloat16
F32 = jnp.float32
MSG = (2048, 128)


def exchange(message, order):
    return lax.all_to_all(message, order, split_axis=0, concat_axis=0, tiled=True)


def swap(value, axis):
    return lax.ppermute(value, axis, [(0, 1), (1, 0)])


def pick(flag, when_zero, when_one):
    return jnp.where(flag == 0, when_zero, when_one)


def dot(a, b):
    return jnp.dot(a, b, preferred_element_type=F32)


def dot_nt(a, b):
    return lax.dot_general(a, b, (((1,), (1,)), ((), ())), preferred_element_type=F32)


def sigmoid(v):
    return 0.5 * jnp.tanh(0.5 * v) + 0.5


def slope(v):
    s = sigmoid(v)
    return s * (1.0 + v * (1.0 - s))


def call(body, name, outs, scratch, args, smem=0, flops=10**8):
    specs = [pl.BlockSpec(memory_space=pltpu.SMEM)] * smem
    specs += [pl.BlockSpec(memory_space=pltpu.VMEM)] * (len(args) - smem)
    out_shape = tuple(jax.ShapeDtypeStruct(s, d) for s, d in outs)
    moved = sum(a.size * a.dtype.itemsize for a in args) + sum(
        o.size * o.dtype.itemsize for o in out_shape
    )
    return pl.pallas_call(
        body,
        out_shape=out_shape,
        in_specs=specs,
        out_specs=tuple(pl.BlockSpec(memory_space=pltpu.VMEM) for _ in outs),
        scratch_shapes=[pltpu.VMEM(s, d) for s, d in scratch],
        compiler_params=pltpu.CompilerParams(vmem_limit_bytes=40 * 2**20),
        cost_estimate=pl.CostEstimate(flops=flops, bytes_accessed=moved, transcendentals=0),
        name=name,
    )(*args)


def pack_quarter(values, a, out, temp):
    for h in range(2):
        temp[...] = values[:, h * 128 : (h + 1) * 128]
        for mm in range(2):
            for oo in range(2):
                out[pl.ds(mm * 1024 + a * 4 + oo * 2 + h, 64, stride=16), :] = temp[
                    pl.ds(mm * 2 + oo, 64, stride=4), :
                ]


def unpack_quarter(source, oo):
    parts = [
        source[pl.ds(mm * 1024 + oo * 2 + h, 256, stride=4), :] for mm in range(2) for h in range(2)
    ]
    return jnp.concatenate(parts, axis=1)


def pack_cols(values, oo, out):
    for cq in range(4):
        out[pl.ds(oo * 4 + cq, 256, stride=8), :] = values[:, cq * 128 : (cq + 1) * 128]


def unpack_cols(source, oo):
    return jnp.concatenate(
        [source[pl.ds(oo * 4 + cq, 256, stride=8), :] for cq in range(4)], axis=1
    )


def pack_rows(values, a2, out, temp):
    for cq in range(4):
        temp[...] = values[:, cq * 128 : (cq + 1) * 128]
        for oo in range(2):
            out[pl.ds(a2 * 8 + oo * 4 + cq, 128, stride=16), :] = temp[pl.ds(oo, 128, stride=2), :]


def unpack_rows(source, a2, temp):
    for cq in range(4):
        for oo in range(2):
            temp[cq, pl.ds(oo, 128, stride=2), :] = source[
                pl.ds(a2 * 8 + oo * 4 + cq, 128, stride=16), :
            ]
    return jnp.concatenate([temp[cq] for cq in range(4)], axis=1)


def pack_body(g_ref, x_ref, out_ref, packed, temp):
    g = g_ref[0]
    for a in range(4):
        pack_quarter(x_ref[4 * g + a].astype(F32), a, packed, temp)
    out_ref[...] = packed[...].astype(BF)


def first_rows_body(g_ref, x_ref, mine_ref, got_ref, key_ref, out_ref, packed, temp):
    g = g_ref[0]
    for a in range(4):
        scaled = (x_ref[4 * g + a].astype(F32) * key_ref[...]).astype(BF)
        factor = jnp.where(g == 0, mine_ref[a], got_ref[a])
        pack_quarter(dot(factor, scaled), a, packed, temp)
    out_ref[...] = packed[...].astype(BF)


def prepare_body(up_ref, down_ref, u_ref, v_ref):
    rho = lax.broadcasted_iota(jnp.int32, (128, 512), 0)
    gam = lax.broadcasted_iota(jnp.int32, (128, 512), 1)
    same = (gam // 128) * 32 + gam % 32 == rho
    for k in range(4):
        place = jnp.where(same & ((gam // 32) % 4 == k), 1.0, 0.0).astype(BF)
        u_ref[k * 128 : (k + 1) * 128, :] = dot(up_ref[k], place).astype(BF)
        spread = lax.dot_general(
            place, down_ref[k], (((0,), (0,)), ((), ())), preferred_element_type=F32
        )
        v_ref[:, k * 128 : (k + 1) * 128] = spread.astype(BF)


def forward_cols_body(
    mixed_msg, x_msg, factor, gate, key, u, v, up2, down1,
    out_msg, mixed_out, x_out, hidden_out, turned_out, middle_out,
    wide, wide_x,
):
    wide[...] = mixed_msg[...].astype(F32)
    wide_x[...] = x_msg[...].astype(F32)
    scaled = []
    for oo in range(2):
        part = slice(oo * 256, (oo + 1) * 256)
        mixed = unpack_quarter(wide, oo).astype(BF)
        x = unpack_quarter(wide_x, oo)
        turned = dot(factor[oo], mixed).astype(BF)
        pre = x * gate[...]
        hidden = (x + pre * sigmoid(pre) * turned.astype(F32)).astype(BF)
        mixed_out[part, :] = mixed
        x_out[part, :] = x.astype(BF)
        hidden_out[part, :] = hidden
        turned_out[part, :] = turned
        permuted = dot(hidden, u[...]).astype(BF)
        folds = []
        for j in range(4):
            preact = dot(permuted[:, j * 128 : (j + 1) * 128], up2[j])
            active = (preact * sigmoid(preact)).astype(BF)
            folds.append(dot(active, down1[j]).astype(BF))
        out = dot(jnp.concatenate(folds, axis=1), v[...])
        middle = (hidden.astype(F32) + out).astype(BF)
        middle_out[part, :] = middle
        scaled.append((middle.astype(F32) * key[...]).astype(BF).astype(F32))
    for oo in range(2):
        pack_cols(scaled[oo], oo, wide)
    out_msg[...] = wide[...].astype(BF)


def rows_body(msg, factor, scale, out_msg, saved, wide, packed, temp, temp4):
    wide[...] = msg[...].astype(F32)
    for a2 in range(2):
        values = unpack_rows(wide, a2, temp4).astype(BF)
        saved[a2] = values
        result = dot(factor[a2], values) * scale[...]
        pack_rows(result, a2, packed, temp)
    out_msg[...] = packed[...].astype(BF)


def last_rows_body(msg, x_ref, key, grad, wide, temp4):
    wide[...] = msg[...].astype(F32)
    for a2 in range(2):
        values = unpack_rows(wide, a2, temp4).astype(BF)
        scaled = (x_ref[a2].astype(F32) * key[...]).astype(BF)
        grad[a2] = dot_nt(values, scaled).astype(BF)


def ffn_back(cot, hidden, u, v, up2, down1):
    permuted = dot(hidden, u[...]).astype(BF)
    fold = dot_nt(cot, v[...]).astype(BF)
    perms = []
    for j in range(4):
        block = slice(j * 128, (j + 1) * 128)
        preact = dot(permuted[:, block], up2[j])
        back_active = dot_nt(fold[:, block], down1[j])
        back_preact = (back_active * slope(preact)).astype(BF)
        perms.append(dot_nt(back_preact, up2[j]).astype(BF))
    return cot.astype(F32) + dot_nt(jnp.concatenate(perms, axis=1), u[...])


def upper_cols_body(
    mixed_msg, cot_msg, x_ref, factor, factor_t, gate, u, v, up2, down1,
    out_msg, mixed_out, back_turned_out, direct_out,
    wide, wide_c, packed,
):
    wide[...] = mixed_msg[...].astype(F32)
    wide_c[...] = cot_msg[...].astype(F32)
    for oo in range(2):
        part = slice(oo * 256, (oo + 1) * 256)
        mixed = unpack_cols(wide, oo).astype(BF)
        cot = unpack_quarter(wide_c, oo).astype(BF)
        mixed_out[part, :] = mixed
        x = x_ref[part, :].astype(F32)
        turned = dot(factor[oo], mixed).astype(BF).astype(F32)
        pre = x * gate[...]
        logistic = sigmoid(pre)
        gated = pre * logistic
        hidden = (x + gated * turned).astype(BF)
        back_hidden = ffn_back(cot, hidden, u, v, up2, down1)
        back_turned = (back_hidden * gated).astype(BF)
        back_turned_out[part, :] = back_turned
        pack_cols(dot(factor_t[oo], back_turned), oo, packed)
        gate_slope = logistic * (1.0 + pre * (1.0 - logistic))
        direct_out[part, :] = back_hidden + back_hidden * turned * gate_slope * gate[...]
    out_msg[...] = packed[...].astype(BF)


def lower_cols_body(
    msg, direct, x_ref, hidden_ref, factor_t, gate, u, v, up2, down1,
    out_msg, back_turned_out,
    wide, packed,
):
    wide[...] = msg[...].astype(F32)
    for oo in range(2):
        part = slice(oo * 256, (oo + 1) * 256)
        passed = (direct[part, :] + unpack_cols(wide, oo)).astype(BF)
        back_hidden = ffn_back(passed, hidden_ref[part, :], u, v, up2, down1)
        pre = x_ref[part, :].astype(F32) * gate[...]
        back_turned = (back_hidden * (pre * sigmoid(pre))).astype(BF)
        back_turned_out[part, :] = back_turned
        pack_cols(dot(factor_t[oo], back_turned), oo, packed)
    out_msg[...] = packed[...].astype(BF)


def channel_grad(outer, inner):
    return jnp.einsum("boc,bic->boi", outer, inner, preferred_element_type=F32).astype(BF)


def on_device(
    inputs,
    cotangent,
    gate_gain,
    key_gain,
    first_factor,
    second_factor,
    up_first,
    up_second,
    down_first,
    down_second_weight,
):
    g = lax.axis_index("segment")
    m = lax.axis_index("mp")
    r = 2 * g + m
    g_arr = g.reshape(1)
    rows = inputs.reshape(8, 256, 256)
    cot_rows = cotangent.reshape(8, 256, 256)
    seq_count = lax.axis_size("seq")
    pairs = [
        (q * 2 + side, (q ^ (seq_count // 2)) * 2 + 1 - side)
        for q in range(seq_count)
        for side in range(2)
    ]

    def swap_mp(value):
        return lax.ppermute(value, ("seq", "mp"), pairs)

    scratch_pack = [(MSG, F32), ((256, 128), F32)]
    (x_msg,) = call(pack_body, "pack_x", [(MSG, BF)], scratch_pack, (g_arr, rows), smem=1)
    (cot_msg,) = call(pack_body, "pack_cot", [(MSG, BF)], scratch_pack, (g_arr, cot_rows), smem=1)
    x_msg = exchange(x_msg, QUARTER_ORDER)
    cot_msg = exchange(cot_msg, QUARTER_ORDER)

    first_mine, second_mine = first_factor[0], second_factor[0]
    first_got = swap(lax.dynamic_slice_in_dim(first_mine, 4 * (1 - g), 4, 0), "segment")
    second_got = swap(lax.dynamic_slice_in_dim(second_mine, 4 * (1 - g) + 2 * m, 2, 0), "segment")
    key_got = swap(key_gain, "segment")

    (mixed_msg,) = call(
        first_rows_body,
        "first_rows",
        [(MSG, BF)],
        scratch_pack,
        (g_arr, rows, first_mine, first_got, pick(g, key_gain, key_got)),
        smem=1,
    )
    mixed_msg = exchange(mixed_msg, QUARTER_ORDER)

    first_own = lax.dynamic_slice_in_dim(first_mine, 2 * r, 2, 0)
    first_oth = lax.dynamic_slice_in_dim(first_got, 2 * m, 2, 0)
    second_own = lax.dynamic_slice_in_dim(second_mine, 2 * r, 2, 0)
    first1 = pick(g, first_oth, first_own)
    first1_t = jnp.swapaxes(first1, 1, 2)
    second0, second1 = pick(g, second_own, second_got), pick(g, second_got, second_own)
    second0_t, second1_t = jnp.swapaxes(second0, 1, 2), jnp.swapaxes(second1, 1, 2)

    narrow = jnp.concatenate([up_first[0], down_second_weight[0], down_first[0]], axis=1)
    wide = up_second[0]

    def every_block(own):
        peer = swap_mp(own)
        whole = pick(m, jnp.concatenate([own, peer]), jnp.concatenate([peer, own]))
        other = swap(whole, "segment")
        return pick(g, whole, other), pick(g, other, whole)

    narrow, up2 = every_block(narrow), every_block(wide)
    down1 = [n[:, 256:] for n in narrow]
    gains = jnp.concatenate([gate_gain, key_gain])
    gains_peer = swap_mp(gains)
    gains_all = pick(
        m,
        jnp.concatenate([gains, gains_peer], axis=1),
        jnp.concatenate([gains_peer, gains], axis=1),
    )
    gains_other = swap(gains_all, "segment")
    layers = (pick(g, gains_all, gains_other), pick(g, gains_other, gains_all))
    gate = [layer[0:1] for layer in layers]
    key = [layer[1:2] for layer in layers]
    dense = [
        call(
            prepare_body,
            f"prepare_{layer}",
            [((512, 512), BF)] * 2,
            [],
            (narrow[layer][:, :128], narrow[layer][:, 128:256]),
        )
        for layer in range(2)
    ]

    act = ((512, 512), BF)
    next_msg, mixed0, x0, hidden0, turned0, middle = call(
        forward_cols_body,
        "forward_cols",
        [(MSG, BF)] + [act] * 5,
        [(MSG, F32)] * 2,
        (mixed_msg, x_msg, second0, gate[0], key[1], *dense[0], up2[0], down1[0]),
    )
    msg = exchange(next_msg, ROWS_ORDER)

    scratch_rows = [(MSG, F32), (MSG, F32), ((256, 128), F32), ((4, 256, 128), F32)]
    out_rows = [(MSG, BF), ((2, 256, 512), BF)]
    next_msg, scaled1 = call(
        rows_body, "rows_1", out_rows, scratch_rows, (msg, first1, jnp.ones((1, 512), F32))
    )
    msg = exchange(next_msg, ROWS_ORDER)

    next_msg, mixed1, back_turned1, direct = call(
        upper_cols_body,
        "upper_cols",
        [(MSG, BF), act, act, ((512, 512), F32)],
        [(MSG, F32)] * 3,
        (msg, cot_msg, middle, second1, second1_t, gate[1], *dense[1], up2[1], down1[1]),
    )
    msg = exchange(next_msg, ROWS_ORDER)
    cols = (2, 256, 512)
    second_grad1 = channel_grad(back_turned1.reshape(cols), mixed1.reshape(cols))

    next_msg, back_rows1 = call(rows_body, "rows_1_back", out_rows, scratch_rows, (msg, first1_t, key[1]))
    msg = exchange(next_msg, ROWS_ORDER)
    first_grad1 = channel_grad(back_rows1, scaled1)

    next_msg, back_turned0 = call(
        lower_cols_body,
        "lower_cols",
        [(MSG, BF), act],
        [(MSG, F32)] * 2,
        (msg, direct, x0, hidden0, second0_t, gate[0], *dense[0], up2[0], down1[0]),
    )
    msg = exchange(next_msg, ROWS_ORDER)
    second_grad0 = channel_grad(back_turned0.reshape(cols), mixed0.reshape(cols))

    own = lax.dynamic_slice_in_dim(rows, 2 * r, 2, 0)
    peer = swap(lax.dynamic_slice_in_dim(rows, 2 * (2 * g + 1 - m), 2, 0), "mp")
    x_rows = pick(m, jnp.concatenate([own, peer], axis=2), jnp.concatenate([peer, own], axis=2))
    (first_grad0,) = call(
        last_rows_body,
        "last_rows",
        [((2, 256, 256), BF)],
        [(MSG, F32), ((4, 256, 128), F32)],
        (msg, x_rows, key[0]),
    )

    def gather_mp(grad):
        halves = grad.reshape(2, 2, 128, 256)
        mine = lax.dynamic_index_in_dim(halves, m, 1, False)
        theirs = swap(lax.dynamic_index_in_dim(halves, 1 - m, 1, False), "mp")
        return pick(m, jnp.concatenate([mine, theirs]), jnp.concatenate([theirs, mine]))

    def place(grad0, grad1):
        four0, four1 = gather_mp(grad0), gather_mp(grad1)
        from1 = lax.ppermute(four1, "segment", [(0, 1)])
        from0 = lax.ppermute(four0, "segment", [(1, 0)])
        mine = pick(g, four0, four1)
        theirs = pick(g, from0, from1)
        eight = pick(g, jnp.concatenate([mine, theirs]), jnp.concatenate([theirs, mine]))
        return eight.astype(F32)[None]

    return place(first_grad0, first_grad1), place(second_grad0, second_grad1)


def solution(mesh):
    placed = (
        P("seq", "mp"),
        P("seq", "mp"),
        P("segment", "mp"),
        P("segment", "mp"),
        P("segment", "seq", None, None),
        P("segment", "seq", None, None),
        P("segment", "mp", None, None),
        P("segment", "mp", None, None),
        P("segment", "mp", None, None),
        P("segment", "mp", None, None),
    )
    return jax.shard_map(
        on_device,
        mesh=mesh,
        in_specs=placed,
        out_specs=(P("segment", "seq", "mp", None), P("segment", "seq", "mp", None)),
        check_vma=False,
    )
```

time: 542 us -> 235 us (0.43); the launches traced: 531 us -> 233 us
  blocking collectives: 134 us -> 0 us
  waiting for transfers between devices: 150 us -> 61.4 us
  local copies, waits for them, and re-layouts: 107 us -> 40.8 us
  matrix products: 55.9 us -> 2.28 us
  starting transfers between devices: 45.2 us -> 86.3 us
  Pallas kernels: 0 us -> 23 us
  between operations: 14.8 us -> 1.25 us
  other arithmetic: 24.8 us -> 18.3 us
    all_to_all x7 -> x0, blocking collectives: 134 us -> none  [the longest x2 47.1 us: sequence_mix(): lax.all_to_all(mixed_rows, 'seq', split_axis=1, concat_axis=0, tiled=True)]
    psum x1 -> x0, waiting for transfers between devices: 71.2 us -> none  [reduce_channels(): lax.psum(first_grad.astype(jnp.bfloat16), 'mp').astype(jnp.float32)]
    convert_element_type x24 -> x0, local copies, waits for them, and re-layouts: 56.9 us -> none  [the longest x6 17.9 us: forward_pass(): turned.astype(jnp.float32)]
    dot_general x20 -> x3, matrix products: 49.4 us -> 2.28 us  [channel_grad(): jnp.einsum('boc,bic->boi', outer, inner, preferred_element_type=F32)]
    ppermute x2 -> x18, starting transfers between devices: 8.04 us -> 33.3 us  [the longest x11 14.5 us: swap(): return lax.ppermute(value, axis, [(0, 1), (1, 0)])]
    pallas_call x0 -> x11, Pallas kernels: none -> 23 us  [call(): pl.pallas_call(body, out_shape=out_shape, in_specs=specs, out_specs=tuple...]
    all_to_all x8, waiting for transfers between devices: 68.6 us -> 48.3 us  [exchange(): lax.all_to_all(message, order, split_axis=0, concat_axis=0, tiled=True)]
    convert_element_type x13 -> x2, other arithmetic: 22.2 us -> 2.14 us  [place(): return eight.astype(F32)[None]]
  transfers between devices with their start and end apart: 11 -> 26, of which waited for: 10 -> 10; matrix products, arithmetic and copies ran while one was open for 7% -> 13% of each run, Pallas kernels for 0% -> 5%
where the time goes in v1:
time: 235 us; the launch traced here: 233 us
  starting transfers between devices  86.3 us (37%)
  waiting for transfers between devices  61.4 us (26%)
  local copies, waits for them, and re-layouts  40.8 us (17%)
  Pallas kernels  23 us (10%)
  other arithmetic  18.3 us (8%)
    all_to_all x8, starting transfers between devices, exchange(): lax.all_to_all(message, order, split_axis=0, concat_axis=0, tiled=True)  53 us
    all_to_all x8, waiting for transfers between devices, exchange(): lax.all_to_all(message, order, split_axis=0, concat_axis=0, tiled=True)  48.3 us
    unnamed x102, local copies, waits for them, and re-layouts  28.9 us
    pallas_call x11, Pallas kernels, call(): pl.pallas_call(body, out_shape=out_shape, in_specs=specs, out_specs=tuple...  23 us
    ppermute x11, starting transfers between devices, swap(): return lax.ppermute(value, axis, [(0, 1), (1, 0)])  14.5 us
    select_n x10, other arithmetic, pick(): return jnp.where(flag == 0, when_zero, when_one)  13.1 us
    ppermute x11, waiting for transfers between devices, swap(): return lax.ppermute(value, axis, [(0, 1), (1, 0)])  12.1 us
    ppermute x2, starting transfers between devices, place(): from0 = lax.ppermute(four0, 'segment', [(1, 0)])  8.71 us
  transfers between devices with their start and end apart: 26, of which 10 were waited for; matrix products, arithmetic and copies ran while one was open for 13% of the time, Pallas kernels for 5%

profile of v1, /device:TPU:1, one launch (start us, length us, event | category | flops | bytes accessed | tf_op | source)
XLA Modules:
  0.0 233.2 jit_solution(3670158856310598585)
XLA Ops:
  0.7 1.8 pad_maximum_fusion
  2.5 4.6 %collective-permute-start.5 = (bf16[2,768,128]{2,1,0:T(8,128)(2,1)}, bf16[2,768,128]{2,1,0:T(8,128)(2,1)}, u32[]{:S(2)}, u32[]{:S(2)}) collective-permute-start(bf16[2,768,128]{2,1,0:T(8,128)(2,1)} %pad_maximum_fusion), channel_id=1, source_target_pairs={{0,33},{1,32},{2,35},{3,34},{4,37},{5,36},{6,39},{7,38},{8,41},{9,... | collective-permute-start | bytes 1179656 | tf_op jit(solution)/shard_map/ppermute | solution.py:277
  7.1 1.1 constant_dynamic-slice_fusion.4
  9.0 1.0 collective-permute-start.2
  10.0 3.0 %collective-permute-start.3 = (f32[2,256]{1,0:T(2,128)S(1)}, f32[2,256]{1,0:T(2,128)S(1)}, u32[]{:S(2)}, u32[]{:S(2)}) collective-permute-start(f32[2,256]{1,0:T(2,128)S(1)} %pad_maximum_fusion.1), channel_id=1, source_target_pairs={{0,33},{1,32},{2,35},{3,34},{4,37},{5,36},{6,39},{7,38},{8,41},{9,... | collective-permute-start | bytes 6152 | tf_op jit(solution)/shard_map/ppermute | solution.py:277
  13.0 1.3 pack_x.1
  14.3 7.5 %all-to-all-start.1 = ((bf16[128,16,128]{2,1,0:T(8,128)(2,1)}), bf16[128,16,128]{2,1,0:T(8,128)(2,1)}, u32[]{:S(2)}, u32[]{:S(2)}) async-start(bf16[128,16,128]{2,1,0:T(8,128)(2,1)} %bitcast.6), calls=%async_computation.1 | async-start | bytes 1048576 | tf_op jit(solution)/shard_map/all_to_all | solution.py:18
  22.7 1.0 copy.12
  23.7 1.1 collective-permute-start
  27.4 2.1 maximum_select_fusion.1
  29.9 2.2 maximum_select_fusion
  32.2 1.7 bitcast_select_fusion.1
  35.7 1.5 first_rows.1
  37.2 2.1 broadcast_select_fusion.2
  39.3 9.9 %all-to-all-start = ((bf16[128,16,128]{2,1,0:T(8,128)(2,1)}), bf16[128,16,128]{2,1,0:T(8,128)(2,1)}, u32[]{:S(2)}, u32[]{:S(2)}) async-start(bf16[128,16,128]{2,1,0:T(8,128)(2,1)} %bitcast.4), calls=%async_computation | async-start | bytes 1048576 | tf_op jit(solution)/shard_map/all_to_all | solution.py:18
  49.2 1.5 broadcast_select_fusion
  53.7 8.8 %all-to-all-done = bf16[128,16,128]{2,1,0:T(8,128)(2,1)} async-done(((bf16[128,16,128]{2,1,0:T(8,128)(2,1)}), bf16[128,16,128]{2,1,0:T(8,128)(2,1)}, u32[]{:S(2)}, u32[]{:S(2)}) %all-to-all-start) | async-done | bytes 524320 | tf_op jit(solution)/shard_map/all_to_all | solution.py:18
  62.5 1.0 copy-done.4
  63.5 1.0 copy-done.7
  64.6 0.9 copy-done.15
  65.5 4.6 %forward_cols.1 = (bf16[2048,128]{1,0:T(8,128)(2,1)S(1)}, bf16[512,512]{1,0:T(8,128)(2,1)S(1)}, bf16[512,512]{1,0:T(8,128)(2,1)S(1)}, bf16[512,512]{1,0:T(8,128)...) custom-call(bf16[2048,128]{1,0:T(8,128)(2,1)} %bitcast.5.mixed_msg, bf16[2048,128]{1,0:T(8,128)(2,1)} %bitcast.7.x_msg, ...), custom_call_target="tpu_custom_call" | custom-call | flops 100000000 | bytes 6557696 | tf_op jit(solution)/shard_map/forward_cols/pallas_call | solution.py:53
  74.1 5.5 %all-to-all-start.2 = ((bf16[128,16,128]{2,1,0:T(8,128)(2,1)}), bf16[128,16,128]{2,1,0:T(8,128)(2,1)}, u32[]{:S(2)}, u32[]{:S(2)}) async-start(bf16[128,16,128]{2,1,0:T(8,128)(2,1)} %bitcast.92), calls=%async_computation.2 | async-start | bytes 1048576 | tf_op jit(solution)/shard_map/all_to_all | solution.py:18
  79.6 1.2 copy-done.12
  82.1 10.1 %all-to-all-done.2 = bf16[128,16,128]{2,1,0:T(8,128)(2,1)} async-done(((bf16[128,16,128]{2,1,0:T(8,128)(2,1)}), bf16[128,16,128]{2,1,0:T(8,128)(2,1)}, u32[]{:S(2)}, u32[]{:S(2)}) %all-to-all-start.2) | async-done | bytes 524320 | tf_op jit(solution)/shard_map/all_to_all | solution.py:18
  92.3 5.8 %all-to-all-start.4 = ((bf16[128,16,128]{2,1,0:T(8,128)(2,1)}), bf16[128,16,128]{2,1,0:T(8,128)(2,1)}, u32[]{:S(2)}, u32[]{:S(2)}) async-start(bf16[128,16,128]{2,1,0:T(8,128)(2,1)} %bitcast.82), calls=%async_computation.4 | async-start | bytes 1048576 | tf_op jit(solution)/shard_map/all_to_all | solution.py:18
  98.8 1.1 copy.17
  99.8 1.0 bitcast_select_fusion
  101.0 2.1 rows_1.1
  104.7 6.5 %all-to-all-done.4 = bf16[128,16,128]{2,1,0:T(8,128)(2,1)} async-done(((bf16[128,16,128]{2,1,0:T(8,128)(2,1)}), bf16[128,16,128]{2,1,0:T(8,128)(2,1)}, u32[]{:S(2)}, u32[]{:S(2)}) %all-to-all-start.4) | async-done | bytes 524320 | tf_op jit(solution)/shard_map/all_to_all | solution.py:18
  111.3 5.4 %all-to-all-start.3 = ((bf16[128,16,128]{2,1,0:T(8,128)(2,1)}), bf16[128,16,128]{2,1,0:T(8,128)(2,1)}, u32[]{:S(2)}, u32[]{:S(2)}) async-start(bf16[128,16,128]{2,1,0:T(8,128)(2,1)} %bitcast.90), calls=%async_computation.3 | async-start | bytes 1048576 | tf_op jit(solution)/shard_map/all_to_all | solution.py:18
  117.6 1.9 slice.48.down1
  121.6 7.8 %all-to-all-done.3 = bf16[128,16,128]{2,1,0:T(8,128)(2,1)} async-done(((bf16[128,16,128]{2,1,0:T(8,128)(2,1)}), bf16[128,16,128]{2,1,0:T(8,128)(2,1)}, u32[]{:S(2)}, u32[]{:S(2)}) %all-to-all-start.3) | async-done | bytes 524320 | tf_op jit(solution)/shard_map/all_to_all | solution.py:18
  129.4 1.0 copy-done.11
  130.4 0.9 copy-done.16
  131.4 1.0 copy-done.36
  132.4 1.0 copy-done.38
  133.4 1.0 copy-done.40
  134.5 5.6 %upper_cols.1 = (bf16[2048,128]{1,0:T(8,128)(2,1)S(1)}, bf16[512,512]{1,0:T(8,128)(2,1)S(1)}, bf16[512,512]{1,0:T(8,128)(2,1)S(1)}, f32[512,512]{1,0:T(8,128)S(1)}) custom-call(bf16[2048,128]{1,0:T(8,128)(2,1)} %bitcast.18.mixed_msg, bf16[2048,128]{1,0:T(8,128)(2,1)} %bitcast.21.cot_msg, bf16[512,512]{1,0:T(8,128)(2,1)S(1)} %copy-done.36, ...), custom_call_target="tpu_custom_call" | custom-call | flops 100000000 | bytes 6817792 | tf_op jit(solution)/shard_map/upper_cols/pallas_call | solution.py:53
  140.1 1.0 copy-done.13
  143.5 5.3 %all-to-all-start.5 = ((bf16[128,16,128]{2,1,0:T(8,128)(2,1)}), bf16[128,16,128]{2,1,0:T(8,128)(2,1)S(1)}, u32[]{:S(2)}, u32[]{:S(2)}) async-start(bf16[128,16,128]{2,1,0:T(8,128)(2,1)} %bitcast.89), calls=%async_computation.5 | async-start | bytes 1048576 | tf_op jit(solution)/shard_map/all_to_all | solution.py:18
  149.6 3.3 %collective-permute-start.9 = (bf16[2,256,256]{2,1,0:T(8,128)(2,1)}, bf16[2,256,256]{2,1,0:T(8,128)(2,1)}, u32[]{:S(2)}, u32[]{:S(2)}) collective-permute-start(bf16[2,256,256]{2,1,0:T(8,128)(2,1)} %get-tuple-element.49), channel_id=1, source_target_pairs={{0,1},{1,0},{2,3},{3,2},{4,5},{5,4},{6,7},{7,6},{8,9},{9,8},{10,11... | collective-permute-start | bytes 786440 | tf_op jit(solution)/shard_map/ppermute | solution.py:22
  152.8 8.9 %all-to-all-done.5 = bf16[128,16,128]{2,1,0:T(8,128)(2,1)S(1)} async-done(((bf16[128,16,128]{2,1,0:T(8,128)(2,1)}), bf16[128,16,128]{2,1,0:T(8,128)(2,1)S(1)}, u32[]{:S(2)}, u32[]{:S(2)}) %all-to-all-start.5) | async-done | bytes 524320 | tf_op jit(solution)/shard_map/all_to_all | solution.py:18
  161.7 1.9 rows_1_back.1
  164.4 8.4 %all-to-all-start.6 = ((bf16[128,16,128]{2,1,0:T(8,128)(2,1)}), bf16[128,16,128]{2,1,0:T(8,128)(2,1)S(1)}, u32[]{:S(2)}, u32[]{:S(2)}) async-start(bf16[128,16,128]{2,1,0:T(8,128)(2,1)} %bitcast.26), calls=%async_computation.6 | async-start | bytes 1048576 | tf_op jit(solution)/shard_map/all_to_all | solution.py:18
  172.8 1.2 maximum_select_fusion.2.x_ref
  174.0 1.6 convolution_convert_fusion
  176.3 3.3 %collective-permute-start.15 = (bf16[2,128,256]{2,1,0:T(8,128)(2,1)}, bf16[2,128,256]{2,1,0:T(8,128)(2,1)}, u32[]{:S(2)}, u32[]{:S(2)}) collective-permute-start(bf16[2,128,256]{2,1,0:T(8,128)(2,1)} %get-tuple-element.62), channel_id=1, source_target_pairs={{0,1},{1,0},{2,3},{3,2},{4,5},{5,4},{6,7},{7,6},{8,9},{9,8},{10,11... | collective-permute-start | bytes 393224 | tf_op jit(solution)/shard_map/ppermute | solution.py:22
  179.5 6.2 %all-to-all-done.6 = bf16[128,16,128]{2,1,0:T(8,128)(2,1)S(1)} async-done(((bf16[128,16,128]{2,1,0:T(8,128)(2,1)}), bf16[128,16,128]{2,1,0:T(8,128)(2,1)S(1)}, u32[]{:S(2)}, u32[]{:S(2)}) %all-to-all-start.6) | async-done | bytes 524320 | tf_op jit(solution)/shard_map/all_to_all | solution.py:18
  185.7 1.2 copy-done.14
  186.9 1.0 copy-done.18
  188.0 1.0 copy-done.20
  189.0 3.8 %lower_cols.1 = (bf16[2048,128]{1,0:T(8,128)(2,1)S(1)}, bf16[512,512]{1,0:T(8,128)(2,1)S(1)}) custom-call(bf16[2048,128]{1,0:T(8,128)(2,1)S(1)} %bitcast.80, f32[512,512]{1,0:T(8,128)S(1)} %copy-done.14, bf16[512,512]{1,0:T(8,128)(2,1)S(1)} %copy-done.18, bf16[512,512]{1,0:T(8,128)(2,1)S(1)} %copy-done.20, bf16[2,256,256]{2,1,0:T(8,128)(2,1)S(1)} %bitcast.77, ...), custom_call_target="tpu_custom_call" | custom-call | flops 100000000 | bytes 6031360 | tf_op jit(solution)/shard_map/lower_cols/pallas_call | solution.py:53
  194.4 5.2 %all-to-all-start.7 = ((bf16[128,16,128]{2,1,0:T(8,128)(2,1)}), bf16[128,16,128]{2,1,0:T(8,128)(2,1)S(1)}, u32[]{:S(2)}, u32[]{:S(2)}) async-start(bf16[128,16,128]{2,1,0:T(8,128)(2,1)} %bitcast.88), calls=%async_computation.7 | async-start | bytes 1048576 | tf_op jit(solution)/shard_map/all_to_all | solution.py:18
  200.1 3.3 %collective-permute-start.14 = (bf16[2,128,256]{2,1,0:T(8,128)(2,1)S(1)}, bf16[2,128,256]{2,1,0:T(8,128)(2,1)S(1)}, u32[]{:S(2)}, u32[]{:S(2)}) collective-permute-start(bf16[2,128,256]{2,1,0:T(8,128)(2,1)S(1)} %get-tuple-element.60), channel_id=1, source_target_pairs={{0,1},{1,0},{2,3},{3,2},{4,5},{5,4},{6,7},{7,6},{8,9},{9,8},{10,11... | collective-permute-start | bytes 393224 | tf_op jit(solution)/shard_map/ppermute | solution.py:22
  204.6 6.8 %collective-permute-done.14 = bf16[2,128,256]{2,1,0:T(8,128)(2,1)S(1)} collective-permute-done((bf16[2,128,256]{2,1,0:T(8,128)(2,1)S(1)}, bf16[2,128,256]{2,1,0:T(8,128)(2,1)S(1)}, u32[]{:S(2)}, u32[]{:S(2)}) %collective-permute-start.14) | collective-permute-done | bytes 131104 | tf_op jit(solution)/shard_map/ppermute | solution.py:22
  211.4 1.1 select_bitcast_fusion.1
  212.4 4.5 %collective-permute-start.16 = (bf16[4,128,256]{2,1,0:T(8,128)(2,1)S(1)}, bf16[4,128,256]{2,1,0:T(8,128)(2,1)S(1)}, u32[]{:S(2)}, u32[]{:S(2)}) collective-permute-start(bf16[4,128,256]{2,1,0:T(8,128)(2,1)S(1)} %get-tuple-element.42), channel_id=1, source_target_pairs={{64,0},{65,1},{66,2},{67,3},{68,4},{69,5},{70,6},{71,7},{72,8},{73... | collective-permute-start | bytes 786440 | tf_op jit(solution)/shard_map/ppermute | solution.py:403
  216.9 1.3 collective-permute-start.17
  219.6 4.8 %collective-permute-done.10 = bf16[2,128,256]{2,1,0:T(8,128)(2,1)S(1)} collective-permute-done((bf16[2,128,256]{2,1,0:T(8,128)(2,1)S(1)}, bf16[2,128,256]{2,1,0:T(8,128)(2,1)S(1)}, u32[]{:S(2)}, u32[]{:S(2)}) %collective-permute-start.10) | collective-permute-done | bytes 131104 | tf_op jit(solution)/shard_map/ppermute | solution.py:22
  224.5 4.2 %collective-permute-start.12 = (bf16[4,128,256]{2,1,0:T(8,128)(2,1)S(1)}, bf16[4,128,256]{2,1,0:T(8,128)(2,1)S(1)}, u32[]{:S(2)}, u32[]{:S(2)}) collective-permute-start(bf16[4,128,256]{2,1,0:T(8,128)(2,1)S(1)} %get-tuple-element.45), channel_id=1, source_target_pairs={{64,0},{65,1},{66,2},{67,3},{68,4},{69,5},{70,6},{71,7},{72,8},{73... | collective-permute-start | bytes 786440 | tf_op jit(solution)/shard_map/ppermute | solution.py:403
  228.7 1.3 collective-permute-start.13
  230.1 1.1 fusion.1
  231.1 1.0 collective-permute-done.13
  232.2 1.1 fusion
  (144 shorter events, 29.6 us)
Async XLA Ops:
  0.6 9.3 %copy-start.48 = (f32[1,256]{1,0:T(1,128)S(1)}, f32[1,256]{1,0:T(1,128)}, u32[]{:S(2)}) copy-start(f32[1,256]{1,0:T(1,128)} %param.13) | copy-start | bytes 3076
  0.6 9.4 %copy-start.49 = (f32[1,256]{1,0:T(1,128)S(1)}, f32[1,256]{1,0:T(1,128)}, u32[]{:S(2)}) copy-start(f32[1,256]{1,0:T(1,128)} %param.12) | copy-start | bytes 3076
  0.6 12.3 %copy-start = (bf16[2048,256]{1,0:T(8,128)(2,1)S(1)}, bf16[2048,256]{1,0:T(8,128)(2,1)}, u32[]{:S(2)}) copy-start(bf16[2048,256]{1,0:T(8,128)(2,1)} %param.10) | copy-start | bytes 3145732
  2.5 27.4 %collective-permute-start.5 = (bf16[2,768,128]{2,1,0:T(8,128)(2,1)}, bf16[2,768,128]{2,1,0:T(8,128)(2,1)}, u32[]{:S(2)}, u32[]{:S(2)}) collective-permute-start(bf16[2,768,128]{2,1,0:T(8,128)(2,1)} %pad_maximum_fusion), channel_id=1, source_target_pairs={{0,33},{1,32},{2,35},{3,34},{4,37},{5,36},{6,39},{7,38},{8,41},{9,... | collective-permute-start | bytes 1179656 | tf_op jit(solution)/shard_map/ppermute | solution.py:277
  9.0 23.2 %collective-permute-start.2 = (bf16[2,256,256]{1,2,0:T(8,128)(2,1)}, bf16[2,256,256]{1,2,0:T(8,128)(2,1)}, u32[]{:S(2)}, u32[]{:S(2)}) collective-permute-start(bf16[2,256,256]{1,2,0:T(8,128)(2,1)} %bitcast.9), channel_id=1, source_target_pairs={{0,64},{64,0},{1,65},{65,1},{2,66},{66,2},{3,67},{67,3},{4,68},{68... | collective-permute-start | bytes 786440 | tf_op jit(solution)/shard_map/ppermute | solution.py:22
  9.9 17.4 %collective-permute-start.7 = (bf16[2,128,512]{2,1,0:T(8,128)(2,1)}, bf16[2,128,512]{2,1,0:T(8,128)(2,1)}, u32[]{:S(2)}, u32[]{:S(2)}) collective-permute-start(bf16[2,128,512]{2,1,0:T(8,128)(2,1)} %bitcast.13), channel_id=1, source_target_pairs={{0,33},{1,32},{2,35},{3,34},{4,37},{5,36},{6,39},{7,38},{8,41},{9,... | collective-permute-start | bytes 786440 | tf_op jit(solution)/shard_map/ppermute | solution.py:277
  9.9 14.9 %collective-permute-start.1 = (f32[1,256]{1,0:T(1,128)S(1)}, f32[1,256]{1,0:T(1,128)}, u32[]{:S(2)}, u32[]{:S(2)}) collective-permute-start(f32[1,256]{1,0:T(1,128)S(1)} %copy-done.48), channel_id=1, source_target_pairs={{0,64},{64,0},{1,65},{65,1},{2,66},{66,2},{3,67},{67,3},{4,68},{68... | collective-permute-start | bytes 3080 | tf_op jit(solution)/shard_map/ppermute | solution.py:22
  10.0 13.7 %collective-permute-start.3 = (f32[2,256]{1,0:T(2,128)S(1)}, f32[2,256]{1,0:T(2,128)S(1)}, u32[]{:S(2)}, u32[]{:S(2)}) collective-permute-start(f32[2,256]{1,0:T(2,128)S(1)} %pad_maximum_fusion.1), channel_id=1, source_target_pairs={{0,33},{1,32},{2,35},{3,34},{4,37},{5,36},{6,39},{7,38},{8,41},{9,... | collective-permute-start | bytes 6152 | tf_op jit(solution)/shard_map/ppermute | solution.py:277
  13.0 8.8 %copy-start.1 = (bf16[1,8,256,256]{3,2,1,0:T(8,128)(2,1)S(1)}, bf16[1,8,256,256]{3,2,1,0:T(8,128)(2,1)}, u32[]{:S(2)}) copy-start(bf16[1,8,256,256]{3,2,1,0:T(8,128)(2,1)} %param.14) | copy-start | bytes 3145732
  14.3 25.0 %all-to-all-start.1 = ((bf16[128,16,128]{2,1,0:T(8,128)(2,1)}), bf16[128,16,128]{2,1,0:T(8,128)(2,1)}, u32[]{:S(2)}, u32[]{:S(2)}) async-start(bf16[128,16,128]{2,1,0:T(8,128)(2,1)} %bitcast.6), calls=%async_computation.1 | async-start | bytes 1048576 | tf_op jit(solution)/shard_map/all_to_all | solution.py:18
  22.7 7.1 %copy-start.44 = (bf16[1,2,512,128]{3,2,1,0:T(8,128)(2,1)S(1)}, bf16[1,2,512,128]{3,2,1,0:T(8,128)(2,1)}, u32[]{:S(2)}) copy-start(bf16[1,2,512,128]{3,2,1,0:T(8,128)(2,1)} %param.18) | copy-start | bytes 786436
  22.7 7.1 %copy-start.46 = (bf16[1,2,128,128]{3,2,1,0:T(8,128)(2,1)S(1)}, bf16[1,2,128,128]{3,2,1,0:T(8,128)(2,1)}, u32[]{:S(2)}) copy-start(bf16[1,2,128,128]{3,2,1,0:T(8,128)(2,1)} %param.19) | copy-start | bytes 196612
  22.7 7.2 %copy-start.47 = (bf16[1,2,128,128]{3,2,1,0:T(8,128)(2,1)S(1)}, bf16[1,2,128,128]{3,2,1,0:T(8,128)(2,1)}, u32[]{:S(2)}) copy-start(bf16[1,2,128,128]{3,2,1,0:T(8,128)(2,1)} %param.16) | copy-start | bytes 196612
  23.7 1.2 copy-start.50
  23.7 11.0 %collective-permute-start = (bf16[4,256,256]{1,2,0:T(8,128)(2,1)}, bf16[4,256,256]{1,2,0:T(8,128)(2,1)S(1)}, u32[]{:S(2)}, u32[]{:S(2)}) collective-permute-start(bf16[4,256,256]{1,2,0:T(8,128)(2,1)} %bitcast.98), channel_id=1, source_target_pairs={{0,64},{64,0},{1,65},{65,1},{2,66},{66,2},{3,67},{67,3},{4,68},{68... | collective-permute-start | bytes 1572872 | tf_op jit(solution)/shard_map/ppermute | solution.py:22
  24.9 1.7 collective-permute-start.4
  29.5 2.7 %copy-start.45 = (bf16[1,2,256,256]{2,3,1,0:T(8,128)(2,1)S(1)}, bf16[1,2,256,256]{2,3,1,0:T(8,128)(2,1)}, u32[]{:S(2)}) copy-start(bf16[1,2,256,256]{2,3,1,0:T(8,128)(2,1)} %copy.14) | copy-start | bytes 786436
  29.5 7.7 %collective-permute-start.8 = (bf16[4,128,512]{2,1,0:T(8,128)(2,1)}, bf16[4,128,512]{2,1,0:T(8,128)(2,1)}, u32[]{:S(2)}, u32[]{:S(2)}) collective-permute-start(bf16[4,128,512]{2,1,0:T(8,128)(2,1)} %maximum_select_fusion.1), channel_id=1, source_target_pairs={{0,64},{64,0},{1,65},{65,1},{2,66},{66,2},{3,67},{67,3},{4,68},{68... | collective-permute-start | bytes 1572872 | tf_op jit(solution)/shard_map/ppermute | solution.py:22
  32.0 17.2 %collective-permute-start.6 = (bf16[4,768,128]{2,1,0:T(8,128)(2,1)}, bf16[4,768,128]{2,1,0:T(8,128)(2,1)}, u32[]{:S(2)}, u32[]{:S(2)}) collective-permute-start(bf16[4,768,128]{2,1,0:T(8,128)(2,1)} %maximum_select_fusion), channel_id=1, source_target_pairs={{0,64},{64,0},{1,65},{65,1},{2,66},{66,2},{3,67},{67,3},{4,68},{68... | collective-permute-start | bytes 2359304 | tf_op jit(solution)/shard_map/ppermute | solution.py:22
  34.7 0.8 copy-start.43
  39.3 23.2 %all-to-all-start = ((bf16[128,16,128]{2,1,0:T(8,128)(2,1)}), bf16[128,16,128]{2,1,0:T(8,128)(2,1)}, u32[]{:S(2)}, u32[]{:S(2)}) async-start(bf16[128,16,128]{2,1,0:T(8,128)(2,1)} %bitcast.4), calls=%async_computation | async-start | bytes 1048576 | tf_op jit(solution)/shard_map/all_to_all | solution.py:18
  50.7 0.9 copy-start.42
  52.9 0.8 copy-start.6
  62.5 1.0 copy-start.4
  63.5 1.0 copy-start.7
  64.6 0.9 copy-start.15
  71.0 0.8 copy-start.19
  74.1 18.1 %all-to-all-start.2 = ((bf16[128,16,128]{2,1,0:T(8,128)(2,1)}), bf16[128,16,128]{2,1,0:T(8,128)(2,1)}, u32[]{:S(2)}, u32[]{:S(2)}) async-start(bf16[128,16,128]{2,1,0:T(8,128)(2,1)} %bitcast.92), calls=%async_computation.2 | async-start | bytes 1048576 | tf_op jit(solution)/shard_map/all_to_all | solution.py:18
  79.6 1.2 copy-start.12
  81.3 0.8 copy-start.9
  92.3 19.0 %all-to-all-start.4 = ((bf16[128,16,128]{2,1,0:T(8,128)(2,1)}), bf16[128,16,128]{2,1,0:T(8,128)(2,1)}, u32[]{:S(2)}, u32[]{:S(2)}) async-start(bf16[128,16,128]{2,1,0:T(8,128)(2,1)} %bitcast.82), calls=%async_computation.4 | async-start | bytes 1048576 | tf_op jit(solution)/shard_map/all_to_all | solution.py:18
  101.0 15.7 %copy-start.2 = (bf16[2,256,256]{1,2,0:T(8,128)(2,1)S(1)}, bf16[2,256,256]{1,2,0:T(8,128)(2,1)}, u32[]{:S(2)}) copy-start(bf16[2,256,256]{1,2,0:T(8,128)(2,1)} %get-tuple-element.58) | copy-start | bytes 786436
  103.1 0.8 copy-start.23
  111.3 18.1 %all-to-all-start.3 = ((bf16[128,16,128]{2,1,0:T(8,128)(2,1)}), bf16[128,16,128]{2,1,0:T(8,128)(2,1)}, u32[]{:S(2)}, u32[]{:S(2)}) async-start(bf16[128,16,128]{2,1,0:T(8,128)(2,1)} %bitcast.90), calls=%async_computation.3 | async-start | bytes 1048576 | tf_op jit(solution)/shard_map/all_to_all | solution.py:18
  116.7 12.6 %copy-start.10 = (bf16[4,128,512]{2,1,0:T(8,128)(2,1)S(1)}, bf16[4,128,512]{2,1,0:T(8,128)(2,1)}, u32[]{:S(2)}) copy-start(bf16[4,128,512]{2,1,0:T(8,128)(2,1)} %get-tuple-element.50.up2) | copy-start | bytes 1572868
  117.6 1.9 copy-start.41
  129.4 1.0 copy-start.11
  130.4 0.9 copy-start.16
  131.4 1.0 copy-start.36
  132.4 1.0 copy-start.38
  133.4 1.0 copy-start.40
  140.1 1.0 copy-start.13
  141.9 0.8 copy-start.28
  143.5 18.2 %all-to-all-start.5 = ((bf16[128,16,128]{2,1,0:T(8,128)(2,1)}), bf16[128,16,128]{2,1,0:T(8,128)(2,1)S(1)}, u32[]{:S(2)}, u32[]{:S(2)}) async-start(bf16[128,16,128]{2,1,0:T(8,128)(2,1)} %bitcast.89), calls=%async_computation.5 | async-start | bytes 1048576 | tf_op jit(solution)/shard_map/all_to_all | solution.py:18
  149.6 23.2 %collective-permute-start.9 = (bf16[2,256,256]{2,1,0:T(8,128)(2,1)}, bf16[2,256,256]{2,1,0:T(8,128)(2,1)}, u32[]{:S(2)}, u32[]{:S(2)}) collective-permute-start(bf16[2,256,256]{2,1,0:T(8,128)(2,1)} %get-tuple-element.49), channel_id=1, source_target_pairs={{0,1},{1,0},{2,3},{3,2},{4,5},{5,4},{6,7},{7,6},{8,9},{9,8},{10,11... | collective-permute-start | bytes 786440 | tf_op jit(solution)/shard_map/ppermute | solution.py:22
  164.4 21.4 %all-to-all-start.6 = ((bf16[128,16,128]{2,1,0:T(8,128)(2,1)}), bf16[128,16,128]{2,1,0:T(8,128)(2,1)S(1)}, u32[]{:S(2)}, u32[]{:S(2)}) async-start(bf16[128,16,128]{2,1,0:T(8,128)(2,1)} %bitcast.26), calls=%async_computation.6 | async-start | bytes 1048576 | tf_op jit(solution)/shard_map/all_to_all | solution.py:18
  174.0 11.7 %copy-start.5 = (bf16[512,512]{1,0:T(8,128)(2,1)S(1)}, bf16[512,512]{1,0:T(8,128)(2,1)}, u32[]{:S(2)}) copy-start(bf16[512,512]{1,0:T(8,128)(2,1)} %copy-done.3) | copy-start | bytes 1572868
  174.0 11.7 %copy-start.8 = (bf16[512,512]{1,0:T(8,128)(2,1)S(1)}, bf16[512,512]{1,0:T(8,128)(2,1)}, u32[]{:S(2)}) copy-start(bf16[512,512]{1,0:T(8,128)(2,1)} %copy-done.6) | copy-start | bytes 1572868
  176.3 28.3 %collective-permute-start.15 = (bf16[2,128,256]{2,1,0:T(8,128)(2,1)}, bf16[2,128,256]{2,1,0:T(8,128)(2,1)}, u32[]{:S(2)}, u32[]{:S(2)}) collective-permute-start(bf16[2,128,256]{2,1,0:T(8,128)(2,1)} %get-tuple-element.62), channel_id=1, source_target_pairs={{0,1},{1,0},{2,3},{3,2},{4,5},{5,4},{6,7},{7,6},{8,9},{9,8},{10,11... | collective-permute-start | bytes 393224 | tf_op jit(solution)/shard_map/ppermute | solution.py:22
  185.7 1.2 copy-start.14
  186.9 1.0 copy-start.18
  188.0 1.0 copy-start.20
  194.4 5.3 %copy-start.22 = (bf16[512,512]{1,0:T(8,128)(2,1)S(1)}, bf16[512,512]{1,0:T(8,128)(2,1)}, u32[]{:S(2)}) copy-start(bf16[512,512]{1,0:T(8,128)(2,1)} %copy-done.21) | copy-start | bytes 1572868
  194.4 5.3 %copy-start.33 = (bf16[512,512]{1,0:T(8,128)(2,1)S(1)}, bf16[512,512]{1,0:T(8,128)(2,1)}, u32[]{:S(2)}) copy-start(bf16[512,512]{1,0:T(8,128)(2,1)} %copy-done.32) | copy-start | bytes 1572868
  194.4 23.8 %all-to-all-start.7 = ((bf16[128,16,128]{2,1,0:T(8,128)(2,1)}), bf16[128,16,128]{2,1,0:T(8,128)(2,1)S(1)}, u32[]{:S(2)}, u32[]{:S(2)}) async-start(bf16[128,16,128]{2,1,0:T(8,128)(2,1)} %bitcast.88), calls=%async_computation.7 | async-start | bytes 1048576 | tf_op jit(solution)/shard_map/all_to_all | solution.py:18
  199.7 3.8 %copy-start.24 = (bf16[2,256,512]{2,1,0:T(8,128)(2,1)S(1)}, bf16[2,256,512]{2,1,0:T(8,128)(2,1)}, u32[]{:S(2)}) copy-start(bf16[2,256,512]{2,1,0:T(8,128)(2,1)} %copy-done.23) | copy-start | bytes 1572868
  199.7 3.7 %copy-start.26 = (bf16[2,256,512]{2,1,0:T(8,128)(2,1)S(1)}, bf16[2,256,512]{2,1,0:T(8,128)(2,1)}, u32[]{:S(2)}) copy-start(bf16[2,256,512]{2,1,0:T(8,128)(2,1)} %copy-done.25) | copy-start | bytes 1572868
  200.1 11.3 %collective-permute-start.14 = (bf16[2,128,256]{2,1,0:T(8,128)(2,1)S(1)}, bf16[2,128,256]{2,1,0:T(8,128)(2,1)S(1)}, u32[]{:S(2)}, u32[]{:S(2)}) collective-permute-start(bf16[2,128,256]{2,1,0:T(8,128)(2,1)S(1)} %get-tuple-element.60), channel_id=1, source_target_pairs={{0,1},{1,0},{2,3},{3,2},{4,5},{5,4},{6,7},{7,6},{8,9},{9,8},{10,11... | collective-permute-start | bytes 393224 | tf_op jit(solution)/shard_map/ppermute | solution.py:22
  203.8 15.8 %collective-permute-start.11 = (bf16[2,128,256]{2,1,0:T(8,128)(2,1)S(1)}, bf16[2,128,256]{2,1,0:T(8,128)(2,1)S(1)}, u32[]{:S(2)}, u32[]{:S(2)}) collective-permute-start(bf16[2,128,256]{2,1,0:T(8,128)(2,1)S(1)} %get-tuple-element.66), channel_id=1, source_target_pairs={{0,1},{1,0},{2,3},{3,2},{4,5},{5,4},{6,7},{7,6},{8,9},{9,8},{10,11... | collective-permute-start | bytes 393224 | tf_op jit(solution)/shard_map/ppermute | solution.py:22
  212.4 17.6 %collective-permute-start.16 = (bf16[4,128,256]{2,1,0:T(8,128)(2,1)S(1)}, bf16[4,128,256]{2,1,0:T(8,128)(2,1)S(1)}, u32[]{:S(2)}, u32[]{:S(2)}) collective-permute-start(bf16[4,128,256]{2,1,0:T(8,128)(2,1)S(1)} %get-tuple-element.42), channel_id=1, source_target_pairs={{64,0},{65,1},{66,2},{67,3},{68,4},{69,5},{70,6},{71,7},{72,8},{73... | collective-permute-start | bytes 786440 | tf_op jit(solution)/shard_map/ppermute | solution.py:403
  216.9 13.1 %collective-permute-start.17 = (bf16[4,128,256]{2,1,0:T(8,128)(2,1)S(1)}, bf16[4,128,256]{2,1,0:T(8,128)(2,1)S(1)}, u32[]{:S(2)}, u32[]{:S(2)}) collective-permute-start(bf16[4,128,256]{2,1,0:T(8,128)(2,1)S(1)} %get-tuple-element.41), channel_id=1, source_target_pairs={{0,64},{1,65},{2,66},{3,67},{4,68},{5,69},{6,70},{7,71},{8,72},{9,... | collective-permute-start | bytes 786440 | tf_op jit(solution)/shard_map/ppermute | solution.py:402
  219.0 5.4 %collective-permute-start.10 = (bf16[2,128,256]{2,1,0:T(8,128)(2,1)S(1)}, bf16[2,128,256]{2,1,0:T(8,128)(2,1)S(1)}, u32[]{:S(2)}, u32[]{:S(2)}) collective-permute-start(bf16[2,128,256]{2,1,0:T(8,128)(2,1)S(1)} %get-tuple-element.64), channel_id=1, source_target_pairs={{0,1},{1,0},{2,3},{3,2},{4,5},{5,4},{6,7},{7,6},{8,9},{9,8},{10,11... | collective-permute-start | bytes 393224 | tf_op jit(solution)/shard_map/ppermute | solution.py:22
  224.5 6.6 %collective-permute-start.12 = (bf16[4,128,256]{2,1,0:T(8,128)(2,1)S(1)}, bf16[4,128,256]{2,1,0:T(8,128)(2,1)S(1)}, u32[]{:S(2)}, u32[]{:S(2)}) collective-permute-start(bf16[4,128,256]{2,1,0:T(8,128)(2,1)S(1)} %get-tuple-element.45), channel_id=1, source_target_pairs={{64,0},{65,1},{66,2},{67,3},{68,4},{69,5},{70,6},{71,7},{72,8},{73... | collective-permute-start | bytes 786440 | tf_op jit(solution)/shard_map/ppermute | solution.py:403
  228.7 3.4 %collective-permute-start.13 = (bf16[4,128,256]{2,1,0:T(8,128)(2,1)S(1)}, bf16[4,128,256]{2,1,0:T(8,128)(2,1)S(1)}, u32[]{:S(2)}, u32[]{:S(2)}) collective-permute-start(bf16[4,128,256]{2,1,0:T(8,128)(2,1)S(1)} %get-tuple-element.44), channel_id=1, source_target_pairs={{0,64},{1,65},{2,66},{3,67},{4,68},{5,69},{6,70},{7,71},{8,72},{9,... | collective-permute-start | bytes 786440 | tf_op jit(solution)/shard_map/ppermute | solution.py:402
  (13 other events, 10.3 us)

commit v2 on v1

v2 whole, which is shorter than its diff:
```python
import math

import jax
import jax.numpy as jnp
from jax import lax
from jax.experimental import pallas as pl
from jax.experimental.pallas import tpu as pltpu
from jax.sharding import PartitionSpec as P


ROWS_ORDER = ("seq", "segment", "mp")
QUARTER_ORDER = ("mp", "seq", "segment")
BF = jnp.bfloat16
F32 = jnp.float32
MSG = (2048, 128)
OWNERS = 128
TILES = (OWNERS, 16, 128)
PAIR = (OWNERS, 2, 16, 128)
VMEM_BYTES = 67043328
SPARE = 2**17
WEIGHT_ROWS = 2560


def exchange(message, order):
    return lax.all_to_all(message, order, split_axis=0, concat_axis=0, tiled=True)


def swap(value, axis):
    return lax.ppermute(value, axis, [(0, 1), (1, 0)])


def dot(a, b):
    return jnp.dot(a, b, preferred_element_type=F32)


def dot_nt(a, b):
    return lax.dot_general(a, b, (((1,), (1,)), ((), ())), preferred_element_type=F32)


def sigmoid(v):
    return 0.5 * jnp.tanh(0.5 * v) + 0.5


def slope(v):
    s = sigmoid(v)
    return s * (1.0 + v * (1.0 - s))


class Loaded:
    def __init__(self, source, buffer, sem):
        self.copy, self.buffer, self.ready = pltpu.make_async_copy(source, buffer, sem), buffer, False
        self.copy.start()

    def get(self):
        if not self.ready:
            self.copy.wait()
            self.ready = True
        return self.buffer

    def __getitem__(self, index):
        return self.get()[index]


class Result:
    def __init__(self, target, buffer, sems):
        self.target, self.ref, self.sems, self.copies = target, buffer, sems, []

    def send(self, *index):
        source, target = (self.ref.at[index], self.target.at[index]) if index else (self.ref, self.target)
        copy = pltpu.make_async_copy(source, target, self.sems.at[len(self.copies)])
        copy.start()
        self.copies.append(copy)


class Near:
    def __init__(self, value):
        self.value = value


def call(body, outs, scratch, args, after=()):
    near_in = [isinstance(a, Near) for a in args]
    near_out = [isinstance(o, Near) for o in outs]
    args = [a.value if isinstance(a, Near) else a for a in args]
    args = [a if isinstance(a, tuple) else (a, None, a.shape) for a in args]
    outs = [o.value if isinstance(o, Near) else o for o in outs]
    far_in = [n for n, near in enumerate(near_in) if not near]
    far_out = [n for n, near in enumerate(near_out) if not near]
    total = len(args) + len(after)

    def kernel(*refs):
        sources, targets = refs[: len(args)], refs[total : total + len(outs)]
        rest = refs[total + len(outs) :]
        buffers, rest = rest[: len(far_in)], rest[len(far_in) :]
        results, rest = rest[: len(far_out)], rest[len(far_out) :]
        sems, out_sems, *extra = rest
        loads, stores = list(sources), list(targets)
        for k, n in enumerate(far_in):
            view = args[n][1]
            loads[n] = Loaded(view(sources[n]) if view else sources[n], buffers[k], sems.at[k])
        for k, n in enumerate(far_out):
            stores[n] = Result(targets[n], results[k], out_sems.at[k])
        body(loads, stores, *extra)
        for n in far_in:
            loads[n].get()
        for n in far_out:
            if not stores[n].copies:
                stores[n].send()
        for n in far_out:
            for copy in stores[n].copies:
                copy.wait()

    moved = sum(math.prod(shape) * a.dtype.itemsize for a, view, shape in args)
    moved += sum(math.prod(shape) * jnp.dtype(dtype).itemsize for shape, dtype in outs)
    held = sum(math.prod(args[n][0].shape) * args[n][0].dtype.itemsize for n in range(len(args)) if near_in[n])
    held += sum(math.prod(outs[n][0]) * jnp.dtype(outs[n][1]).itemsize for n in range(len(outs)) if near_out[n])
    near, far = pl.BlockSpec(memory_space=pltpu.VMEM), pl.BlockSpec(memory_space=pltpu.HBM)
    return pl.pallas_call(
        kernel,
        out_shape=tuple(jax.ShapeDtypeStruct(*o) for o in outs),
        in_specs=[near if n else far for n in near_in]
        + [pl.BlockSpec(memory_space=pl.ANY)] * len(after),
        out_specs=tuple(near if n else far for n in near_out),
        scratch_shapes=[pltpu.VMEM(args[n][2], args[n][0].dtype) for n in far_in]
        + [pltpu.VMEM(*outs[n]) for n in far_out]
        + [pltpu.SemaphoreType.DMA((max(1, len(far_in)),)), pltpu.SemaphoreType.DMA((max(1, len(far_out)), 8))]
        + [pltpu.VMEM(s, d) for s, d in scratch],
        compiler_params=pltpu.CompilerParams(vmem_limit_bytes=VMEM_BYTES - held - SPARE),
        cost_estimate=pl.CostEstimate(flops=10**8, bytes_accessed=moved, transcendentals=0),
    )(*[a[0] for a in args], *after)


def core():
    return lax.axis_index("segment")


def side():
    return lax.axis_index("mp")


def widen(msg, wide):
    wide[...] = msg.reshape(MSG).astype(F32)


def narrow(packed):
    return packed[...].reshape(TILES).astype(BF)


def pack_quarter(values, a, out, temp):
    for h in range(2):
        temp[...] = values[:, h * 128 : (h + 1) * 128]
        for mm in range(2):
            for oo in range(2):
                row = mm * 1024 + a * 4 + oo * 2 + h
                out[pl.ds(row, 64, stride=16), :] = temp[pl.ds(mm * 2 + oo, 64, stride=4), :]


def unpack_quarter(source, oo):
    parts = [
        source[pl.ds(mm * 1024 + oo * 2 + h, 256, stride=4), :] for mm in range(2) for h in range(2)
    ]
    return jnp.concatenate(parts, axis=1)


def pack_quarter_rows(values, a, out, temp):
    for h in range(2):
        temp[...] = values[:, h * 128 : (h + 1) * 128]
        for oo in range(2):
            out[pl.ds(a * 4 + oo * 2 + h, 128, stride=16), :] = temp[pl.ds(oo, 128, stride=2), :]


def unpack_quarter_rows(source, oo, temp):
    for mm in range(2):
        for h in range(2):
            for a in range(4):
                temp[mm * 2 + h, pl.ds(a, 64, stride=4), :] = source[
                    pl.ds(mm * 16 + a * 4 + oo * 2 + h, 64, stride=32), :
                ]
    return jnp.concatenate([temp[n] for n in range(4)], axis=1)


def pack_cols(values, oo, out):
    for cq in range(4):
        out[pl.ds(oo * 4 + cq, 256, stride=8), :] = values[:, cq * 128 : (cq + 1) * 128]


def unpack_cols(source, oo):
    return jnp.concatenate(
        [source[pl.ds(oo * 4 + cq, 256, stride=8), :] for cq in range(4)], axis=1
    )


def pack_rows(values, a2, out, temp):
    for cq in range(4):
        temp[...] = values[:, cq * 128 : (cq + 1) * 128]
        for oo in range(2):
            out[pl.ds(a2 * 8 + oo * 4 + cq, 128, stride=16), :] = temp[pl.ds(oo, 128, stride=2), :]


def unpack_rows(source, a2, temp):
    for cq in range(4):
        for oo in range(2):
            temp[cq, pl.ds(oo, 128, stride=2), :] = source[
                pl.ds(a2 * 8 + oo * 4 + cq, 128, stride=16), :
            ]
    return jnp.concatenate([temp[cq] for cq in range(4)], axis=1)


def slice_body(ins, outs):
    outs[0].ref[...] = ins[0][...]


def pack_cot_body(ins, outs, packed, temp):
    (x_ref,) = ins
    for a in range(4):
        pack_quarter_rows(x_ref[a].astype(F32), a, packed, temp)
    outs[0][...] = narrow(packed)


def pack_body(ins, outs, packed, temp):
    x_ref, up1, ds, d1, up2 = ins
    out, x_out, x_tiles = outs
    for i in range(2):
        out[i * 128 : (i + 1) * 128, :] = up1[i]
        out[256 + i * 128 : 256 + (i + 1) * 128, :] = ds[i]
        out[512 + i * 512 : 512 + (i + 1) * 512, :] = d1[i]
        for cq in range(4):
            row = 1536 + (i * 4 + cq) * 128
            out[row : row + 128, :] = up2[i, :, cq * 128 : (cq + 1) * 128]
    for a in range(4):
        x_out[a] = x_ref[a]
        pack_quarter(x_ref[a].astype(F32), a, packed, temp)
    x_tiles[...] = narrow(packed)


def first_rows_body(ins, outs, packed, temp):
    x_ref, x_tiles, key_mine, key_got, mine_ref, got_ref = ins
    g = core()
    key = jnp.where(g == 0, key_mine[...], key_got[...])
    for a in range(4):
        factor = jnp.where(g == 0, mine_ref[a], got_ref[4 * g + a])
        scaled = (x_ref[a].astype(F32) * key).astype(BF)
        pack_quarter(dot(factor, scaled), a, packed, temp)
    outs[0][:, 1] = x_tiles[...]
    outs[0][:, 0] = narrow(packed)


def weights_body(layer, ins, outs):
    g, m = core(), side()
    own_ref, peer_ref, other_ref, both_ref = ins[:4]
    u_ref, v_ref, up2_ref, d1_ref = (o.ref for o in outs[:4])

    def block(start, rows, mine):
        part = slice(start, start + rows)
        here = jnp.where(mine, own_ref[part, :], peer_ref[part, :])
        there = jnp.where(mine, other_ref[part, :], both_ref[part, :])
        return jnp.where(g == layer, here, there)

    rho = lax.broadcasted_iota(jnp.int32, (128, 512), 0)
    gam = lax.broadcasted_iota(jnp.int32, (128, 512), 1)
    same = (gam // 128) * 32 + gam % 32 == rho
    for k in range(4):
        i, mine = k % 2, m == k // 2
        spot = jnp.where(same & ((gam // 32) % 4 == k), 1.0, 0.0).astype(BF)
        u_ref[k * 128 : (k + 1) * 128, :] = dot(block(i * 128, 128, mine), spot).astype(BF)
        spread = lax.dot_general(
            spot, block(256 + i * 128, 128, mine), (((0,), (0,)), ((), ())),
            preferred_element_type=F32,
        )
        v_ref[:, k * 128 : (k + 1) * 128] = spread.astype(BF)
        d1_ref[k] = block(512 + i * 512, 512, mine)
        for cq in range(4):
            up2_ref[k, :, cq * 128 : (cq + 1) * 128] = block(1536 + (i * 4 + cq) * 128, 128, mine)
        for out in outs[2:4]:
            out.send(k)
    if layer == 1:
        return
    own, peer, other, both = (n[...] for n in ins[6:10])
    for half in range(2):
        lanes = slice(half * 256, (half + 1) * 256)
        mine = jnp.where(m == half, own, peer)
        got = jnp.where(m == half, other, both)
        outs[4].ref[:, lanes] = jnp.where(g == 0, mine, got)
        outs[5].ref[:, lanes] = jnp.where(g == 0, got, mine)
    for oo in range(2):
        outs[6].ref[oo] = jnp.where(g == 0, ins[4][oo], ins[5][oo])


def factors_body(ins, outs):
    g = core()
    first_mine, first_got, second_mine, second_got = ins
    first1, first1_t, second1, second1_t, second0_t = (o.ref for o in outs)
    for i in range(2):
        first = jnp.where(g == 1, first_mine[i], first_got[i])
        first1[i] = first
        first1_t[i] = first.astype(F32).T.astype(BF)
        second = jnp.where(g == 1, second_mine[i], second_got[i])
        second1[i] = second
        second1_t[i] = second.astype(F32).T.astype(BF)
        second = jnp.where(g == 0, second_mine[i], second_got[i])
        second0_t[i] = second.astype(F32).T.astype(BF)


def forward_cols_body(ins, outs, wide, wide_x, packed):
    msg, factor, gains0, gains1, u, up2, down1, v = ins
    out_msg, mixed_out, x_out, hidden_out, middle_out = outs
    widen(msg[:, 0], wide)
    widen(msg[:, 1], wide_x)
    for oo in range(2):
        mixed = unpack_quarter(wide, oo).astype(BF)
        x = unpack_quarter(wide_x, oo)
        turned = dot(factor[oo], mixed).astype(BF)
        pre = x * gains0[0:1, :]
        hidden = (x + pre * sigmoid(pre) * turned.astype(F32)).astype(BF)
        for out, value in ((mixed_out, mixed), (x_out, x.astype(BF)), (hidden_out, hidden)):
            out.ref[oo] = value
            out.send(oo)
        permuted = dot(hidden, u[...]).astype(BF)
        folds = []
        for j in range(4):
            preact = dot(permuted[:, j * 128 : (j + 1) * 128], up2[j])
            active = (preact * sigmoid(preact)).astype(BF)
            folds.append(dot(active, down1[j]).astype(BF))
        out = dot(jnp.concatenate(folds, axis=1), v[...])
        middle = (hidden.astype(F32) + out).astype(BF)
        middle_out.ref[oo] = middle
        middle_out.send(oo)
        pack_cols(middle.astype(F32) * gains1[1:2, :], oo, packed)
    out_msg[...] = narrow(packed)


def rows_body(ins, outs, wide, packed, temp, temp4):
    msg, factor, more = ins
    widen(msg[...], wide)
    for a2 in range(2):
        values = unpack_rows(wide, a2, temp4).astype(BF)
        outs[1].ref[a2] = values
        outs[1].send(a2)
        result = dot(factor[a2], values)
        if len(outs[0].shape) == 3:
            result = result * more[1:2, :]
        pack_rows(result, a2, packed, temp)
    if len(outs[0].shape) == 3:
        outs[0][...] = narrow(packed)
    else:
        outs[0][:, 1] = more[...]
        outs[0][:, 0] = narrow(packed)


def grad_body(ins, outs):
    outer, inner = ins
    for i in range(2):
        grad = dot_nt(outer[i], inner[i]).astype(BF)
        outs[0].ref[0, i] = grad[:128]
        outs[0].ref[1, i] = grad[128:]


def second_grads_body(ins, outs, own, other):
    g, m = core(), side()
    outer, inner, upper = ins
    for i in range(2):
        grad = dot_nt(outer[i], inner[i]).astype(BF)
        for half in range(2):
            lower = grad[half * 128 : (half + 1) * 128]
            own[half, i] = jnp.where(g == 0, lower, upper[half, i])
            other[half, i] = jnp.where(g == 0, upper[half, i], lower)
    for out, (source, half) in zip(outs, ((own, m), (own, 1 - m), (other, m), (other, 1 - m))):
        out[...] = source[half]


def last_rows_body(ins, outs, wide, temp4):
    msg, x_own, x_peer, gains, upper = ins
    m = side()
    widen(msg[...], wide)
    for a2 in range(2):
        values = unpack_rows(wide, a2, temp4).astype(BF)
        own, peer = x_own[a2].astype(F32), x_peer[a2].astype(F32)
        low = (jnp.where(m == 0, own, peer) * gains[1:2, :256]).astype(BF)
        high = (jnp.where(m == 0, peer, own) * gains[1:2, 256:]).astype(BF)
        grad = dot_nt(values[:, :256], low) + dot_nt(values[:, 256:], high)
        outs[0][0, a2] = grad[:128].astype(BF)
        outs[0][1, a2] = grad[128:].astype(BF)
    for half in range(2):
        outs[0][2 + half] = upper[half]


def collect_body(ins, outs):
    g, m = core(), side()
    owners = 2 * g + m, 2 * (1 - g) + m, 2 * g + 1 - m, 2 * (1 - g) + 1 - m
    for n, owner in enumerate(owners):
        part = pl.ds(2 * owner, 2)
        outs[0].ref[part] = ins[n][...].astype(F32)
        outs[0].send(part)


def ffn_back(cot, hidden, u, v, up2, down1):
    permuted = dot(hidden, u[...]).astype(BF)
    fold = dot_nt(cot, v[...]).astype(BF)
    perms = []
    for j in range(4):
        block = slice(j * 128, (j + 1) * 128)
        preact = dot(permuted[:, block], up2[j])
        back_active = dot_nt(fold[:, block], down1[j])
        back_preact = (back_active * slope(preact)).astype(BF)
        perms.append(dot_nt(back_preact, up2[j]).astype(BF))
    return cot.astype(F32) + dot_nt(jnp.concatenate(perms, axis=1), u[...])


def upper_cols_body(ins, outs, wide, wide_c, packed, temp4):
    msg, factor, x_ref, gains, v, u, up2, down1, factor_t = ins
    out_msg, mixed_out, back_turned_out, direct_out = outs
    widen(msg[:, 0], wide)
    widen(msg[:, 1], wide_c)
    for oo in range(2):
        mixed = unpack_cols(wide, oo).astype(BF)
        cot = unpack_quarter_rows(wide_c, oo, temp4).astype(BF)
        mixed_out.ref[oo] = mixed
        mixed_out.send(oo)
        gate = gains[0:1, :]
        x = x_ref[oo].astype(F32)
        turned = dot(factor[oo], mixed).astype(BF).astype(F32)
        pre = x * gate
        logistic = sigmoid(pre)
        gated = pre * logistic
        hidden = (x + gated * turned).astype(BF)
        back_hidden = ffn_back(cot, hidden, u, v, up2, down1)
        back_turned = (back_hidden * gated).astype(BF)
        back_turned_out.ref[oo] = back_turned
        back_turned_out.send(oo)
        pack_cols(dot(factor_t[oo], back_turned), oo, packed)
        gate_slope = logistic * (1.0 + pre * (1.0 - logistic))
        direct_out.ref[oo] = back_hidden + back_hidden * turned * gate_slope * gate
        direct_out.send(oo)
    out_msg[...] = narrow(packed)


def lower_cols_body(ins, outs, wide, packed):
    msg, direct0, hidden_ref, v, u, up2, down1, direct1, x_ref, gains, factor_t = ins
    direct = direct0, direct1
    out_msg, back_turned_out = outs
    widen(msg[...], wide)
    for oo in range(2):
        passed = (direct[oo][...] + unpack_cols(wide, oo)).astype(BF)
        back_hidden = ffn_back(passed, hidden_ref[oo], u, v, up2, down1)
        pre = x_ref[oo].astype(F32) * gains[0:1, :]
        back_turned = (back_hidden * (pre * sigmoid(pre))).astype(BF)
        back_turned_out.ref[oo] = back_turned
        back_turned_out.send(oo)
        pack_cols(dot(factor_t[oo], back_turned), oo, packed)
    out_msg[...] = narrow(packed)


def layer_pair(
    inputs,
    cotangent,
    gate_gain,
    key_gain,
    first_factor,
    second_factor,
    up_first,
    up_second,
    down_first,
    down_second_weight,
):
    g, m = core(), side()
    rows = inputs.reshape(8, 256, 256)
    cot_rows = cotangent.reshape(8, 256, 256)
    first_mine, second_mine = first_factor[0], second_factor[0]
    seq_count = lax.axis_size("seq")

    def swap_z(value, layers):
        pairs = [
            ((layer * seq_count + q) * 2 + end, (layer * seq_count + (q ^ (seq_count // 2))) * 2 + 1 - end)
            for layer in layers
            for q in range(seq_count)
            for end in range(2)
        ]
        return lax.ppermute(value, ("segment", "seq", "mp"), pairs)

    def give(value, layer):
        return lax.ppermute(value, "segment", [(layer, 1 - layer)])

    def two(array):
        def view(ref):
            return ref.at[pl.ds(2 * (2 * core() + side()), 2)]

        return array, view, (2,) + array.shape[1:]

    def four(array):
        def view(ref):
            return ref.at[pl.ds(4 * core(), 4)]

        return array, view, (4,) + array.shape[1:]

    def part(array, n):
        return array, lambda ref: ref.at[n], array.shape[1:]

    tiles = Near((TILES, BF))
    scratch_pack = [(MSG, F32), ((256, 128), F32)]

    key_got = swap(key_gain, "segment")
    own, x_rows, x_tiles = call(
        pack_body,
        [Near(((WEIGHT_ROWS, 128), BF)), Near(((4, 256, 256), BF)), tiles],
        scratch_pack,
        (four(rows), up_first[0], down_second_weight[0], down_first[0], up_second[0]),
    )
    first_got = swap(first_mine, "segment")
    peer0 = swap_z(own, (0,))
    (rows_msg,) = call(
        first_rows_body,
        [Near((PAIR, BF))],
        scratch_pack,
        (Near(x_rows), Near(x_tiles), key_gain, key_got, Near(first_mine), Near(first_got)),
    )

    def send(message, order=ROWS_ORDER):
        shape = message.shape
        return exchange(message.reshape(-1, 128), order).reshape(shape)

    msg = send(rows_msg, QUARTER_ORDER)

    second_got = swap(second_mine, "segment")
    gains = jnp.concatenate([gate_gain, key_gain])
    gains_peer = swap_z(gains, (0, 1))
    gains_got = swap(gains, "segment")
    gains_both = swap(gains_peer, "segment")
    other0 = give(own, 0)
    both0 = give(peer0, 0)
    square = ((512, 512), BF)
    layer_outs = [square, square, ((4, 128, 512), BF), ((4, 512, 128), BF)]
    gain = ((2, 512), F32)
    pair = ((2, 256, 256), BF)
    u0, v0, up0, down0, gains0, gains1, second0 = call(
        lambda ins, outs: weights_body(0, ins, outs),
        layer_outs + [gain, gain, pair],
        [],
        (
            own, peer0, other0, both0, two(second_mine), two(second_got),
            gains, gains_peer, gains_got, gains_both,
        ),
    )

    (x_sent,) = call(
        slice_body,
        [((2, 256, 256), BF)],
        [],
        ((rows, lambda ref: ref.at[pl.ds(2 * (2 * core() + 1 - side()), 2)], (2, 256, 256)),),
        after=(u0,),
    )
    x_peer = swap(x_sent, "mp")

    block = ((2, 256, 512), BF)
    next_msg, mixed0, x0, hidden0, middle = call(
        forward_cols_body,
        [tiles] + [block] * 4,
        [(MSG, F32)] * 3,
        (Near(msg), second0, gains0, gains1, u0, up0, down0, v0),
    )
    msg = send(next_msg)
    peer1 = swap_z(own, (1,))
    other1 = give(own, 1)
    first1, first1_t, second1, second1_t, second0_t = call(
        factors_body,
        [pair] * 5,
        [],
        (two(first_mine), two(first_got), two(second_mine), two(second_got)),
        after=(next_msg,),
    )
    (cot_tiles,) = call(pack_cot_body, [tiles], scratch_pack, (four(cot_rows),), after=(first1,))

    scratch_rows = [(MSG, F32), (MSG, F32), ((256, 128), F32), ((4, 256, 128), F32)]
    next_msg, scaled1 = call(
        rows_body, [Near((PAIR, BF)), block], scratch_rows, (Near(msg), first1, Near(cot_tiles))
    )
    msg = send(next_msg)
    both1 = give(peer1, 1)
    u1, v1, up1, down1 = call(
        lambda ins, outs: weights_body(1, ins, outs), layer_outs, [], (own, peer1, other1, both1)
    )
    next_msg, mixed1, back_turned1, direct = call(
        upper_cols_body,
        [tiles, block, block, ((2, 256, 512), F32)],
        [(MSG, F32)] * 3 + [((4, 256, 128), F32)],
        (Near(msg), *(Near(a) for a in (second1, middle, gains1, v1, u1, up1, down1, second1_t))),
    )
    msg = send(next_msg)

    halves = ((2, 2, 128, 256), BF)

    def channel_grad(outer, inner, after):
        (grad,) = call(grad_body, [halves], [], (outer, inner), after=(after,))
        return grad

    second_grad1 = channel_grad(back_turned1, mixed1, next_msg)

    next_msg, back_rows1 = call(
        rows_body, [tiles, block], scratch_rows, (Near(msg), first1_t, gains1)
    )
    msg = send(next_msg)
    first_grad1 = channel_grad(back_rows1, scaled1, next_msg)

    next_msg, back_turned0 = call(
        lower_cols_body,
        [tiles, block],
        [(MSG, F32)] * 2,
        (Near(msg), part(direct, 0), hidden0, v0, u0, up0, down0, part(direct, 1), x0, gains0, second0_t),
    )
    msg = send(next_msg)
    half = Near(((2, 128, 256), BF))
    mine, own_theirs, other_mine, other_theirs = call(
        second_grads_body,
        [half] * 4,
        [halves] * 2,
        (back_turned0, mixed0, second_grad1),
        after=(next_msg,),
    )
    from_side = swap(own_theirs, "mp")
    from_both = lax.ppermute(other_theirs, ("segment", "mp"), [(0, 3), (1, 2), (2, 1), (3, 0)])
    from_core = swap(other_mine, "segment")

    (message,) = call(
        last_rows_body,
        [Near(((4, 2, 128, 256), BF))],
        [(MSG, F32), ((4, 256, 128), F32)],
        (Near(msg), two(rows), x_peer, gains0, first_grad1),
    )
    grad_first = lax.all_to_all(message, ("segment", "mp"), split_axis=0, concat_axis=0, tiled=True)
    (grad_second,) = call(
        collect_body,
        [((8, 128, 256), F32)],
        [],
        (mine, from_core, from_side, from_both),
        after=(message,),
    )
    return grad_first.reshape(1, 8, 128, 256).astype(F32), grad_second[None]


def solution(mesh):
    placed = (
        P("seq", "mp"),
        P("seq", "mp"),
        P("segment", "mp"),
        P("segment", "mp"),
        P("segment", "seq", None, None),
        P("segment", "seq", None, None),
        P("segment", "mp", None, None),
        P("segment", "mp", None, None),
        P("segment", "mp", None, None),
        P("segment", "mp", None, None),
    )
    return jax.shard_map(
        layer_pair,
        mesh=mesh,
        in_specs=placed,
        out_specs=(P("segment", "seq", "mp", None), P("segment", "seq", "mp", None)),
        check_vma=False,
    )
```

time: 235 us -> 214 us (0.911)
  Pallas kernels: 23 us -> 69.5 us
  local copies, waits for them, and re-layouts: 40.8 us -> 2.44 us
  blocking collectives: 0 us -> 37.3 us
  waiting for transfers between devices: 61.4 us -> 29.5 us
  other arithmetic: 18.3 us -> 2.11 us
  starting transfers between devices: 86.3 us -> 70.6 us
    pallas_call x11 -> x17, Pallas kernels: 23 us -> 69.5 us  [call(): pl.pallas_call(kernel, out_shape=tuple((jax.ShapeDtypeStruct(*o) for o in...]
    all_to_all x8 -> x4, waiting for transfers between devices: 48.3 us -> 9.41 us  [exchange(): lax.all_to_all(message, order, split_axis=0, concat_axis=0, tiled=True)]
    all_to_all x0 -> x2, blocking collectives: none -> 37.3 us  [exchange(): lax.all_to_all(message, order, split_axis=0, concat_axis=0, tiled=True)]
    unnamed x102 -> x26, local copies, waits for them, and re-layouts: 28.9 us -> 2.44 us
    all_to_all x8 -> x4, starting transfers between devices: 53 us -> 28.7 us  [exchange(): lax.all_to_all(message, order, split_axis=0, concat_axis=0, tiled=True)]
    select_n x10 -> x0, other arithmetic: 13.1 us -> none  [pick(): return jnp.where(flag == 0, when_zero, when_one)]
    dynamic_slice x8 -> x0, local copies, waits for them, and re-layouts: 6.35 us -> none  [the longest x2 1.92 us: on_device(): second_own = lax.dynamic_slice_in_dim(second_mine, 2 * r, 2, 0)]
    all_to_all x0 -> x1, starting transfers between devices: none -> 4.76 us  [layer_pair(): lax.all_to_all(message, ('segment', 'mp'), split_axis=0, concat_axis=0, t...]
  transfers between devices with their start and end apart: 26 -> 21, of which waited for: 10 -> 9; matrix products, arithmetic and copies ran while one was open for 13% -> 0% of each run, Pallas kernels for 5% -> 17%
where the time goes in v2:
time: 214 us; the launch traced here: 212 us
  starting transfers between devices  70.6 us (33%)
  Pallas kernels  69.5 us (32%)
  blocking collectives  37.3 us (17%)
  waiting for transfers between devices  29.5 us (14%)
  local copies, waits for them, and re-layouts  2.44 us (1%)
    pallas_call x17, Pallas kernels, call(): pl.pallas_call(kernel, out_shape=tuple((jax.ShapeDtypeStruct(*o) for o in...  69.5 us
    all_to_all x2, blocking collectives, exchange(): lax.all_to_all(message, order, split_axis=0, concat_axis=0, tiled=True)  37.3 us
    all_to_all x4, starting transfers between devices, exchange(): lax.all_to_all(message, order, split_axis=0, concat_axis=0, tiled=True)  28.7 us
    ppermute x8, starting transfers between devices, swap(): return lax.ppermute(value, axis, [(0, 1), (1, 0)])  18.8 us
    ppermute x8, waiting for transfers between devices, swap(): return lax.ppermute(value, axis, [(0, 1), (1, 0)])  15.2 us
    all_to_all x4, waiting for transfers between devices, exchange(): lax.all_to_all(message, order, split_axis=0, concat_axis=0, tiled=True)  9.41 us
    ppermute x3, starting transfers between devices, swap_z(): return lax.ppermute(value, ('segment', 'seq', 'mp'), pairs)  9.15 us
    ppermute x4, starting transfers between devices, give(): return lax.ppermute(value, 'segment', [(layer, 1 - layer)])  8.81 us
  transfers between devices with their start and end apart: 21, of which 9 were waited for; matrix products, arithmetic and copies ran while one was open for 0% of the time, Pallas kernels for 17%

profile of v2, /device:TPU:1, one launch (start us, length us, event | category | flops | bytes accessed | tf_op | source)
XLA Modules:
  0.0 212.3 jit_solution(3573154708945107036)
XLA Ops:
  0.6 0.0 copy-start
  0.6 1.5 collective-permute-start.1
  2.1 2.8 %shard_map.113 = (bf16[2560,128]{1,0:T(8,128)(2,1)}, bf16[4,256,256]{2,1,0:T(8,128)(2,1)}, bf16[128,16,128]{2,1,0:T(8,128)(2,1)}) custom-call(bf16[8,256,256]{2,1,0:T(8,128)(2,1)} %bitcast.17, bf16[2,128,128]{2,1,0:T(8,128)(2,1)} %bitcast.32, bf16[2,128,128]{2,1,0:T(8,128)(2,1)} %bitcast.33, bf16[2,512,128]{2,1,0:T(8,128)(2,1)} %bitcast.30, ...), custom_call_target="tpu_custom_call" | custom-call | flops 100000000 | bytes 2883584 | tf_op jit(solution)/shard_map/pallas_call | solution.py:117
  4.9 0.0 copy-start.6
  4.9 0.7 collective-permute-start.2
  5.7 5.5 %collective-permute-start.5 = (bf16[8,256,256]{2,1,0:T(8,128)(2,1)S(1)}, bf16[8,256,256]{2,1,0:T(8,128)(2,1)S(1)}, u32[]{:S(2)}, u32[]{:S(2)}) collective-permute-start(bf16[8,256,256]{2,1,0:T(8,128)(2,1)S(1)} %bitcast.26), channel_id=1, source_target_pairs={{0,64},{64,0},{1,65},{65,1},{2,66},{66,2},{3,67},{67,3},{4,68},{68... | collective-permute-start | bytes 3145736 | tf_op jit(solution)/shard_map/ppermute | solution.py:29
  11.2 0.1 collective-permute-start
  11.3 2.2 %collective-permute-done.refs_3_ = f32[1,256]{1,0:T(1,128)S(1)} collective-permute-done((f32[1,256]{1,0:T(1,128)S(1)}, f32[1,256]{1,0:T(1,128)S(1)}, u32[]{:S(2)}, u32[]{:S(2)}) %collective-permute-start) | collective-permute-done | bytes 1056 | tf_op jit(solution)/shard_map/ppermute | solution.py:29
  13.5 0.0 collective-permute-done.1.refs_5_.refs_1_
  13.5 0.6 copy-done.12
  14.1 4.3 %shard_map.114 = bf16[128,2,16,128]{3,2,1,0:T(8,128)(2,1)} custom-call(bf16[4,256,256]{2,1,0:T(8,128)(2,1)} %get-tuple-element.40.refs_0_, bf16[128,16,128]{2,1,0:T(8,128)(2,1)} %get-tuple-element.41.refs_1_, f32[1,256]{1,0:T(1,128)} %refs_2_.1, f32[1,256]{1,0:T(1,128)} %copy-done.12, bf16[8,256,256]{2,1,0:T(8,128)(2,1)} %bitcast.22, ...), custom_call_target="tpu_custom_call" | custom-call | flops 100000000 | bytes 4196352 | tf_op jit(solution)/shard_map/pallas_call | solution.py:117
  18.4 0.0 copy-start.7
  18.4 0.0 copy-start.11
  18.4 7.4 %all-to-all-start = ((bf16[128,32,128]{2,1,0:T(8,128)(2,1)}), bf16[128,32,128]{2,1,0:T(8,128)(2,1)}, u32[]{:S(2)}, u32[]{:S(2)}) async-start(bf16[128,32,128]{2,1,0:T(8,128)(2,1)} %bitcast.20), calls=%async_computation | async-start | bytes 2097152 | tf_op jit(solution)/shard_map/all_to_all | solution.py:25
  25.8 1.3 collective-permute-start.3
  27.1 1.3 collective-permute-start.4
  28.4 3.3 %collective-permute-start.6 = (f32[2,256]{1,0:T(2,128)S(1)}, f32[2,256]{1,0:T(2,128)S(1)}, u32[]{:S(2)}, u32[]{:S(2)}) collective-permute-start(f32[2,256]{1,0:T(2,128)S(1)} %pad_maximum_fusion.refs_6_), channel_id=1, source_target_pairs={{0,33},{1,32},{2,35},{3,34},{4,37},{5,36},{6,39},{7,38},{8,41},{9,... | collective-permute-start | bytes 6152 | tf_op jit(solution)/shard_map/ppermute | solution.py:477
  31.7 2.3 %collective-permute-start.7 = (f32[2,256]{1,0:T(2,128)S(1)}, f32[2,256]{1,0:T(2,128)S(1)}, u32[]{:S(2)}, u32[]{:S(2)}) collective-permute-start(f32[2,256]{1,0:T(2,128)S(1)} %pad_maximum_fusion.refs_6_), channel_id=1, source_target_pairs={{0,64},{64,0},{1,65},{65,1},{2,66},{66,2},{3,67},{67,3},{4,68},{68... | collective-permute-start | bytes 6152 | tf_op jit(solution)/shard_map/ppermute | solution.py:29
  34.0 2.7 %collective-permute-start.8 = (f32[2,256]{1,0:T(2,128)S(1)}, f32[2,256]{1,0:T(2,128)S(1)}, u32[]{:S(2)}, u32[]{:S(2)}) collective-permute-start(f32[2,256]{1,0:T(2,128)S(1)} %collective-permute-done.6.refs_7_), channel_id=1, source_target_pairs={{0,64},{64,0},{1,65},{65,1},{2,66},{66,2},{3,67},{67,3},{4,68},{68... | collective-permute-start | bytes 6152 | tf_op jit(solution)/shard_map/ppermute | solution.py:29
  36.8 0.0 collective-permute-done.7.refs_8_
  36.8 0.8 collective-permute-done.8.refs_9_
  37.6 0.0 collective-permute-done.3.refs_2_
  37.6 0.0 collective-permute-done.5.refs_5_.refs_3_
  37.6 0.8 copy-done.3
  38.4 1.0 copy-done.1
  39.4 4.4 %shard_map.115 = (bf16[512,512]{1,0:T(8,128)(2,1)}, bf16[512,512]{1,0:T(8,128)(2,1)}, bf16[4,128,512]{2,1,0:T(8,128)(2,1)}, bf16[4,512,128]{2,1,0:T(8,128)(2,1)}...) custom-call(bf16[2560,128]{1,0:T(8,128)(2,1)} %get-tuple-element.42.refs_0_, ...), custom_call_target="tpu_custom_call" | custom-call | flops 100000000 | bytes 5521408 | tf_op jit(solution)/shard_map/pallas_call | solution.py:117
  43.8 0.8 all-to-all-done
  44.6 8.1 %shard_map.116 = (bf16[128,16,128]{2,1,0:T(8,128)(2,1)}, bf16[2,256,512]{2,1,0:T(8,128)(2,1)}, bf16[2,256,512]{2,1,0:T(8,128)(2,1)}, bf16[2,256,512]{2,1,0:T(8,128)(2,1)}, bf16[2,256,512]{2,1,0:T(8,128)(2,1)}) custom-call(bf16[128,2,16,128]{3,2,1,0:T(8,128)(2,1)} %bitcast.7.refs_0_, bf16[2,256,256]{2,1,0:T(8,128)(2,1)} %get-tuple-element.43.refs_1_, ...), custom_call_target="tpu_custom_call" | custom-call | flops 100000000 | bytes 6037504 | tf_op jit(solution)/shard_map/pallas_call | solution.py:117
  52.7 9.8 %all-to-all-start.1 = ((bf16[128,16,128]{2,1,0:T(8,128)(2,1)}), bf16[128,16,128]{2,1,0:T(8,128)(2,1)}, u32[]{:S(2)}, u32[]{:S(2)}) async-start(bf16[128,16,128]{2,1,0:T(8,128)(2,1)} %get-tuple-element.50.refs_4_), calls=%async_computation.1 | async-start | bytes 1048576 | tf_op jit(solution)/shard_map/all_to_all | solution.py:25
  62.5 5.1 %collective-permute-start.9 = (bf16[2560,128]{1,0:T(8,128)(2,1)}, bf16[2560,128]{1,0:T(8,128)(2,1)}, u32[]{:S(2)}, u32[]{:S(2)}) collective-permute-start(bf16[2560,128]{1,0:T(8,128)(2,1)} %get-tuple-element.42.refs_0_), channel_id=1, source_target_pairs={{64,97},{65,96},{66,99},{67,98},{68,101},{69,100},{70,103},{71,102... | collective-permute-start | bytes 1966088 | tf_op jit(solution)/shard_map/ppermute | solution.py:477
  67.7 2.7 %shard_map.117 = (bf16[2,256,256]{2,1,0:T(8,128)(2,1)}, bf16[2,256,256]{2,1,0:T(8,128)(2,1)}, bf16[2,256,256]{2,1,0:T(8,128)(2,1)}, bf16[2,256,256]{2,1,0:T(8,128)(2,1)}, bf16[2,256,256]{2,1,0:T(8,128)(2,1)}) custom-call(bf16[8,256,256]{2,1,0:T(8,128)(2,1)} %bitcast.23, bf16[8,256,256]{2,1,0:T(8,128)(2,1)} %collective-permute-done.1.refs_5_.refs_1_, ...), custom_call_target="tpu_custom_call" | custom-call | flops 100000000 | bytes 2359296 | tf_op jit(solution)/shard_map/pallas_call | solution.py:117
  70.4 2.4 %shard_map.118.refs_2_ = bf16[128,16,128]{2,1,0:T(8,128)(2,1)} custom-call(bf16[8,256,256]{2,1,0:T(8,128)(2,1)} %bitcast.27, bf16[2,256,256]{2,1,0:T(8,128)(2,1)} %get-tuple-element.51.refs_1_), custom_call_target="tpu_custom_call" | custom-call | flops 100000000 | bytes 1048576 | tf_op jit(solution)/shard_map/pallas_call | solution.py:117
  72.9 2.2 %all-to-all-done.1.refs_0_ = bf16[128,16,128]{2,1,0:T(8,128)(2,1)} async-done(((bf16[128,16,128]{2,1,0:T(8,128)(2,1)}), bf16[128,16,128]{2,1,0:T(8,128)(2,1)}, u32[]{:S(2)}, u32[]{:S(2)}) %all-to-all-start.1) | async-done | bytes 524320 | tf_op jit(solution)/shard_map/all_to_all | solution.py:25
  75.0 4.4 %shard_map.119 = (bf16[128,2,16,128]{3,2,1,0:T(8,128)(2,1)}, bf16[2,256,512]{2,1,0:T(8,128)(2,1)}) custom-call(bf16[128,16,128]{2,1,0:T(8,128)(2,1)} %all-to-all-done.1.refs_0_, bf16[2,256,256]{2,1,0:T(8,128)(2,1)} %get-tuple-element.51.refs_1_, bf16[128,16,128]{2,1,0:T(8,128)(2,1)} %shard_map.118.refs_2_), custom_call_target="tpu_custom_call" | custom-call | flops 100000000 | bytes 2883584 | tf_op jit(solution)/shard_map/pallas_call | solution.py:117
  79.4 5.8 %all-to-all-start.2 = ((bf16[128,32,128]{2,1,0:T(8,128)(2,1)}), bf16[128,32,128]{2,1,0:T(8,128)(2,1)}, u32[]{:S(2)}, u32[]{:S(2)}) async-start(bf16[128,32,128]{2,1,0:T(8,128)(2,1)} %bitcast.28), calls=%async_computation.2 | async-start | bytes 2097152 | tf_op jit(solution)/shard_map/all_to_all | solution.py:25
  85.2 4.1 %collective-permute-start.10 = (bf16[2560,128]{1,0:T(8,128)(2,1)}, bf16[2560,128]{1,0:T(8,128)(2,1)}, u32[]{:S(2)}, u32[]{:S(2)}) collective-permute-start(bf16[2560,128]{1,0:T(8,128)(2,1)} %get-tuple-element.42.refs_0_), channel_id=1, source_target_pairs={{64,0},{65,1},{66,2},{67,3},{68,4},{69,5},{70,6},{71,7},{72,8},{73... | collective-permute-start | bytes 1966088 | tf_op jit(solution)/shard_map/ppermute | solution.py:480
  89.3 0.0 collective-permute-done.9.refs_1_
  89.3 2.1 %collective-permute-start.11 = (bf16[2560,128]{1,0:T(8,128)(2,1)}, bf16[2560,128]{1,0:T(8,128)(2,1)}, u32[]{:S(2)}, u32[]{:S(2)}) collective-permute-start(bf16[2560,128]{1,0:T(8,128)(2,1)} %collective-permute-done.9.refs_1_), channel_id=1, source_target_pairs={{64,0},{65,1},{66,2},{67,3},{68,4},{69,5},{70,6},{71,7},{72,8},{73... | collective-permute-start | bytes 1966088 | tf_op jit(solution)/shard_map/ppermute | solution.py:480
  91.4 0.0 collective-permute-done.10.refs_2_
  91.4 1.2 collective-permute-done.11.refs_3_
  92.6 4.0 %shard_map.120 = (bf16[512,512]{1,0:T(8,128)(2,1)}, bf16[512,512]{1,0:T(8,128)(2,1)}, bf16[4,128,512]{2,1,0:T(8,128)(2,1)}, bf16[4,512,128]{2,1,0:T(8,128)(2,1)}) custom-call(bf16[2560,128]{1,0:T(8,128)(2,1)} %get-tuple-element.42.refs_0_, bf16[2560,128]{1,0:T(8,128)(2,1)} %collective-permute-done.9.refs_1_, ...), custom_call_target="tpu_custom_call" | custom-call | flops 100000000 | bytes 4718592 | tf_op jit(solution)/shard_map/pallas_call | solution.py:117
  96.6 6.4 %all-to-all-done.2 = bf16[128,32,128]{2,1,0:T(8,128)(2,1)} async-done(((bf16[128,32,128]{2,1,0:T(8,128)(2,1)}), bf16[128,32,128]{2,1,0:T(8,128)(2,1)}, u32[]{:S(2)}, u32[]{:S(2)}) %all-to-all-start.2) | async-done | bytes 1048608 | tf_op jit(solution)/shard_map/all_to_all | solution.py:25
  103.0 9.0 %shard_map.121 = (bf16[128,16,128]{2,1,0:T(8,128)(2,1)}, bf16[2,256,512]{2,1,0:T(8,128)(2,1)}, bf16[2,256,512]{2,1,0:T(8,128)(2,1)}, f32[2,256,512]{2,1,0:T(8,128)}) custom-call(bf16[128,2,16,128]{3,2,1,0:T(8,128)(2,1)} %bitcast.11.refs_0_, bf16[2,256,256]{2,1,0:T(8,128)(2,1)} %get-tuple-element.53.refs_1_, bf16[2,256,512]{2,1,0:T(8,128)(2,1)} %get-tuple-element.54.refs_2_, ...), custom_call_target="tpu_custom_call" | custom-call | flops 100000000 | bytes 6819840 | tf_op jit(solution)/shard_map/pallas_call | solution.py:117
  112.0 18.8 %all_to_all.47.refs_0_ = bf16[128,16,128]{2,1,0:T(8,128)(2,1)} all-to-all(bf16[128,16,128]{2,1,0:T(8,128)(2,1)} %get-tuple-element.60.refs_2_), channel_id=1, replica_groups=mesh['segment'=2,'seq'=32,'mp'=2] {'seq','segment','mp'}, dimensions={0} | all-to-all | bytes 1048576 | tf_op jit(solution)/shard_map/all_to_all | solution.py:25
  130.7 4.0 %shard_map.122 = (bf16[128,16,128]{2,1,0:T(8,128)(2,1)}, bf16[2,256,512]{2,1,0:T(8,128)(2,1)}) custom-call(bf16[128,16,128]{2,1,0:T(8,128)(2,1)} %all_to_all.47.refs_0_, bf16[2,256,256]{2,1,0:T(8,128)(2,1)} %get-tuple-element.61.refs_1_, f32[2,512]{1,0:T(2,128)} %get-tuple-element.45.refs_3_.refs_2_), custom_call_target="tpu_custom_call" | custom-call | flops 100000000 | bytes 1839104 | tf_op jit(solution)/shard_map/pallas_call | solution.py:117
  134.8 18.5 %all_to_all.48.refs_0_ = bf16[128,16,128]{2,1,0:T(8,128)(2,1)} all-to-all(bf16[128,16,128]{2,1,0:T(8,128)(2,1)} %get-tuple-element.62.refs_2_), channel_id=1, replica_groups=mesh['segment'=2,'seq'=32,'mp'=2] {'seq','segment','mp'}, dimensions={0} | all-to-all | bytes 1048576 | tf_op jit(solution)/shard_map/all_to_all | solution.py:25
  153.3 8.7 %shard_map.123 = (bf16[128,16,128]{2,1,0:T(8,128)(2,1)}, bf16[2,256,512]{2,1,0:T(8,128)(2,1)}) custom-call(bf16[128,16,128]{2,1,0:T(8,128)(2,1)} %all_to_all.48.refs_0_, f32[2,256,512]{2,1,0:T(8,128)} %get-tuple-element.63.refs_1_.refs_7_, bf16[2,256,512]{2,1,0:T(8,128)(2,1)} %get-tuple-element.64.refs_2_, ...), custom_call_target="tpu_custom_call" | custom-call | flops 100000000 | bytes 6033408 | tf_op jit(solution)/shard_map/pallas_call | solution.py:117
  162.0 5.8 %all-to-all-start.5 = ((bf16[128,16,128]{2,1,0:T(8,128)(2,1)}), bf16[128,16,128]{2,1,0:T(8,128)(2,1)}, u32[]{:S(2)}, u32[]{:S(2)}) async-start(bf16[128,16,128]{2,1,0:T(8,128)(2,1)} %get-tuple-element.67.refs_3_), calls=%async_computation.5 | async-start | bytes 1048576 | tf_op jit(solution)/shard_map/all_to_all | solution.py:25
  167.8 1.8 shard_map.124
  169.5 3.3 %collective-permute-start.12 = (bf16[2,256,256]{2,1,0:T(8,128)(2,1)}, bf16[2,256,256]{2,1,0:T(8,128)(2,1)}, u32[]{:S(2)}, u32[]{:S(2)}) collective-permute-start(bf16[2,256,256]{2,1,0:T(8,128)(2,1)} %shard_map.124), channel_id=1, source_target_pairs={{0,1},{1,0},{2,3},{3,2},{4,5},{5,4},{6,7},{7,6},{8,9},{9,8},{10,11... | collective-permute-start | bytes 786440 | tf_op jit(solution)/shard_map/ppermute | solution.py:29
  172.9 2.4 %shard_map.125.refs_4_ = bf16[2,2,128,256]{3,2,1,0:T(8,128)(2,1)} custom-call(bf16[2,256,512]{2,1,0:T(8,128)(2,1)} %get-tuple-element.68.refs_0_, bf16[2,256,512]{2,1,0:T(8,128)(2,1)} %get-tuple-element.69.refs_1_, bf16[128,16,128]{2,1,0:T(8,128)(2,1)} %get-tuple-element.62.refs_2_), custom_call_target="tpu_custom_call" | custom-call | flops 100000000 | bytes 1310720 | tf_op jit(solution)/shard_map/pallas_call | solution.py:117
  175.2 8.9 %collective-permute-done.12.refs_2_ = bf16[2,256,256]{2,1,0:T(8,128)(2,1)} collective-permute-done((bf16[2,256,256]{2,1,0:T(8,128)(2,1)}, bf16[2,256,256]{2,1,0:T(8,128)(2,1)}, u32[]{:S(2)}, u32[]{:S(2)}) %collective-permute-start.12) | collective-permute-done | bytes 262176 | tf_op jit(solution)/shard_map/ppermute | solution.py:29
  184.1 0.0 all-to-all-done.5.refs_0_
  184.1 3.5 %shard_map.126.refs_4_ = bf16[4,2,128,256]{3,2,1,0:T(8,128)(2,1)} custom-call(bf16[128,16,128]{2,1,0:T(8,128)(2,1)} %all-to-all-done.5.refs_0_, bf16[8,256,256]{2,1,0:T(8,128)(2,1)} %bitcast.19, bf16[2,256,256]{2,1,0:T(8,128)(2,1)} %collective-permute-done.12.refs_2_, f32[2,512]{1,0:T(2,128)} %get-tuple-element.44.refs_2_.refs_9_.refs_3_, ...), custom_call_target="tpu_custom_call" | custom-call | flops 100000000 | bytes 1839104 | tf_op jit(solution)/shard_map/pallas_call | solution.py:117
  187.6 4.8 %all-to-all-start.6 = ((bf16[4,2,128,256]{3,2,1,0:T(8,128)(2,1)}), bf16[4,2,128,256]{3,2,1,0:T(8,128)(2,1)}, u32[]{:S(2)}, u32[]{:S(2)}) async-start(bf16[4,2,128,256]{3,2,1,0:T(8,128)(2,1)} %shard_map.126.refs_4_), calls=%async_computation.6 | async-start | bytes 1048576 | tf_op jit(solution)/shard_map/all_to_all | solution.py:627
  192.4 2.3 %shard_map.127.refs_2_ = bf16[2,2,128,256]{3,2,1,0:T(8,128)(2,1)} custom-call(bf16[2,256,512]{2,1,0:T(8,128)(2,1)} %get-tuple-element.72.refs_0_, bf16[2,256,512]{2,1,0:T(8,128)(2,1)} %get-tuple-element.73.refs_1_, bf16[128,16,128]{2,1,0:T(8,128)(2,1)} %get-tuple-element.60.refs_2_), custom_call_target="tpu_custom_call" | custom-call | flops 100000000 | bytes 1310720 | tf_op jit(solution)/shard_map/pallas_call | solution.py:117
  194.7 2.8 %shard_map.128 = (bf16[2,128,256]{2,1,0:T(8,128)(2,1)}, bf16[2,128,256]{2,1,0:T(8,128)(2,1)}, bf16[2,128,256]{2,1,0:T(8,128)(2,1)}, bf16[2,128,256]{2,1,0:T(8,128)(2,1)}) custom-call(bf16[2,256,512]{2,1,0:T(8,128)(2,1)} %get-tuple-element.70.refs_0_, bf16[2,256,512]{2,1,0:T(8,128)(2,1)} %get-tuple-element.71.refs_1_, ...), custom_call_target="tpu_custom_call" | custom-call | flops 100000000 | bytes 1835008 | tf_op jit(solution)/shard_map/pallas_call | solution.py:117
  197.5 0.1 collective-permute-start.13
  197.6 3.2 %collective-permute-start.14 = (bf16[2,128,256]{2,1,0:T(8,128)(2,1)}, bf16[2,128,256]{2,1,0:T(8,128)(2,1)}, u32[]{:S(2)}, u32[]{:S(2)}) collective-permute-start(bf16[2,128,256]{2,1,0:T(8,128)(2,1)} %get-tuple-element.76), channel_id=1, source_target_pairs={{0,1},{1,0},{2,3},{3,2},{4,5},{5,4},{6,7},{7,6},{8,9},{9,8},{10,11... | collective-permute-start | bytes 393224 | tf_op jit(solution)/shard_map/ppermute | solution.py:29
  200.8 0.4 collective-permute-start.15
  201.2 3.3 %collective-permute-done.14.refs_2_ = bf16[2,128,256]{2,1,0:T(8,128)(2,1)} collective-permute-done((bf16[2,128,256]{2,1,0:T(8,128)(2,1)}, bf16[2,128,256]{2,1,0:T(8,128)(2,1)}, u32[]{:S(2)}, u32[]{:S(2)}) %collective-permute-start.14) | collective-permute-done | bytes 131104 | tf_op jit(solution)/shard_map/ppermute | solution.py:29
  204.5 3.6 %collective-permute-done.15.refs_3_ = bf16[2,128,256]{2,1,0:T(8,128)(2,1)} collective-permute-done((bf16[2,128,256]{2,1,0:T(8,128)(2,1)}, bf16[2,128,256]{2,1,0:T(8,128)(2,1)}, u32[]{:S(2)}, u32[]{:S(2)}) %collective-permute-start.15) | collective-permute-done | bytes 131104 | tf_op jit(solution)/shard_map/ppermute | solution.py:618
  208.2 2.0 shard_map.129
  210.2 2.1 bitcast_convert_fusion
  (25 shorter events, 0.1 us)
Async XLA Ops:
  0.6 5.0 %copy-start = (bf16[1,8,256,256]{3,2,1,0:T(8,128)(2,1)S(1)}, bf16[1,8,256,256]{3,2,1,0:T(8,128)(2,1)}, u32[]{:S(2)}) copy-start(bf16[1,8,256,256]{3,2,1,0:T(8,128)(2,1)} %param.15) | copy-start | bytes 3145732
  0.6 12.8 %collective-permute-start.1 = (bf16[8,256,256]{2,1,0:T(8,128)(2,1)}, bf16[8,256,256]{2,1,0:T(8,128)(2,1)}, u32[]{:S(2)}, u32[]{:S(2)}) collective-permute-start(bf16[8,256,256]{2,1,0:T(8,128)(2,1)} %bitcast.21), channel_id=1, source_target_pairs={{0,64},{64,0},{1,65},{65,1},{2,66},{66,2},{3,67},{67,3},{4,68},{68... | collective-permute-start | bytes 3145736 | tf_op jit(solution)/shard_map/ppermute | solution.py:29
  4.9 6.3 %copy-start.6 = (f32[1,256]{1,0:T(1,128)S(1)}, f32[1,256]{1,0:T(1,128)}, u32[]{:S(2)}) copy-start(f32[1,256]{1,0:T(1,128)} %refs_2_.1) | copy-start | bytes 3076
  4.9 22.1 %collective-permute-start.2 = (bf16[2560,128]{1,0:T(8,128)(2,1)}, bf16[2560,128]{1,0:T(8,128)(2,1)S(1)}, u32[]{:S(2)}, u32[]{:S(2)}) collective-permute-start(bf16[2560,128]{1,0:T(8,128)(2,1)} %get-tuple-element.42.refs_0_), channel_id=1, source_target_pairs={{0,33},{1,32},{2,35},{3,34},{4,37},{5,36},{6,39},{7,38},{8,41},{9,... | collective-permute-start | bytes 1966088 | tf_op jit(solution)/shard_map/ppermute | solution.py:477
  5.7 31.9 %collective-permute-start.5 = (bf16[8,256,256]{2,1,0:T(8,128)(2,1)S(1)}, bf16[8,256,256]{2,1,0:T(8,128)(2,1)S(1)}, u32[]{:S(2)}, u32[]{:S(2)}) collective-permute-start(bf16[8,256,256]{2,1,0:T(8,128)(2,1)S(1)} %bitcast.26), channel_id=1, source_target_pairs={{0,64},{64,0},{1,65},{65,1},{2,66},{66,2},{3,67},{67,3},{4,68},{68... | collective-permute-start | bytes 3145736 | tf_op jit(solution)/shard_map/ppermute | solution.py:29
  11.2 2.3 %collective-permute-start = (f32[1,256]{1,0:T(1,128)S(1)}, f32[1,256]{1,0:T(1,128)S(1)}, u32[]{:S(2)}, u32[]{:S(2)}) collective-permute-start(f32[1,256]{1,0:T(1,128)S(1)} %copy-done.6), channel_id=1, source_target_pairs={{0,64},{64,0},{1,65},{65,1},{2,66},{66,2},{3,67},{67,3},{4,68},{68... | collective-permute-start | bytes 3080 | tf_op jit(solution)/shard_map/ppermute | solution.py:29
  13.5 0.6 copy-start.12
  18.4 10.0 %copy-start.7 = (f32[1,256]{1,0:T(1,128)S(1)}, f32[1,256]{1,0:T(1,128)}, u32[]{:S(2)}) copy-start(f32[1,256]{1,0:T(1,128)} %refs_2_.1) | copy-start | bytes 3076
  18.4 10.0 %copy-start.11 = (f32[1,256]{1,0:T(1,128)S(1)}, f32[1,256]{1,0:T(1,128)}, u32[]{:S(2)}) copy-start(f32[1,256]{1,0:T(1,128)} %param.12) | copy-start | bytes 3076
  18.4 26.2 %all-to-all-start = ((bf16[128,32,128]{2,1,0:T(8,128)(2,1)}), bf16[128,32,128]{2,1,0:T(8,128)(2,1)}, u32[]{:S(2)}, u32[]{:S(2)}) async-start(bf16[128,32,128]{2,1,0:T(8,128)(2,1)} %bitcast.20), calls=%async_computation | async-start | bytes 2097152 | tf_op jit(solution)/shard_map/all_to_all | solution.py:25
  25.8 11.8 %collective-permute-start.3 = (bf16[2560,128]{1,0:T(8,128)(2,1)}, bf16[2560,128]{1,0:T(8,128)(2,1)S(1)}, u32[]{:S(2)}, u32[]{:S(2)}) collective-permute-start(bf16[2560,128]{1,0:T(8,128)(2,1)} %get-tuple-element.42.refs_0_), channel_id=1, source_target_pairs={{0,64},{1,65},{2,66},{3,67},{4,68},{5,69},{6,70},{7,71},{8,72},{9,... | collective-permute-start | bytes 1966088 | tf_op jit(solution)/shard_map/ppermute | solution.py:480
  27.1 10.5 %copy-start.2 = (bf16[2560,128]{1,0:T(8,128)(2,1)}, bf16[2560,128]{1,0:T(8,128)(2,1)S(1)}, u32[]{:S(2)}) copy-start(bf16[2560,128]{1,0:T(8,128)(2,1)S(1)} %collective-permute-done.2.refs_1_) | copy-start | bytes 1966084
  27.1 12.3 %collective-permute-start.4 = (bf16[2560,128]{1,0:T(8,128)(2,1)S(1)}, bf16[2560,128]{1,0:T(8,128)(2,1)}, u32[]{:S(2)}, u32[]{:S(2)}) collective-permute-start(bf16[2560,128]{1,0:T(8,128)(2,1)S(1)} %collective-permute-done.2.refs_1_), channel_id=1, source_target_pairs={{0,64},{1,65},{2,66},{3,67},{4,68},{5,69},{6,70},{7,71},{8,72},{9,... | collective-permute-start | bytes 1966088 | tf_op jit(solution)/shard_map/ppermute | solution.py:480
  28.4 11.0 %copy-start.5 = (f32[2,256]{1,0:T(2,128)}, f32[2,256]{1,0:T(2,128)S(1)}, u32[]{:S(2)}) copy-start(f32[2,256]{1,0:T(2,128)S(1)} %pad_maximum_fusion.refs_6_) | copy-start | bytes 6148
  28.4 5.6 %collective-permute-start.6 = (f32[2,256]{1,0:T(2,128)S(1)}, f32[2,256]{1,0:T(2,128)S(1)}, u32[]{:S(2)}, u32[]{:S(2)}) collective-permute-start(f32[2,256]{1,0:T(2,128)S(1)} %pad_maximum_fusion.refs_6_), channel_id=1, source_target_pairs={{0,33},{1,32},{2,35},{3,34},{4,37},{5,36},{6,39},{7,38},{8,41},{9,... | collective-permute-start | bytes 6152 | tf_op jit(solution)/shard_map/ppermute | solution.py:477
  31.7 5.0 %collective-permute-start.7 = (f32[2,256]{1,0:T(2,128)S(1)}, f32[2,256]{1,0:T(2,128)S(1)}, u32[]{:S(2)}, u32[]{:S(2)}) collective-permute-start(f32[2,256]{1,0:T(2,128)S(1)} %pad_maximum_fusion.refs_6_), channel_id=1, source_target_pairs={{0,64},{64,0},{1,65},{65,1},{2,66},{66,2},{3,67},{67,3},{4,68},{68... | collective-permute-start | bytes 6152 | tf_op jit(solution)/shard_map/ppermute | solution.py:29
  34.0 5.4 %copy-start.8 = (f32[2,256]{1,0:T(2,128)}, f32[2,256]{1,0:T(2,128)S(1)}, u32[]{:S(2)}) copy-start(f32[2,256]{1,0:T(2,128)S(1)} %collective-permute-done.6.refs_7_) | copy-start | bytes 6148
  34.0 3.6 %collective-permute-start.8 = (f32[2,256]{1,0:T(2,128)S(1)}, f32[2,256]{1,0:T(2,128)S(1)}, u32[]{:S(2)}, u32[]{:S(2)}) collective-permute-start(f32[2,256]{1,0:T(2,128)S(1)} %collective-permute-done.6.refs_7_), channel_id=1, source_target_pairs={{0,64},{64,0},{1,65},{65,1},{2,66},{66,2},{3,67},{67,3},{4,68},{68... | collective-permute-start | bytes 6152 | tf_op jit(solution)/shard_map/ppermute | solution.py:29
  36.8 2.7 %copy-start.9 = (f32[2,256]{1,0:T(2,128)}, f32[2,256]{1,0:T(2,128)S(1)}, u32[]{:S(2)}) copy-start(f32[2,256]{1,0:T(2,128)S(1)} %collective-permute-done.7.refs_8_) | copy-start | bytes 6148
  37.6 1.9 copy-start.10
  37.6 0.9 copy-start.3
  38.4 1.0 copy-start.1
  52.7 22.3 %all-to-all-start.1 = ((bf16[128,16,128]{2,1,0:T(8,128)(2,1)}), bf16[128,16,128]{2,1,0:T(8,128)(2,1)}, u32[]{:S(2)}, u32[]{:S(2)}) async-start(bf16[128,16,128]{2,1,0:T(8,128)(2,1)} %get-tuple-element.50.refs_4_), calls=%async_computation.1 | async-start | bytes 1048576 | tf_op jit(solution)/shard_map/all_to_all | solution.py:25
  62.5 26.7 %collective-permute-start.9 = (bf16[2560,128]{1,0:T(8,128)(2,1)}, bf16[2560,128]{1,0:T(8,128)(2,1)}, u32[]{:S(2)}, u32[]{:S(2)}) collective-permute-start(bf16[2560,128]{1,0:T(8,128)(2,1)} %get-tuple-element.42.refs_0_), channel_id=1, source_target_pairs={{64,97},{65,96},{66,99},{67,98},{68,101},{69,100},{70,103},{71,102... | collective-permute-start | bytes 1966088 | tf_op jit(solution)/shard_map/ppermute | solution.py:477
  79.4 23.6 %all-to-all-start.2 = ((bf16[128,32,128]{2,1,0:T(8,128)(2,1)}), bf16[128,32,128]{2,1,0:T(8,128)(2,1)}, u32[]{:S(2)}, u32[]{:S(2)}) async-start(bf16[128,32,128]{2,1,0:T(8,128)(2,1)} %bitcast.28), calls=%async_computation.2 | async-start | bytes 2097152 | tf_op jit(solution)/shard_map/all_to_all | solution.py:25
  85.2 6.2 %collective-permute-start.10 = (bf16[2560,128]{1,0:T(8,128)(2,1)}, bf16[2560,128]{1,0:T(8,128)(2,1)}, u32[]{:S(2)}, u32[]{:S(2)}) collective-permute-start(bf16[2560,128]{1,0:T(8,128)(2,1)} %get-tuple-element.42.refs_0_), channel_id=1, source_target_pairs={{64,0},{65,1},{66,2},{67,3},{68,4},{69,5},{70,6},{71,7},{72,8},{73... | collective-permute-start | bytes 1966088 | tf_op jit(solution)/shard_map/ppermute | solution.py:480
  89.3 3.3 %collective-permute-start.11 = (bf16[2560,128]{1,0:T(8,128)(2,1)}, bf16[2560,128]{1,0:T(8,128)(2,1)}, u32[]{:S(2)}, u32[]{:S(2)}) collective-permute-start(bf16[2560,128]{1,0:T(8,128)(2,1)} %collective-permute-done.9.refs_1_), channel_id=1, source_target_pairs={{64,0},{65,1},{66,2},{67,3},{68,4},{69,5},{70,6},{71,7},{72,8},{73... | collective-permute-start | bytes 1966088 | tf_op jit(solution)/shard_map/ppermute | solution.py:480
  162.0 22.1 %all-to-all-start.5 = ((bf16[128,16,128]{2,1,0:T(8,128)(2,1)}), bf16[128,16,128]{2,1,0:T(8,128)(2,1)}, u32[]{:S(2)}, u32[]{:S(2)}) async-start(bf16[128,16,128]{2,1,0:T(8,128)(2,1)} %get-tuple-element.67.refs_3_), calls=%async_computation.5 | async-start | bytes 1048576 | tf_op jit(solution)/shard_map/all_to_all | solution.py:25
  169.5 14.6 %collective-permute-start.12 = (bf16[2,256,256]{2,1,0:T(8,128)(2,1)}, bf16[2,256,256]{2,1,0:T(8,128)(2,1)}, u32[]{:S(2)}, u32[]{:S(2)}) collective-permute-start(bf16[2,256,256]{2,1,0:T(8,128)(2,1)} %shard_map.124), channel_id=1, source_target_pairs={{0,1},{1,0},{2,3},{3,2},{4,5},{5,4},{6,7},{7,6},{8,9},{9,8},{10,11... | collective-permute-start | bytes 786440 | tf_op jit(solution)/shard_map/ppermute | solution.py:29
  187.6 22.6 %all-to-all-start.6 = ((bf16[4,2,128,256]{3,2,1,0:T(8,128)(2,1)}), bf16[4,2,128,256]{3,2,1,0:T(8,128)(2,1)}, u32[]{:S(2)}, u32[]{:S(2)}) async-start(bf16[4,2,128,256]{3,2,1,0:T(8,128)(2,1)} %shard_map.126.refs_4_), calls=%async_computation.6 | async-start | bytes 1048576 | tf_op jit(solution)/shard_map/all_to_all | solution.py:627
  197.5 3.7 %collective-permute-start.13 = (bf16[2,128,256]{2,1,0:T(8,128)(2,1)}, bf16[2,128,256]{2,1,0:T(8,128)(2,1)S(1)}, u32[]{:S(2)}, u32[]{:S(2)}) collective-permute-start(bf16[2,128,256]{2,1,0:T(8,128)(2,1)} %get-tuple-element.75), channel_id=1, source_target_pairs={{0,64},{64,0},{1,65},{65,1},{2,66},{66,2},{3,67},{67,3},{4,68},{68... | collective-permute-start | bytes 393224 | tf_op jit(solution)/shard_map/ppermute | solution.py:29
  197.6 6.9 %collective-permute-start.14 = (bf16[2,128,256]{2,1,0:T(8,128)(2,1)}, bf16[2,128,256]{2,1,0:T(8,128)(2,1)}, u32[]{:S(2)}, u32[]{:S(2)}) collective-permute-start(bf16[2,128,256]{2,1,0:T(8,128)(2,1)} %get-tuple-element.76), channel_id=1, source_target_pairs={{0,1},{1,0},{2,3},{3,2},{4,5},{5,4},{6,7},{7,6},{8,9},{9,8},{10,11... | collective-permute-start | bytes 393224 | tf_op jit(solution)/shard_map/ppermute | solution.py:29
  200.8 7.3 %collective-permute-start.15 = (bf16[2,128,256]{2,1,0:T(8,128)(2,1)}, bf16[2,128,256]{2,1,0:T(8,128)(2,1)}, u32[]{:S(2)}, u32[]{:S(2)}) collective-permute-start(bf16[2,128,256]{2,1,0:T(8,128)(2,1)} %get-tuple-element.77), channel_id=1, source_target_pairs={{0,65},{1,64},{64,1},{65,0},{2,67},{3,66},{66,3},{67,2},{4,69},{5,... | collective-permute-start | bytes 393224 | tf_op jit(solution)/shard_map/ppermute | solution.py:618
  201.2 6.9 %copy-start.4 = (bf16[2,128,256]{2,1,0:T(8,128)(2,1)}, bf16[2,128,256]{2,1,0:T(8,128)(2,1)S(1)}, u32[]{:S(2)}) copy-start(bf16[2,128,256]{2,1,0:T(8,128)(2,1)S(1)} %collective-permute-done.13.refs_1_) | copy-start | bytes 393220

commit v3 on v2

--- a/solution.py
+++ b/solution.py
@@ -14,10 +14,9 @@
 F32 = jnp.float32
 MSG = (2048, 128)
 OWNERS = 128
-TILES = (OWNERS, 16, 128)
-PAIR = (OWNERS, 2, 16, 128)
+PAIR = (4096, 128)
 VMEM_BYTES = 67043328
-SPARE = 2**17
+SPARE = 16 * 2**20
 WEIGHT_ROWS = 2560
 
 
@@ -116,7 +115,9 @@
     near, far = pl.BlockSpec(memory_space=pltpu.VMEM), pl.BlockSpec(memory_space=pltpu.HBM)
     return pl.pallas_call(
         kernel,
-        out_shape=tuple(jax.ShapeDtypeStruct(*o) for o in outs),
+        out_shape=tuple(
+            jax.ShapeDtypeStruct(*o) if n else pltpu.HBM(*o) for n, o in zip(near_out, outs)
+        ),
         in_specs=[near if n else far for n in near_in]
         + [pl.BlockSpec(memory_space=pl.ANY)] * len(after),
         out_specs=tuple(near if n else far for n in near_out),
@@ -126,7 +127,10 @@
         + [pltpu.VMEM(s, d) for s, d in scratch],
         compiler_params=pltpu.CompilerParams(vmem_limit_bytes=VMEM_BYTES - held - SPARE),
         cost_estimate=pl.CostEstimate(flops=10**8, bytes_accessed=moved, transcendentals=0),
-    )(*[a[0] for a in args], *after)
+    )(
+        *[a[0] if n else pltpu.with_memory_space_constraint(a[0], pltpu.HBM) for n, a in zip(near_in, args)],
+        *after,
+    )
 
 
 def core():
@@ -138,11 +142,22 @@
 
 
 def widen(msg, wide):
-    wide[...] = msg.reshape(MSG).astype(F32)
+    wide[...] = msg[...].astype(F32)
 
 
 def narrow(packed):
-    return packed[...].reshape(TILES).astype(BF)
+    return packed[...].astype(BF)
+
+
+def joined(packed, tiles):
+    parts = [values.reshape(OWNERS, 16, 128) for values in (packed[...], tiles[...].astype(F32))]
+    return jnp.concatenate(parts, axis=1).reshape(PAIR).astype(BF)
+
+
+def parted(msg, wide, wide_more):
+    both = msg[...].astype(F32).reshape(OWNERS, 32, 128)
+    wide[...] = both[:, :16].reshape(MSG)
+    wide_more[...] = both[:, 16:].reshape(MSG)
 
 
 def pack_quarter(values, a, out, temp):
@@ -240,8 +255,7 @@
         factor = jnp.where(g == 0, mine_ref[a], got_ref[4 * g + a])
         scaled = (x_ref[a].astype(F32) * key).astype(BF)
         pack_quarter(dot(factor, scaled), a, packed, temp)
-    outs[0][:, 1] = x_tiles[...]
-    outs[0][:, 0] = narrow(packed)
+    outs[0][...] = joined(packed, x_tiles)
 
 
 def weights_body(layer, ins, outs):
@@ -303,8 +317,7 @@
 def forward_cols_body(ins, outs, wide, wide_x, packed):
     msg, factor, gains0, gains1, u, up2, down1, v = ins
     out_msg, mixed_out, x_out, hidden_out, middle_out = outs
-    widen(msg[:, 0], wide)
-    widen(msg[:, 1], wide_x)
+    parted(msg, wide, wide_x)
     for oo in range(2):
         mixed = unpack_quarter(wide, oo).astype(BF)
         x = unpack_quarter(wide_x, oo)
@@ -330,20 +343,19 @@
 
 def rows_body(ins, outs, wide, packed, temp, temp4):
     msg, factor, more = ins
-    widen(msg[...], wide)
+    widen(msg, wide)
     for a2 in range(2):
         values = unpack_rows(wide, a2, temp4).astype(BF)
         outs[1].ref[a2] = values
         outs[1].send(a2)
         result = dot(factor[a2], values)
-        if len(outs[0].shape) == 3:
+        if outs[0].shape == MSG:
             result = result * more[1:2, :]
         pack_rows(result, a2, packed, temp)
-    if len(outs[0].shape) == 3:
+    if outs[0].shape == MSG:
         outs[0][...] = narrow(packed)
     else:
-        outs[0][:, 1] = more[...]
-        outs[0][:, 0] = narrow(packed)
+        outs[0][...] = joined(packed, more)
 
 
 def grad_body(ins, outs):
@@ -370,7 +382,7 @@
 def last_rows_body(ins, outs, wide, temp4):
     msg, x_own, x_peer, gains, upper = ins
     m = side()
-    widen(msg[...], wide)
+    widen(msg, wide)
     for a2 in range(2):
         values = unpack_rows(wide, a2, temp4).astype(BF)
         own, peer = x_own[a2].astype(F32), x_peer[a2].astype(F32)
@@ -408,8 +420,7 @@
 def upper_cols_body(ins, outs, wide, wide_c, packed, temp4):
     msg, factor, x_ref, gains, v, u, up2, down1, factor_t = ins
     out_msg, mixed_out, back_turned_out, direct_out = outs
-    widen(msg[:, 0], wide)
-    widen(msg[:, 1], wide_c)
+    parted(msg, wide, wide_c)
     for oo in range(2):
         mixed = unpack_cols(wide, oo).astype(BF)
         cot = unpack_quarter_rows(wide_c, oo, temp4).astype(BF)
@@ -426,10 +437,10 @@
         back_turned = (back_hidden * gated).astype(BF)
         back_turned_out.ref[oo] = back_turned
         back_turned_out.send(oo)
-        pack_cols(dot(factor_t[oo], back_turned), oo, packed)
         gate_slope = logistic * (1.0 + pre * (1.0 - logistic))
         direct_out.ref[oo] = back_hidden + back_hidden * turned * gate_slope * gate
         direct_out.send(oo)
+        pack_cols(dot(factor_t[oo], back_turned), oo, packed)
     out_msg[...] = narrow(packed)
 
 
@@ -437,7 +448,7 @@
     msg, direct0, hidden_ref, v, u, up2, down1, direct1, x_ref, gains, factor_t = ins
     direct = direct0, direct1
     out_msg, back_turned_out = outs
-    widen(msg[...], wide)
+    widen(msg, wide)
     for oo in range(2):
         passed = (direct[oo][...] + unpack_cols(wide, oo)).astype(BF)
         back_hidden = ffn_back(passed, hidden_ref[oo], u, v, up2, down1)
@@ -494,7 +505,7 @@
     def part(array, n):
         return array, lambda ref: ref.at[n], array.shape[1:]
 
-    tiles = Near((TILES, BF))
+    tiles = Near((MSG, BF))
     scratch_pack = [(MSG, F32), ((256, 128), F32)]
 
     key_got = swap(key_gain, "segment")
@@ -514,8 +525,7 @@
     )
 
     def send(message, order=ROWS_ORDER):
-        shape = message.shape
-        return exchange(message.reshape(-1, 128), order).reshape(shape)
+        return exchange(message, order)
 
     msg = send(rows_msg, QUARTER_ORDER)
 
@@ -540,15 +550,6 @@
         ),
     )
 
-    (x_sent,) = call(
-        slice_body,
-        [((2, 256, 256), BF)],
-        [],
-        ((rows, lambda ref: ref.at[pl.ds(2 * (2 * core() + 1 - side()), 2)], (2, 256, 256)),),
-        after=(u0,),
-    )
-    x_peer = swap(x_sent, "mp")
-
     block = ((2, 256, 512), BF)
     next_msg, mixed0, x0, hidden0, middle = call(
         forward_cols_body,
@@ -581,7 +582,7 @@
         upper_cols_body,
         [tiles, block, block, ((2, 256, 512), F32)],
         [(MSG, F32)] * 3 + [((4, 256, 128), F32)],
-        (Near(msg), *(Near(a) for a in (second1, middle, gains1, v1, u1, up1, down1, second1_t))),
+        (Near(msg), second1, middle, gains1, v1, u1, up1, down1, second1_t),
     )
     msg = send(next_msg)
 
@@ -598,6 +599,15 @@
     )
     msg = send(next_msg)
     first_grad1 = channel_grad(back_rows1, scaled1, next_msg)
+
+    (x_sent,) = call(
+        slice_body,
+        [((2, 256, 256), BF)],
+        [],
+        ((rows, lambda ref: ref.at[pl.ds(2 * (2 * core() + 1 - side()), 2)], (2, 256, 256)),),
+        after=(first_grad1,),
+    )
+    x_peer = swap(x_sent, "mp")
 
     next_msg, back_turned0 = call(
         lower_cols_body,

time: 214 us -> 201 us (0.939)
  Pallas kernels: 69.5 us -> 57.4 us
  starting transfers between devices: 70.6 us -> 63.6 us
  local copies, waits for them, and re-layouts: 2.44 us -> 6.97 us
  waiting for transfers between devices: 29.5 us -> 34 us
    pallas_call x17, Pallas kernels: 69.5 us -> 57.4 us  [call(): pl.pallas_call(kernel, out_shape=tuple((jax.ShapeDtypeStruct(*o) if n els...]
    unnamed x26 -> x44, local copies, waits for them, and re-layouts: 2.44 us -> 6.97 us
    all_to_all x4, waiting for transfers between devices: 9.41 us -> 13 us  [exchange(): lax.all_to_all(message, order, split_axis=0, concat_axis=0, tiled=True)]
    ppermute x8, starting transfers between devices: 18.8 us -> 15.7 us  [swap(): return lax.ppermute(value, axis, [(0, 1), (1, 0)])]
    all_to_all x4, starting transfers between devices: 28.7 us -> 26.4 us  [exchange(): lax.all_to_all(message, order, split_axis=0, concat_axis=0, tiled=True)]
  transfers between devices with their start and end apart: 21 -> 21, of which waited for: 9 -> 11; matrix products, arithmetic and copies ran while one was open for 0% -> 0% of each run, Pallas kernels for 17% -> 15%
where the time goes in v3:
time: 201 us; the launch traced here: 200 us
  starting transfers between devices  63.6 us (32%)
  Pallas kernels  57.4 us (29%)
  blocking collectives  36.1 us (18%)
  waiting for transfers between devices  34 us (17%)
  local copies, waits for them, and re-layouts  6.97 us (3%)
    pallas_call x17, Pallas kernels, call(): pl.pallas_call(kernel, out_shape=tuple((jax.ShapeDtypeStruct(*o) if n els...  57.4 us
    all_to_all x2, blocking collectives, exchange(): lax.all_to_all(message, order, split_axis=0, concat_axis=0, tiled=True)  36.1 us
    all_to_all x4, starting transfers between devices, exchange(): lax.all_to_all(message, order, split_axis=0, concat_axis=0, tiled=True)  26.4 us
    ppermute x8, waiting for transfers between devices, swap(): return lax.ppermute(value, axis, [(0, 1), (1, 0)])  16.1 us
    ppermute x8, starting transfers between devices, swap(): return lax.ppermute(value, axis, [(0, 1), (1, 0)])  15.7 us
    all_to_all x4, waiting for transfers between devices, exchange(): lax.all_to_all(message, order, split_axis=0, concat_axis=0, tiled=True)  13 us
    ppermute x3, starting transfers between devices, swap_z(): return lax.ppermute(value, ('segment', 'seq', 'mp'), pairs)  9.96 us
    unnamed x44, local copies, waits for them, and re-layouts  6.97 us
  transfers between devices with their start and end apart: 21, of which 11 were waited for; matrix products, arithmetic and copies ran while one was open for 0% of the time, Pallas kernels for 15%

profile of v3, /device:TPU:1, one launch (start us, length us, event | category | flops | bytes accessed | tf_op | source)
XLA Modules:
  0.0 200.2 jit_solution(2770423773918398629)
XLA Ops:
  0.6 0.0 copy-start
  0.6 1.5 collective-permute-start.1
  2.1 2.2 %shard_map.113 = (bf16[2560,128]{1,0:T(8,128)(2,1)}, bf16[4,256,256]{2,1,0:T(8,128)(2,1)S(1)}, bf16[2048,128]{1,0:T(8,128)(2,1)S(1)}) custom-call(bf16[8,256,256]{2,1,0:T(8,128)(2,1)} %bitcast.36, bf16[2,128,128]{2,1,0:T(8,128)(2,1)} %bitcast.47, bf16[2,128,128]{2,1,0:T(8,128)(2,1)} %bitcast.48, bf16[2,512,128]{2,1,0:T(8,128)(2,1)} %bitcast.45, ...), custom_call_target="tpu_custom_call" | custom-call | flops 100000000 | bytes 2883584 | tf_op jit(solution)/shard_map/pallas_call | solution.py:116
  4.3 0.0 copy-start.15
  4.4 1.5 collective-permute-start.2
  5.9 4.7 %collective-permute-start.5 = (bf16[8,256,256]{2,1,0:T(8,128)(2,1)}, bf16[8,256,256]{2,1,0:T(8,128)(2,1)}, u32[]{:S(2)}, u32[]{:S(2)}) collective-permute-start(bf16[8,256,256]{2,1,0:T(8,128)(2,1)} %bitcast.39), channel_id=1, source_target_pairs={{0,64},{64,0},{1,65},{65,1},{2,66},{66,2},{3,67},{67,3},{4,68},{68... | collective-permute-start | bytes 3145736 | tf_op jit(solution)/shard_map/ppermute | solution.py:28
  10.6 0.1 collective-permute-start
  10.7 2.5 %collective-permute-done.refs_3_ = f32[1,256]{1,0:T(1,128)S(1)} collective-permute-done((f32[1,256]{1,0:T(1,128)S(1)}, f32[1,256]{1,0:T(1,128)S(1)}, u32[]{:S(2)}, u32[]{:S(2)}) %collective-permute-start) | collective-permute-done | bytes 1056 | tf_op jit(solution)/shard_map/ppermute | solution.py:28
  13.2 0.6 copy-done.21
  13.8 2.5 %shard_map.114 = bf16[4096,128]{1,0:T(8,128)(2,1)} custom-call(bf16[4,256,256]{2,1,0:T(8,128)(2,1)S(1)} %get-tuple-element.40.refs_0_, bf16[2048,128]{1,0:T(8,128)(2,1)S(1)} %get-tuple-element.41.refs_1_, f32[1,256]{1,0:T(1,128)} %refs_2_.1, f32[1,256]{1,0:T(1,128)} %copy-done.21, bf16[8,256,256]{2,1,0:T(8,128)(2,1)S(1)} %bitcast.29, ...), custom_call_target="tpu_custom_call" | custom-call | flops 100000000 | bytes 4196352 | tf_op jit(solution)/shard_map/pallas_call | solution.py:116
  16.3 6.9 %all-to-all-start = ((bf16[128,32,128]{2,1,0:T(8,128)(2,1)}), bf16[128,32,128]{2,1,0:T(8,128)(2,1)S(1)}, u32[]{:S(2)}, u32[]{:S(2)}) async-start(bf16[128,32,128]{2,1,0:T(8,128)(2,1)} %bitcast.6), calls=%async_computation | async-start | bytes 2097152 | tf_op jit(solution)/shard_map/all_to_all | solution.py:24
  23.2 1.3 collective-permute-start.3
  24.5 1.3 collective-permute-start.4
  25.9 3.3 %collective-permute-start.6 = (f32[2,256]{1,0:T(2,128)S(1)}, f32[2,256]{1,0:T(2,128)S(1)}, u32[]{:S(2)}, u32[]{:S(2)}) collective-permute-start(f32[2,256]{1,0:T(2,128)S(1)} %pad_maximum_fusion.refs_6_), channel_id=1, source_target_pairs={{0,33},{1,32},{2,35},{3,34},{4,37},{5,36},{6,39},{7,38},{8,41},{9,... | collective-permute-start | bytes 6152 | tf_op jit(solution)/shard_map/ppermute | solution.py:488
  29.2 1.5 collective-permute-start.7
  30.7 0.2 collective-permute-done.6.refs_7_
  30.9 1.3 collective-permute-start.8
  32.2 0.8 collective-permute-done.8.refs_9_
  33.1 0.5 copy-done.19
  33.6 0.3 copy-done.6
  33.9 0.8 copy-done.7
  34.7 4.3 %shard_map.115 = (bf16[512,512]{1,0:T(8,128)(2,1)}, bf16[512,512]{1,0:T(8,128)(2,1)}, bf16[4,128,512]{2,1,0:T(8,128)(2,1)}, bf16[4,512,128]{2,1,0:T(8,128)(2,1)}...) custom-call(bf16[2560,128]{1,0:T(8,128)(2,1)} %get-tuple-element.42.refs_0_, ...), custom_call_target="tpu_custom_call" | custom-call | flops 100000000 | bytes 5521408 | tf_op jit(solution)/shard_map/pallas_call | solution.py:116
  39.0 3.4 %all-to-all-done = bf16[128,32,128]{2,1,0:T(8,128)(2,1)S(1)} async-done(((bf16[128,32,128]{2,1,0:T(8,128)(2,1)}), bf16[128,32,128]{2,1,0:T(8,128)(2,1)S(1)}, u32[]{:S(2)}, u32[]{:S(2)}) %all-to-all-start) | async-done | bytes 1048608 | tf_op jit(solution)/shard_map/all_to_all | solution.py:24
  42.4 6.8 %shard_map.116 = (bf16[2048,128]{1,0:T(8,128)(2,1)}, bf16[2,256,512]{2,1,0:T(8,128)(2,1)}, bf16[2,256,512]{2,1,0:T(8,128)(2,1)}, bf16[2,256,512]{2,1,0:T(8,128)(2,1)}, bf16[2,256,512]{2,1,0:T(8,128)(2,1)}) custom-call(bf16[4096,128]{1,0:T(8,128)(2,1)S(1)} %bitcast.26, bf16[2,256,256]{2,1,0:T(8,128)(2,1)} %get-tuple-element.43.refs_1_, ...), custom_call_target="tpu_custom_call" | custom-call | flops 100000000 | bytes 6037504 | tf_op jit(solution)/shard_map/pallas_call | solution.py:116
  49.3 8.9 %all-to-all-start.1 = ((bf16[128,16,128]{2,1,0:T(8,128)(2,1)}), bf16[128,16,128]{2,1,0:T(8,128)(2,1)S(1)}, u32[]{:S(2)}, u32[]{:S(2)}) async-start(bf16[128,16,128]{2,1,0:T(8,128)(2,1)} %bitcast.9), calls=%async_computation.1 | async-start | bytes 1048576 | tf_op jit(solution)/shard_map/all_to_all | solution.py:24
  58.2 5.1 %collective-permute-start.9 = (bf16[2560,128]{1,0:T(8,128)(2,1)}, bf16[2560,128]{1,0:T(8,128)(2,1)S(1)}, u32[]{:S(2)}, u32[]{:S(2)}) collective-permute-start(bf16[2560,128]{1,0:T(8,128)(2,1)} %get-tuple-element.42.refs_0_), channel_id=1, source_target_pairs={{64,97},{65,96},{66,99},{67,98},{68,101},{69,100},{70,103},{71,102... | collective-permute-start | bytes 1966088 | tf_op jit(solution)/shard_map/ppermute | solution.py:488
  63.4 2.7 %shard_map.117 = (bf16[2,256,256]{2,1,0:T(8,128)(2,1)}, bf16[2,256,256]{2,1,0:T(8,128)(2,1)}, bf16[2,256,256]{2,1,0:T(8,128)(2,1)}, bf16[2,256,256]{2,1,0:T(8,128)(2,1)}, bf16[2,256,256]{2,1,0:T(8,128)(2,1)}) custom-call(bf16[8,256,256]{2,1,0:T(8,128)(2,1)} %bitcast.28, bf16[8,256,256]{2,1,0:T(8,128)(2,1)} %copy-done.1, bf16[8,256,256]{2,1,0:T(8,128)(2,1)} %bitcast.41, ...), custom_call_target="tpu_custom_call" | custom-call | flops 100000000 | bytes 2359296 | tf_op jit(solution)/shard_map/pallas_call | solution.py:116
  66.1 0.9 copy-done.3
  67.0 1.6 shard_map.118.refs_2_
  68.7 2.4 %all-to-all-done.1 = bf16[128,16,128]{2,1,0:T(8,128)(2,1)S(1)} async-done(((bf16[128,16,128]{2,1,0:T(8,128)(2,1)}), bf16[128,16,128]{2,1,0:T(8,128)(2,1)S(1)}, u32[]{:S(2)}, u32[]{:S(2)}) %all-to-all-start.1) | async-done | bytes 524320 | tf_op jit(solution)/shard_map/all_to_all | solution.py:24
  71.1 3.2 %shard_map.119 = (bf16[4096,128]{1,0:T(8,128)(2,1)}, bf16[2,256,512]{2,1,0:T(8,128)(2,1)}) custom-call(bf16[2048,128]{1,0:T(8,128)(2,1)S(1)} %bitcast.34, bf16[2,256,256]{2,1,0:T(8,128)(2,1)} %get-tuple-element.51.refs_1_, bf16[2048,128]{1,0:T(8,128)(2,1)S(1)} %shard_map.118.refs_2_), custom_call_target="tpu_custom_call" | custom-call | flops 100000000 | bytes 2883584 | tf_op jit(solution)/shard_map/pallas_call | solution.py:116
  74.3 5.3 %all-to-all-start.2 = ((bf16[128,32,128]{2,1,0:T(8,128)(2,1)}), bf16[128,32,128]{2,1,0:T(8,128)(2,1)S(1)}, u32[]{:S(2)}, u32[]{:S(2)}) async-start(bf16[128,32,128]{2,1,0:T(8,128)(2,1)} %bitcast.12), calls=%async_computation.2 | async-start | bytes 2097152 | tf_op jit(solution)/shard_map/all_to_all | solution.py:24
  79.6 3.0 %collective-permute-start.10 = (bf16[2560,128]{1,0:T(8,128)(2,1)}, bf16[2560,128]{1,0:T(8,128)(2,1)S(1)}, u32[]{:S(2)}, u32[]{:S(2)}) collective-permute-start(bf16[2560,128]{1,0:T(8,128)(2,1)} %get-tuple-element.42.refs_0_), channel_id=1, source_target_pairs={{64,0},{65,1},{66,2},{67,3},{68,4},{69,5},{70,6},{71,7},{72,8},{73... | collective-permute-start | bytes 1966088 | tf_op jit(solution)/shard_map/ppermute | solution.py:491
  82.6 1.3 collective-permute-start.11
  84.0 0.5 collective-permute-done.10.refs_2_
  84.5 1.1 collective-permute-done.11.refs_3_
  85.6 0.8 copy-done.9
  86.5 4.0 %shard_map.120 = (bf16[512,512]{1,0:T(8,128)(2,1)}, bf16[512,512]{1,0:T(8,128)(2,1)}, bf16[4,128,512]{2,1,0:T(8,128)(2,1)}, bf16[4,512,128]{2,1,0:T(8,128)(2,1)}) custom-call(bf16[2560,128]{1,0:T(8,128)(2,1)} %get-tuple-element.42.refs_0_, bf16[2560,128]{1,0:T(8,128)(2,1)} %copy-done.5, bf16[2560,128]{1,0:T(8,128)(2,1)} %copy-done.8, bf16[2560,128]{1,0:T(8,128)(2,1)} %copy-done.9), custom_call_target="tpu_custom_call" | custom-call | flops 100000000 | bytes 4718592 | tf_op jit(solution)/shard_map/pallas_call | solution.py:116
  90.5 7.2 %all-to-all-done.2 = bf16[128,32,128]{2,1,0:T(8,128)(2,1)S(1)} async-done(((bf16[128,32,128]{2,1,0:T(8,128)(2,1)}), bf16[128,32,128]{2,1,0:T(8,128)(2,1)S(1)}, u32[]{:S(2)}, u32[]{:S(2)}) %all-to-all-start.2) | async-done | bytes 1048608 | tf_op jit(solution)/shard_map/all_to_all | solution.py:24
  97.7 7.4 %shard_map.121 = (bf16[2048,128]{1,0:T(8,128)(2,1)S(1)}, bf16[2,256,512]{2,1,0:T(8,128)(2,1)}, bf16[2,256,512]{2,1,0:T(8,128)(2,1)}, f32[2,256,512]{2,1,0:T(8,128)}) custom-call(bf16[4096,128]{1,0:T(8,128)(2,1)S(1)} %bitcast.25, bf16[2,256,256]{2,1,0:T(8,128)(2,1)} %get-tuple-element.53.refs_1_, bf16[2,256,512]{2,1,0:T(8,128)(2,1)} %get-tuple-element.54.refs_2_, ...), custom_call_target="tpu_custom_call" | custom-call | flops 100000000 | bytes 6819840 | tf_op jit(solution)/shard_map/pallas_call | solution.py:116
  105.1 18.2 %all_to_all.71 = bf16[128,16,128]{2,1,0:T(8,128)(2,1)S(1)} all-to-all(bf16[128,16,128]{2,1,0:T(8,128)(2,1)S(1)} %bitcast.30), channel_id=1, replica_groups=mesh['segment'=2,'seq'=32,'mp'=2] {'seq','segment','mp'}, dimensions={0} | all-to-all | bytes 1048576 | tf_op jit(solution)/shard_map/all_to_all | solution.py:24
  123.3 2.2 %shard_map.122 = (bf16[2048,128]{1,0:T(8,128)(2,1)S(1)}, bf16[2,256,512]{2,1,0:T(8,128)(2,1)}) custom-call(bf16[2048,128]{1,0:T(8,128)(2,1)S(1)} %bitcast.35, bf16[2,256,256]{2,1,0:T(8,128)(2,1)} %get-tuple-element.61.refs_1_, f32[2,512]{1,0:T(2,128)} %get-tuple-element.45.refs_3_.refs_2_), custom_call_target="tpu_custom_call" | custom-call | flops 100000000 | bytes 1839104 | tf_op jit(solution)/shard_map/pallas_call | solution.py:116
  125.5 18.0 %all_to_all.72 = bf16[128,16,128]{2,1,0:T(8,128)(2,1)S(1)} all-to-all(bf16[128,16,128]{2,1,0:T(8,128)(2,1)S(1)} %bitcast.31), channel_id=1, replica_groups=mesh['segment'=2,'seq'=32,'mp'=2] {'seq','segment','mp'}, dimensions={0} | all-to-all | bytes 1048576 | tf_op jit(solution)/shard_map/all_to_all | solution.py:24
  143.4 7.7 %shard_map.123 = (bf16[2048,128]{1,0:T(8,128)(2,1)}, bf16[2,256,512]{2,1,0:T(8,128)(2,1)}) custom-call(bf16[2048,128]{1,0:T(8,128)(2,1)S(1)} %bitcast.33, f32[2,256,512]{2,1,0:T(8,128)} %get-tuple-element.63.refs_1_.refs_7_, bf16[2,256,512]{2,1,0:T(8,128)(2,1)} %get-tuple-element.64.refs_2_, bf16[512,512]{1,0:T(8,128)(2,1)} %get-tuple-element.49.refs_7_.refs_3_, ...), custom_call_target="tpu_custom_call" | custom-call | flops 100000000 | bytes 6033408 | tf_op jit(solution)/shard_map/pallas_call | solution.py:116
  151.1 5.3 %all-to-all-start.5 = ((bf16[128,16,128]{2,1,0:T(8,128)(2,1)}), bf16[128,16,128]{2,1,0:T(8,128)(2,1)S(1)}, u32[]{:S(2)}, u32[]{:S(2)}) async-start(bf16[128,16,128]{2,1,0:T(8,128)(2,1)} %bitcast.18), calls=%async_computation.5 | async-start | bytes 1048576 | tf_op jit(solution)/shard_map/all_to_all | solution.py:24
  156.4 2.3 %shard_map.124.refs_1_.refs_4_ = bf16[2,2,128,256]{3,2,1,0:T(8,128)(2,1)} custom-call(bf16[2,256,512]{2,1,0:T(8,128)(2,1)} %get-tuple-element.68.refs_0_, bf16[2,256,512]{2,1,0:T(8,128)(2,1)} %get-tuple-element.69.refs_1_, bf16[2048,128]{1,0:T(8,128)(2,1)S(1)} %get-tuple-element.62.refs_2_), custom_call_target="tpu_custom_call" | custom-call | flops 100000000 | bytes 1310720 | tf_op jit(solution)/shard_map/pallas_call | solution.py:116
  158.8 0.9 copy-done.2
  159.7 1.7 shard_map.125
  161.5 3.3 %collective-permute-start.12 = (bf16[2,256,256]{2,1,0:T(8,128)(2,1)}, bf16[2,256,256]{2,1,0:T(8,128)(2,1)S(1)}, u32[]{:S(2)}, u32[]{:S(2)}) collective-permute-start(bf16[2,256,256]{2,1,0:T(8,128)(2,1)} %shard_map.125), channel_id=1, source_target_pairs={{0,1},{1,0},{2,3},{3,2},{4,5},{5,4},{6,7},{7,6},{8,9},{9,8},{10,11... | collective-permute-start | bytes 786440 | tf_op jit(solution)/shard_map/ppermute | solution.py:28
  164.8 9.1 %collective-permute-done.12.refs_2_ = bf16[2,256,256]{2,1,0:T(8,128)(2,1)S(1)} collective-permute-done((bf16[2,256,256]{2,1,0:T(8,128)(2,1)}, bf16[2,256,256]{2,1,0:T(8,128)(2,1)S(1)}, u32[]{:S(2)}, u32[]{:S(2)}) %collective-permute-start.12) | collective-permute-done | bytes 262176 | tf_op jit(solution)/shard_map/ppermute | solution.py:28
  173.9 0.7 copy-done.10
  174.6 2.4 %shard_map.126.refs_4_ = bf16[4,2,128,256]{3,2,1,0:T(8,128)(2,1)} custom-call(bf16[2048,128]{1,0:T(8,128)(2,1)S(1)} %bitcast.32, bf16[8,256,256]{2,1,0:T(8,128)(2,1)} %bitcast.38, bf16[2,256,256]{2,1,0:T(8,128)(2,1)} %copy-done.10, f32[2,512]{1,0:T(2,128)} %get-tuple-element.44.refs_2_.refs_9_.refs_3_, bf16[2,2,128,256]{3,2,1,0:T(8,128)(2,1)} %shard_map.124.refs_1_.refs_4_), custom_call_target="tpu_custom_call" | custom-call | flops 100000000 | bytes 1839104 | tf_op jit(solution)/shard_map/pallas_call | solution.py:116
  177.0 4.2 %all-to-all-start.6 = ((bf16[4,2,128,256]{3,2,1,0:T(8,128)(2,1)}), bf16[4,2,128,256]{3,2,1,0:T(8,128)(2,1)S(1)}, u32[]{:S(2)}, u32[]{:S(2)}) async-start(bf16[4,2,128,256]{3,2,1,0:T(8,128)(2,1)} %shard_map.126.refs_4_), calls=%async_computation.6 | async-start | bytes 1048576 | tf_op jit(solution)/shard_map/all_to_all | solution.py:637
  181.2 2.3 %shard_map.127.refs_2_ = bf16[2,2,128,256]{3,2,1,0:T(8,128)(2,1)} custom-call(bf16[2,256,512]{2,1,0:T(8,128)(2,1)} %get-tuple-element.72.refs_0_, bf16[2,256,512]{2,1,0:T(8,128)(2,1)} %get-tuple-element.73.refs_1_, bf16[2048,128]{1,0:T(8,128)(2,1)S(1)} %get-tuple-element.60.refs_2_), custom_call_target="tpu_custom_call" | custom-call | flops 100000000 | bytes 1310720 | tf_op jit(solution)/shard_map/pallas_call | solution.py:116
  183.6 2.0 shard_map.128
  185.6 0.6 copy-done.4
  186.2 0.0 collective-permute-start.13
  186.3 3.2 %collective-permute-start.14 = (bf16[2,128,256]{2,1,0:T(8,128)(2,1)S(1)}, bf16[2,128,256]{2,1,0:T(8,128)(2,1)S(1)}, u32[]{:S(2)}, u32[]{:S(2)}) collective-permute-start(bf16[2,128,256]{2,1,0:T(8,128)(2,1)S(1)} %get-tuple-element.76), channel_id=1, source_target_pairs={{0,1},{1,0},{2,3},{3,2},{4,5},{5,4},{6,7},{7,6},{8,9},{9,8},{10,11... | collective-permute-start | bytes 393224 | tf_op jit(solution)/shard_map/ppermute | solution.py:28
  189.5 0.4 collective-permute-start.15
  189.9 3.7 %collective-permute-done.14.refs_2_ = bf16[2,128,256]{2,1,0:T(8,128)(2,1)S(1)} collective-permute-done((bf16[2,128,256]{2,1,0:T(8,128)(2,1)S(1)}, bf16[2,128,256]{2,1,0:T(8,128)(2,1)S(1)}, u32[]{:S(2)}, u32[]{:S(2)}) %collective-permute-start.14) | collective-permute-done | bytes 131104 | tf_op jit(solution)/shard_map/ppermute | solution.py:28
  193.5 3.0 %collective-permute-done.15.refs_3_ = bf16[2,128,256]{2,1,0:T(8,128)(2,1)S(1)} collective-permute-done((bf16[2,128,256]{2,1,0:T(8,128)(2,1)S(1)}, bf16[2,128,256]{2,1,0:T(8,128)(2,1)S(1)}, u32[]{:S(2)}, u32[]{:S(2)}) %collective-permute-start.15) | collective-permute-done | bytes 131104 | tf_op jit(solution)/shard_map/ppermute | solution.py:628
  196.5 0.7 copy-done.13
  197.2 2.0 shard_map.129
  199.2 1.1 bitcast_convert_fusion
  (43 shorter events, 0.1 us)
Async XLA Ops:
  0.6 13.2 %copy-start = (bf16[1,8,256,256]{3,2,1,0:T(8,128)(2,1)S(1)}, bf16[1,8,256,256]{3,2,1,0:T(8,128)(2,1)}, u32[]{:S(2)}) copy-start(bf16[1,8,256,256]{3,2,1,0:T(8,128)(2,1)} %param.14) | copy-start | bytes 3145732
  0.6 12.6 %collective-permute-start.1 = (bf16[8,256,256]{2,1,0:T(8,128)(2,1)}, bf16[8,256,256]{2,1,0:T(8,128)(2,1)S(1)}, u32[]{:S(2)}, u32[]{:S(2)}) collective-permute-start(bf16[8,256,256]{2,1,0:T(8,128)(2,1)} %bitcast.27), channel_id=1, source_target_pairs={{0,64},{64,0},{1,65},{65,1},{2,66},{66,2},{3,67},{67,3},{4,68},{68... | collective-permute-start | bytes 3145736 | tf_op jit(solution)/shard_map/ppermute | solution.py:28
  4.3 6.3 %copy-start.15 = (f32[1,256]{1,0:T(1,128)S(1)}, f32[1,256]{1,0:T(1,128)}, u32[]{:S(2)}) copy-start(f32[1,256]{1,0:T(1,128)} %refs_2_.1) | copy-start | bytes 3076
  4.4 20.2 %collective-permute-start.2 = (bf16[2560,128]{1,0:T(8,128)(2,1)}, bf16[2560,128]{1,0:T(8,128)(2,1)}, u32[]{:S(2)}, u32[]{:S(2)}) collective-permute-start(bf16[2560,128]{1,0:T(8,128)(2,1)} %get-tuple-element.42.refs_0_), channel_id=1, source_target_pairs={{0,33},{1,32},{2,35},{3,34},{4,37},{5,36},{6,39},{7,38},{8,41},{9,... | collective-permute-start | bytes 1966088 | tf_op jit(solution)/shard_map/ppermute | solution.py:488
  5.9 27.2 %collective-permute-start.5 = (bf16[8,256,256]{2,1,0:T(8,128)(2,1)}, bf16[8,256,256]{2,1,0:T(8,128)(2,1)}, u32[]{:S(2)}, u32[]{:S(2)}) collective-permute-start(bf16[8,256,256]{2,1,0:T(8,128)(2,1)} %bitcast.39), channel_id=1, source_target_pairs={{0,64},{64,0},{1,65},{65,1},{2,66},{66,2},{3,67},{67,3},{4,68},{68... | collective-permute-start | bytes 3145736 | tf_op jit(solution)/shard_map/ppermute | solution.py:28
  10.6 2.6 %collective-permute-start = (f32[1,256]{1,0:T(1,128)S(1)}, f32[1,256]{1,0:T(1,128)S(1)}, u32[]{:S(2)}, u32[]{:S(2)}) collective-permute-start(f32[1,256]{1,0:T(1,128)S(1)} %copy-done.15), channel_id=1, source_target_pairs={{0,64},{64,0},{1,65},{65,1},{2,66},{66,2},{3,67},{67,3},{4,68},{68... | collective-permute-start | bytes 3080 | tf_op jit(solution)/shard_map/ppermute | solution.py:28
  13.2 0.6 copy-start.21
  13.2 3.0 %copy-start.1 = (bf16[8,256,256]{2,1,0:T(8,128)(2,1)}, bf16[8,256,256]{2,1,0:T(8,128)(2,1)S(1)}, u32[]{:S(2)}) copy-start(bf16[8,256,256]{2,1,0:T(8,128)(2,1)S(1)} %collective-permute-done.1.refs_5_.refs_1_) | copy-start | bytes 3145732
  16.3 9.5 %copy-start.16 = (f32[1,256]{1,0:T(1,128)S(1)}, f32[1,256]{1,0:T(1,128)}, u32[]{:S(2)}) copy-start(f32[1,256]{1,0:T(1,128)} %refs_2_.1) | copy-start | bytes 3076
  16.3 9.5 %copy-start.20 = (f32[1,256]{1,0:T(1,128)S(1)}, f32[1,256]{1,0:T(1,128)}, u32[]{:S(2)}) copy-start(f32[1,256]{1,0:T(1,128)} %param.12) | copy-start | bytes 3076
  16.3 26.1 %all-to-all-start = ((bf16[128,32,128]{2,1,0:T(8,128)(2,1)}), bf16[128,32,128]{2,1,0:T(8,128)(2,1)S(1)}, u32[]{:S(2)}, u32[]{:S(2)}) async-start(bf16[128,32,128]{2,1,0:T(8,128)(2,1)} %bitcast.6), calls=%async_computation | async-start | bytes 2097152 | tf_op jit(solution)/shard_map/all_to_all | solution.py:24
  23.2 9.8 %collective-permute-start.3 = (bf16[2560,128]{1,0:T(8,128)(2,1)}, bf16[2560,128]{1,0:T(8,128)(2,1)S(1)}, u32[]{:S(2)}, u32[]{:S(2)}) collective-permute-start(bf16[2560,128]{1,0:T(8,128)(2,1)} %get-tuple-element.42.refs_0_), channel_id=1, source_target_pairs={{0,64},{1,65},{2,66},{3,67},{4,68},{5,69},{6,70},{7,71},{8,72},{9,... | collective-permute-start | bytes 1966088 | tf_op jit(solution)/shard_map/ppermute | solution.py:491
  24.5 8.5 %collective-permute-start.4 = (bf16[2560,128]{1,0:T(8,128)(2,1)}, bf16[2560,128]{1,0:T(8,128)(2,1)S(1)}, u32[]{:S(2)}, u32[]{:S(2)}) collective-permute-start(bf16[2560,128]{1,0:T(8,128)(2,1)} %collective-permute-done.2.refs_1_), channel_id=1, source_target_pairs={{0,64},{1,65},{2,66},{3,67},{4,68},{5,69},{6,70},{7,71},{8,72},{9,... | collective-permute-start | bytes 1966088 | tf_op jit(solution)/shard_map/ppermute | solution.py:491
  25.9 7.2 %copy-start.14 = (f32[2,256]{1,0:T(2,128)}, f32[2,256]{1,0:T(2,128)S(1)}, u32[]{:S(2)}) copy-start(f32[2,256]{1,0:T(2,128)S(1)} %pad_maximum_fusion.refs_6_) | copy-start | bytes 6148
  25.9 5.0 %collective-permute-start.6 = (f32[2,256]{1,0:T(2,128)S(1)}, f32[2,256]{1,0:T(2,128)S(1)}, u32[]{:S(2)}, u32[]{:S(2)}) collective-permute-start(f32[2,256]{1,0:T(2,128)S(1)} %pad_maximum_fusion.refs_6_), channel_id=1, source_target_pairs={{0,33},{1,32},{2,35},{3,34},{4,37},{5,36},{6,39},{7,38},{8,41},{9,... | collective-permute-start | bytes 6152 | tf_op jit(solution)/shard_map/ppermute | solution.py:488
  29.2 3.1 %collective-permute-start.7 = (f32[2,256]{1,0:T(2,128)S(1)}, f32[2,256]{1,0:T(2,128)S(1)}, u32[]{:S(2)}, u32[]{:S(2)}) collective-permute-start(f32[2,256]{1,0:T(2,128)S(1)} %pad_maximum_fusion.refs_6_), channel_id=1, source_target_pairs={{0,64},{64,0},{1,65},{65,1},{2,66},{66,2},{3,67},{67,3},{4,68},{68... | collective-permute-start | bytes 6152 | tf_op jit(solution)/shard_map/ppermute | solution.py:28
  30.9 2.2 %copy-start.17 = (f32[2,256]{1,0:T(2,128)}, f32[2,256]{1,0:T(2,128)S(1)}, u32[]{:S(2)}) copy-start(f32[2,256]{1,0:T(2,128)S(1)} %collective-permute-done.6.refs_7_) | copy-start | bytes 6148
  30.9 2.2 %collective-permute-start.8 = (f32[2,256]{1,0:T(2,128)S(1)}, f32[2,256]{1,0:T(2,128)S(1)}, u32[]{:S(2)}, u32[]{:S(2)}) collective-permute-start(f32[2,256]{1,0:T(2,128)S(1)} %collective-permute-done.6.refs_7_), channel_id=1, source_target_pairs={{0,64},{64,0},{1,65},{65,1},{2,66},{66,2},{3,67},{67,3},{4,68},{68... | collective-permute-start | bytes 6152 | tf_op jit(solution)/shard_map/ppermute | solution.py:28
  32.2 0.9 copy-start.18
  33.1 0.6 copy-start.19
  33.1 0.8 copy-start.6
  33.9 0.8 copy-start.7
  49.3 21.8 %all-to-all-start.1 = ((bf16[128,16,128]{2,1,0:T(8,128)(2,1)}), bf16[128,16,128]{2,1,0:T(8,128)(2,1)S(1)}, u32[]{:S(2)}, u32[]{:S(2)}) async-start(bf16[128,16,128]{2,1,0:T(8,128)(2,1)} %bitcast.9), calls=%async_computation.1 | async-start | bytes 1048576 | tf_op jit(solution)/shard_map/all_to_all | solution.py:24
  58.2 24.4 %collective-permute-start.9 = (bf16[2560,128]{1,0:T(8,128)(2,1)}, bf16[2560,128]{1,0:T(8,128)(2,1)S(1)}, u32[]{:S(2)}, u32[]{:S(2)}) collective-permute-start(bf16[2560,128]{1,0:T(8,128)(2,1)} %get-tuple-element.42.refs_0_), channel_id=1, source_target_pairs={{64,97},{65,96},{66,99},{67,98},{68,101},{69,100},{70,103},{71,102... | collective-permute-start | bytes 1966088 | tf_op jit(solution)/shard_map/ppermute | solution.py:488
  66.1 1.0 copy-start.3
  74.3 23.5 %all-to-all-start.2 = ((bf16[128,32,128]{2,1,0:T(8,128)(2,1)}), bf16[128,32,128]{2,1,0:T(8,128)(2,1)S(1)}, u32[]{:S(2)}, u32[]{:S(2)}) async-start(bf16[128,32,128]{2,1,0:T(8,128)(2,1)} %bitcast.12), calls=%async_computation.2 | async-start | bytes 2097152 | tf_op jit(solution)/shard_map/all_to_all | solution.py:24
  79.6 4.9 %collective-permute-start.10 = (bf16[2560,128]{1,0:T(8,128)(2,1)}, bf16[2560,128]{1,0:T(8,128)(2,1)S(1)}, u32[]{:S(2)}, u32[]{:S(2)}) collective-permute-start(bf16[2560,128]{1,0:T(8,128)(2,1)} %get-tuple-element.42.refs_0_), channel_id=1, source_target_pairs={{64,0},{65,1},{66,2},{67,3},{68,4},{69,5},{70,6},{71,7},{72,8},{73... | collective-permute-start | bytes 1966088 | tf_op jit(solution)/shard_map/ppermute | solution.py:491
  82.6 3.0 %copy-start.5 = (bf16[2560,128]{1,0:T(8,128)(2,1)}, bf16[2560,128]{1,0:T(8,128)(2,1)S(1)}, u32[]{:S(2)}) copy-start(bf16[2560,128]{1,0:T(8,128)(2,1)S(1)} %collective-permute-done.9.refs_1_) | copy-start | bytes 1966084
  82.6 3.0 %collective-permute-start.11 = (bf16[2560,128]{1,0:T(8,128)(2,1)S(1)}, bf16[2560,128]{1,0:T(8,128)(2,1)S(1)}, u32[]{:S(2)}, u32[]{:S(2)}) collective-permute-start(bf16[2560,128]{1,0:T(8,128)(2,1)S(1)} %collective-permute-done.9.refs_1_), channel_id=1, source_target_pairs={{64,0},{65,1},{66,2},{67,3},{68,4},{69,5},{70,6},{71,7},{72,8},{73... | collective-permute-start | bytes 1966088 | tf_op jit(solution)/shard_map/ppermute | solution.py:491
  84.5 1.2 copy-start.8
  85.6 0.8 copy-start.9
  151.1 22.7 %all-to-all-start.5 = ((bf16[128,16,128]{2,1,0:T(8,128)(2,1)}), bf16[128,16,128]{2,1,0:T(8,128)(2,1)S(1)}, u32[]{:S(2)}, u32[]{:S(2)}) async-start(bf16[128,16,128]{2,1,0:T(8,128)(2,1)} %bitcast.18), calls=%async_computation.5 | async-start | bytes 1048576 | tf_op jit(solution)/shard_map/all_to_all | solution.py:24
  158.8 1.0 copy-start.2
  161.5 12.4 %collective-permute-start.12 = (bf16[2,256,256]{2,1,0:T(8,128)(2,1)}, bf16[2,256,256]{2,1,0:T(8,128)(2,1)S(1)}, u32[]{:S(2)}, u32[]{:S(2)}) collective-permute-start(bf16[2,256,256]{2,1,0:T(8,128)(2,1)} %shard_map.125), channel_id=1, source_target_pairs={{0,1},{1,0},{2,3},{3,2},{4,5},{5,4},{6,7},{7,6},{8,9},{9,8},{10,11... | collective-permute-start | bytes 786440 | tf_op jit(solution)/shard_map/ppermute | solution.py:28
  173.9 0.7 copy-start.10
  177.0 22.1 %all-to-all-start.6 = ((bf16[4,2,128,256]{3,2,1,0:T(8,128)(2,1)}), bf16[4,2,128,256]{3,2,1,0:T(8,128)(2,1)S(1)}, u32[]{:S(2)}, u32[]{:S(2)}) async-start(bf16[4,2,128,256]{3,2,1,0:T(8,128)(2,1)} %shard_map.126.refs_4_), calls=%async_computation.6 | async-start | bytes 1048576 | tf_op jit(solution)/shard_map/all_to_all | solution.py:637
  185.6 0.7 copy-start.4
  186.2 3.6 %collective-permute-start.13 = (bf16[2,128,256]{2,1,0:T(8,128)(2,1)S(1)}, bf16[2,128,256]{2,1,0:T(8,128)(2,1)S(1)}, u32[]{:S(2)}, u32[]{:S(2)}) collective-permute-start(bf16[2,128,256]{2,1,0:T(8,128)(2,1)S(1)} %get-tuple-element.75), channel_id=1, source_target_pairs={{0,64},{64,0},{1,65},{65,1},{2,66},{66,2},{3,67},{67,3},{4,68},{68... | collective-permute-start | bytes 393224 | tf_op jit(solution)/shard_map/ppermute | solution.py:28
  186.3 7.3 %collective-permute-start.14 = (bf16[2,128,256]{2,1,0:T(8,128)(2,1)S(1)}, bf16[2,128,256]{2,1,0:T(8,128)(2,1)S(1)}, u32[]{:S(2)}, u32[]{:S(2)}) collective-permute-start(bf16[2,128,256]{2,1,0:T(8,128)(2,1)S(1)} %get-tuple-element.76), channel_id=1, source_target_pairs={{0,1},{1,0},{2,3},{3,2},{4,5},{5,4},{6,7},{7,6},{8,9},{9,8},{10,11... | collective-permute-start | bytes 393224 | tf_op jit(solution)/shard_map/ppermute | solution.py:28
  189.5 7.0 %collective-permute-start.15 = (bf16[2,128,256]{2,1,0:T(8,128)(2,1)S(1)}, bf16[2,128,256]{2,1,0:T(8,128)(2,1)S(1)}, u32[]{:S(2)}, u32[]{:S(2)}) collective-permute-start(bf16[2,128,256]{2,1,0:T(8,128)(2,1)S(1)} %get-tuple-element.77), channel_id=1, source_target_pairs={{0,65},{1,64},{64,1},{65,0},{2,67},{3,66},{66,3},{67,2},{4,69},{5,... | collective-permute-start | bytes 393224 | tf_op jit(solution)/shard_map/ppermute | solution.py:628
  189.9 6.7 %copy-start.11 = (bf16[2,128,256]{2,1,0:T(8,128)(2,1)}, bf16[2,128,256]{2,1,0:T(8,128)(2,1)S(1)}, u32[]{:S(2)}) copy-start(bf16[2,128,256]{2,1,0:T(8,128)(2,1)S(1)} %collective-permute-done.13.refs_1_) | copy-start | bytes 393220
  193.5 3.0 %copy-start.12 = (bf16[2,128,256]{2,1,0:T(8,128)(2,1)}, bf16[2,128,256]{2,1,0:T(8,128)(2,1)S(1)}, u32[]{:S(2)}) copy-start(bf16[2,128,256]{2,1,0:T(8,128)(2,1)S(1)} %collective-permute-done.14.refs_2_) | copy-start | bytes 393220
  196.5 0.7 copy-start.13

commit v4 on v3

--- a/solution.py
+++ b/solution.py
@@ -232,8 +232,10 @@
 
 
 def pack_body(ins, outs, packed, temp):
-    x_ref, up1, ds, d1, up2 = ins
-    out, x_out, x_tiles = outs
+    x_ref, up1, ds, d1, up2, gate, key = ins
+    out, x_out, x_tiles, gains = outs
+    gains[0:1, :] = gate[...]
+    gains[1:2, :] = key[...]
     for i in range(2):
         out[i * 128 : (i + 1) * 128, :] = up1[i]
         out[256 + i * 128 : 256 + (i + 1) * 128, :] = ds[i]
@@ -248,9 +250,9 @@
 
 
 def first_rows_body(ins, outs, packed, temp):
-    x_ref, x_tiles, key_mine, key_got, mine_ref, got_ref = ins
+    x_ref, x_tiles, gains, key_got, mine_ref, got_ref = ins
     g = core()
-    key = jnp.where(g == 0, key_mine[...], key_got[...])
+    key = jnp.where(g == 0, gains[1:2, :], key_got[...])
     for a in range(4):
         factor = jnp.where(g == 0, mine_ref[a], got_ref[4 * g + a])
         scaled = (x_ref[a].astype(F32) * key).astype(BF)
@@ -404,15 +406,23 @@
         outs[0].send(part)
 
 
-def ffn_back(cot, hidden, u, v, up2, down1):
-    permuted = dot(hidden, u[...]).astype(BF)
+def slope_body(ins, outs):
+    hidden, u, up2 = ins
+    for oo in range(2):
+        permuted = dot(hidden[oo], u[...]).astype(BF)
+        for j in range(4):
+            block = slice(j * 128, (j + 1) * 128)
+            outs[0].ref[oo, j] = slope(dot(permuted[:, block], up2[j])).astype(BF)
+        outs[0].send(oo)
+
+
+def ffn_back(cot, slope_of, u, v, up2, down1):
     fold = dot_nt(cot, v[...]).astype(BF)
     perms = []
     for j in range(4):
         block = slice(j * 128, (j + 1) * 128)
-        preact = dot(permuted[:, block], up2[j])
         back_active = dot_nt(fold[:, block], down1[j])
-        back_preact = (back_active * slope(preact)).astype(BF)
+        back_preact = (back_active * slope_of(j)).astype(BF)
         perms.append(dot_nt(back_preact, up2[j]).astype(BF))
     return cot.astype(F32) + dot_nt(jnp.concatenate(perms, axis=1), u[...])
 
@@ -433,7 +443,12 @@
         logistic = sigmoid(pre)
         gated = pre * logistic
         hidden = (x + gated * turned).astype(BF)
-        back_hidden = ffn_back(cot, hidden, u, v, up2, down1)
+        permuted = dot(hidden, u[...]).astype(BF)
+
+        def slope_of(j):
+            return slope(dot(permuted[:, j * 128 : (j + 1) * 128], up2[j]))
+
+        back_hidden = ffn_back(cot, slope_of, u, v, up2, down1)
         back_turned = (back_hidden * gated).astype(BF)
         back_turned_out.ref[oo] = back_turned
         back_turned_out.send(oo)
@@ -445,13 +460,13 @@
 
 
 def lower_cols_body(ins, outs, wide, packed):
-    msg, direct0, hidden_ref, v, u, up2, down1, direct1, x_ref, gains, factor_t = ins
-    direct = direct0, direct1
+    msg, direct0, v, down1, slopes0, up2, u, x_ref, gains, direct1, slopes1, factor_t = ins
+    direct, slopes = (direct0, direct1), (slopes0, slopes1)
     out_msg, back_turned_out = outs
     widen(msg, wide)
     for oo in range(2):
         passed = (direct[oo][...] + unpack_cols(wide, oo)).astype(BF)
-        back_hidden = ffn_back(passed, hidden_ref[oo], u, v, up2, down1)
+        back_hidden = ffn_back(passed, lambda j: slopes[oo][j].astype(F32), u, v, up2, down1)
         pre = x_ref[oo].astype(F32) * gains[0:1, :]
         back_turned = (back_hidden * (pre * sigmoid(pre))).astype(BF)
         back_turned_out.ref[oo] = back_turned
@@ -509,11 +524,11 @@
     scratch_pack = [(MSG, F32), ((256, 128), F32)]
 
     key_got = swap(key_gain, "segment")
-    own, x_rows, x_tiles = call(
+    own, x_rows, x_tiles, gains = call(
         pack_body,
-        [Near(((WEIGHT_ROWS, 128), BF)), Near(((4, 256, 256), BF)), tiles],
+        [Near(((WEIGHT_ROWS, 128), BF)), Near(((4, 256, 256), BF)), tiles, Near(((2, 256), F32))],
         scratch_pack,
-        (four(rows), up_first[0], down_second_weight[0], down_first[0], up_second[0]),
+        (four(rows), up_first[0], down_second_weight[0], down_first[0], up_second[0], gate_gain, key_gain),
     )
     first_got = swap(first_mine, "segment")
     peer0 = swap_z(own, (0,))
@@ -521,7 +536,7 @@
         first_rows_body,
         [Near((PAIR, BF))],
         scratch_pack,
-        (Near(x_rows), Near(x_tiles), key_gain, key_got, Near(first_mine), Near(first_got)),
+        (Near(x_rows), Near(x_tiles), Near(gains), Near(key_got), Near(first_mine), Near(first_got)),
     )
 
     def send(message, order=ROWS_ORDER):
@@ -530,7 +545,6 @@
     msg = send(rows_msg, QUARTER_ORDER)
 
     second_got = swap(second_mine, "segment")
-    gains = jnp.concatenate([gate_gain, key_gain])
     gains_peer = swap_z(gains, (0, 1))
     gains_got = swap(gains, "segment")
     gains_both = swap(gains_peer, "segment")
@@ -594,6 +608,10 @@
 
     second_grad1 = channel_grad(back_turned1, mixed1, next_msg)
 
+    (slopes,) = call(
+        slope_body, [((2, 4, 256, 512), BF)], [], (hidden0, u0, up0), after=(second_grad1,)
+    )
+
     next_msg, back_rows1 = call(
         rows_body, [tiles, block], scratch_rows, (Near(msg), first1_t, gains1)
     )
@@ -613,7 +631,10 @@
         lower_cols_body,
         [tiles, block],
         [(MSG, F32)] * 2,
-        (Near(msg), part(direct, 0), hidden0, v0, u0, up0, down0, part(direct, 1), x0, gains0, second0_t),
+        (
+            Near(msg), part(direct, 0), v0, down0, part(slopes, 0), up0, u0, x0, gains0,
+            part(direct, 1), part(slopes, 1), second0_t,
+        ),
     )
     msg = send(next_msg)
     half = Near(((2, 128, 256), BF))

time: 201 us -> 200 us (level)
  blocking collectives: 36.1 us -> 18.1 us
  waiting for transfers between devices: 34 us -> 41.7 us
  starting transfers between devices: 63.6 us -> 69 us
  Pallas kernels: 57.4 us -> 60.8 us
    all_to_all x2 -> x1, blocking collectives: 36.1 us -> 18.1 us  [exchange(): lax.all_to_all(message, order, split_axis=0, concat_axis=0, tiled=True)]
    all_to_all x4 -> x5, waiting for transfers between devices: 13 us -> 18.4 us  [exchange(): lax.all_to_all(message, order, split_axis=0, concat_axis=0, tiled=True)]
    all_to_all x4 -> x5, starting transfers between devices: 26.4 us -> 31.8 us  [exchange(): lax.all_to_all(message, order, split_axis=0, concat_axis=0, tiled=True)]
    pallas_call x17 -> x18, Pallas kernels: 57.4 us -> 60.8 us  [call(): pl.pallas_call(kernel, out_shape=tuple((jax.ShapeDtypeStruct(*o) if n els...]
    ppermute x8, waiting for transfers between devices: 16.1 us -> 18.3 us  [swap(): return lax.ppermute(value, axis, [(0, 1), (1, 0)])]
    unnamed x44 -> x38, local copies, waits for them, and re-layouts: 6.97 us -> 7.34 us
  transfers between devices with their start and end apart: 21 -> 22, of which waited for: 11 -> 12; matrix products, arithmetic and copies ran while one was open for 0% -> 0% of each run, Pallas kernels for 15% -> 17%
where the time goes in v4:
time: 200 us; the launch traced here: 199 us
  starting transfers between devices  69 us (34%)
  Pallas kernels  60.8 us (30%)
  waiting for transfers between devices  41.7 us (21%)
  blocking collectives  18.1 us (9%)
  local copies, waits for them, and re-layouts  7.34 us (4%)
    pallas_call x18, Pallas kernels, call(): pl.pallas_call(kernel, out_shape=tuple((jax.ShapeDtypeStruct(*o) if n els...  60.8 us
    all_to_all x5, starting transfers between devices, exchange(): lax.all_to_all(message, order, split_axis=0, concat_axis=0, tiled=True)  31.8 us
    all_to_all x5, waiting for transfers between devices, exchange(): lax.all_to_all(message, order, split_axis=0, concat_axis=0, tiled=True)  18.4 us
    ppermute x8, waiting for transfers between devices, swap(): return lax.ppermute(value, axis, [(0, 1), (1, 0)])  18.3 us
    all_to_all x1, blocking collectives, exchange(): lax.all_to_all(message, order, split_axis=0, concat_axis=0, tiled=True)  18.1 us
    ppermute x8, starting transfers between devices, swap(): return lax.ppermute(value, axis, [(0, 1), (1, 0)])  15.7 us
    ppermute x3, starting transfers between devices, swap_z(): return lax.ppermute(value, ('segment', 'seq', 'mp'), pairs)  9.96 us
    unnamed x38, local copies, waits for them, and re-layouts  7.34 us
  transfers between devices with their start and end apart: 22, of which 12 were waited for; matrix products, arithmetic and copies ran while one was open for 0% of the time, Pallas kernels for 17%

profile of v4, /device:TPU:1, one launch (start us, length us, event | category | flops | bytes accessed | tf_op | source)
XLA Modules:
  0.0 199.0 jit_solution(1958905862098042009)
XLA Ops:
  0.6 1.5 collective-permute-start.1
  2.1 2.3 %shard_map.113 = (bf16[2560,128]{1,0:T(8,128)(2,1)}, bf16[4,256,256]{2,1,0:T(8,128)(2,1)S(1)}, bf16[2048,128]{1,0:T(8,128)(2,1)S(1)}, f32[2,256]{1,0:T(2,128)S(1)}) custom-call(bf16[8,256,256]{2,1,0:T(8,128)(2,1)} %bitcast.35, bf16[2,128,128]{2,1,0:T(8,128)(2,1)} %bitcast.46, bf16[2,128,128]{2,1,0:T(8,128)(2,1)} %bitcast.47, bf16[2,512,128]{2,1,0:T(8,128)(2,1)} %bitcast.44, ...), custom_call_target="tpu_custom_call" | custom-call | flops 100000000 | bytes 2887680 | tf_op jit(solution)/shard_map/pallas_call | solution.py:116
  4.4 1.5 collective-permute-start.2
  5.9 4.7 %collective-permute-start.5 = (bf16[8,256,256]{2,1,0:T(8,128)(2,1)}, bf16[8,256,256]{2,1,0:T(8,128)(2,1)}, u32[]{:S(2)}, u32[]{:S(2)}) collective-permute-start(bf16[8,256,256]{2,1,0:T(8,128)(2,1)} %bitcast.38), channel_id=1, source_target_pairs={{0,64},{64,0},{1,65},{65,1},{2,66},{66,2},{3,67},{67,3},{4,68},{68... | collective-permute-start | bytes 3145736 | tf_op jit(solution)/shard_map/ppermute | solution.py:28
  10.6 0.1 collective-permute-start
  10.7 2.5 %collective-permute-done.refs_3_ = f32[1,256]{1,0:T(1,128)S(1)} collective-permute-done((f32[1,256]{1,0:T(1,128)}, f32[1,256]{1,0:T(1,128)S(1)}, u32[]{:S(2)}, u32[]{:S(2)}) %collective-permute-start) | collective-permute-done | bytes 1056 | tf_op jit(solution)/shard_map/ppermute | solution.py:28
  13.3 1.8 shard_map.114
  15.1 6.9 %all-to-all-start = ((bf16[128,32,128]{2,1,0:T(8,128)(2,1)}), bf16[128,32,128]{2,1,0:T(8,128)(2,1)S(1)}, u32[]{:S(2)}, u32[]{:S(2)}) async-start(bf16[128,32,128]{2,1,0:T(8,128)(2,1)} %bitcast.6), calls=%async_computation | async-start | bytes 2097152 | tf_op jit(solution)/shard_map/all_to_all | solution.py:24
  22.0 1.3 collective-permute-start.3
  23.3 1.3 collective-permute-start.4
  24.6 3.3 %collective-permute-start.6 = (f32[2,256]{1,0:T(2,128)S(1)}, f32[2,256]{1,0:T(2,128)S(1)}, u32[]{:S(2)}, u32[]{:S(2)}) collective-permute-start(f32[2,256]{1,0:T(2,128)S(1)} %get-tuple-element.43.refs_2_.refs_6_), channel_id=1, source_target_pairs={{0,33},{1,32},{2,35},{3,34},{4,37},{5,36},{6,39},{7,38},{8,41},{9,... | collective-permute-start | bytes 6152 | tf_op jit(solution)/shard_map/ppermute | solution.py:503
  27.9 1.5 collective-permute-start.7
  29.4 0.3 collective-permute-done.6.refs_7_
  29.7 1.3 collective-permute-start.8
  31.0 0.8 collective-permute-done.8.refs_9_
  31.9 0.5 copy-done.18
  32.4 0.3 copy-done.8
  32.7 0.8 copy-done.9
  33.5 4.3 %shard_map.115 = (bf16[512,512]{1,0:T(8,128)(2,1)}, bf16[512,512]{1,0:T(8,128)(2,1)}, bf16[4,128,512]{2,1,0:T(8,128)(2,1)}, bf16[4,512,128]{2,1,0:T(8,128)(2,1)}...) custom-call(bf16[2560,128]{1,0:T(8,128)(2,1)} %get-tuple-element.44.refs_0_, ...), custom_call_target="tpu_custom_call" | custom-call | flops 100000000 | bytes 5521408 | tf_op jit(solution)/shard_map/pallas_call | solution.py:116
  37.8 3.4 %all-to-all-done = bf16[128,32,128]{2,1,0:T(8,128)(2,1)S(1)} async-done(((bf16[128,32,128]{2,1,0:T(8,128)(2,1)}), bf16[128,32,128]{2,1,0:T(8,128)(2,1)S(1)}, u32[]{:S(2)}, u32[]{:S(2)}) %all-to-all-start) | async-done | bytes 1048608 | tf_op jit(solution)/shard_map/all_to_all | solution.py:24
  41.2 6.8 %shard_map.116 = (bf16[2048,128]{1,0:T(8,128)(2,1)}, bf16[2,256,512]{2,1,0:T(8,128)(2,1)}, bf16[2,256,512]{2,1,0:T(8,128)(2,1)}, bf16[2,256,512]{2,1,0:T(8,128)(2,1)}, bf16[2,256,512]{2,1,0:T(8,128)(2,1)}) custom-call(bf16[4096,128]{1,0:T(8,128)(2,1)S(1)} %bitcast.26, bf16[2,256,256]{2,1,0:T(8,128)(2,1)} %get-tuple-element.45.refs_1_, ...), custom_call_target="tpu_custom_call" | custom-call | flops 100000000 | bytes 6037504 | tf_op jit(solution)/shard_map/pallas_call | solution.py:116
  48.0 9.0 %all-to-all-start.1 = ((bf16[128,16,128]{2,1,0:T(8,128)(2,1)}), bf16[128,16,128]{2,1,0:T(8,128)(2,1)S(1)}, u32[]{:S(2)}, u32[]{:S(2)}) async-start(bf16[128,16,128]{2,1,0:T(8,128)(2,1)} %bitcast.9), calls=%async_computation.1 | async-start | bytes 1048576 | tf_op jit(solution)/shard_map/all_to_all | solution.py:24
  57.0 5.1 %collective-permute-start.9 = (bf16[2560,128]{1,0:T(8,128)(2,1)}, bf16[2560,128]{1,0:T(8,128)(2,1)S(1)}, u32[]{:S(2)}, u32[]{:S(2)}) collective-permute-start(bf16[2560,128]{1,0:T(8,128)(2,1)} %get-tuple-element.44.refs_0_), channel_id=1, source_target_pairs={{64,97},{65,96},{66,99},{67,98},{68,101},{69,100},{70,103},{71,102... | collective-permute-start | bytes 1966088 | tf_op jit(solution)/shard_map/ppermute | solution.py:503
  62.2 2.7 %shard_map.117 = (bf16[2,256,256]{2,1,0:T(8,128)(2,1)}, bf16[2,256,256]{2,1,0:T(8,128)(2,1)}, bf16[2,256,256]{2,1,0:T(8,128)(2,1)}, bf16[2,256,256]{2,1,0:T(8,128)(2,1)}, bf16[2,256,256]{2,1,0:T(8,128)(2,1)}) custom-call(bf16[8,256,256]{2,1,0:T(8,128)(2,1)} %bitcast.28, bf16[8,256,256]{2,1,0:T(8,128)(2,1)} %copy-done.1, bf16[8,256,256]{2,1,0:T(8,128)(2,1)} %bitcast.40, ...), custom_call_target="tpu_custom_call" | custom-call | flops 100000000 | bytes 2359296 | tf_op jit(solution)/shard_map/pallas_call | solution.py:116
  64.9 0.9 copy-done.4
  65.9 1.6 shard_map.118.refs_2_
  67.5 2.4 %all-to-all-done.1 = bf16[128,16,128]{2,1,0:T(8,128)(2,1)S(1)} async-done(((bf16[128,16,128]{2,1,0:T(8,128)(2,1)}), bf16[128,16,128]{2,1,0:T(8,128)(2,1)S(1)}, u32[]{:S(2)}, u32[]{:S(2)}) %all-to-all-start.1) | async-done | bytes 524320 | tf_op jit(solution)/shard_map/all_to_all | solution.py:24
  69.9 3.2 %shard_map.119 = (bf16[4096,128]{1,0:T(8,128)(2,1)}, bf16[2,256,512]{2,1,0:T(8,128)(2,1)}) custom-call(bf16[2048,128]{1,0:T(8,128)(2,1)S(1)} %bitcast.33, bf16[2,256,256]{2,1,0:T(8,128)(2,1)} %get-tuple-element.53.refs_1_, bf16[2048,128]{1,0:T(8,128)(2,1)S(1)} %shard_map.118.refs_2_), custom_call_target="tpu_custom_call" | custom-call | flops 100000000 | bytes 2883584 | tf_op jit(solution)/shard_map/pallas_call | solution.py:116
  73.1 5.3 %all-to-all-start.2 = ((bf16[128,32,128]{2,1,0:T(8,128)(2,1)}), bf16[128,32,128]{2,1,0:T(8,128)(2,1)S(1)}, u32[]{:S(2)}, u32[]{:S(2)}) async-start(bf16[128,32,128]{2,1,0:T(8,128)(2,1)} %bitcast.12), calls=%async_computation.2 | async-start | bytes 2097152 | tf_op jit(solution)/shard_map/all_to_all | solution.py:24
  78.4 3.0 %collective-permute-start.10 = (bf16[2560,128]{1,0:T(8,128)(2,1)}, bf16[2560,128]{1,0:T(8,128)(2,1)S(1)}, u32[]{:S(2)}, u32[]{:S(2)}) collective-permute-start(bf16[2560,128]{1,0:T(8,128)(2,1)} %get-tuple-element.44.refs_0_), channel_id=1, source_target_pairs={{64,0},{65,1},{66,2},{67,3},{68,4},{69,5},{70,6},{71,7},{72,8},{73... | collective-permute-start | bytes 1966088 | tf_op jit(solution)/shard_map/ppermute | solution.py:506
  81.4 1.3 collective-permute-start.11
  82.8 0.5 collective-permute-done.10.refs_2_
  83.3 1.1 collective-permute-done.11.refs_3_
  84.4 0.8 copy-done.11
  85.3 4.0 %shard_map.120 = (bf16[512,512]{1,0:T(8,128)(2,1)}, bf16[512,512]{1,0:T(8,128)(2,1)}, bf16[4,128,512]{2,1,0:T(8,128)(2,1)}, bf16[4,512,128]{2,1,0:T(8,128)(2,1)}) custom-call(bf16[2560,128]{1,0:T(8,128)(2,1)} %get-tuple-element.44.refs_0_, bf16[2560,128]{1,0:T(8,128)(2,1)} %copy-done.7, bf16[2560,128]{1,0:T(8,128)(2,1)} %copy-done.10, ...), custom_call_target="tpu_custom_call" | custom-call | flops 100000000 | bytes 4718592 | tf_op jit(solution)/shard_map/pallas_call | solution.py:116
  89.3 7.2 %all-to-all-done.2 = bf16[128,32,128]{2,1,0:T(8,128)(2,1)S(1)} async-done(((bf16[128,32,128]{2,1,0:T(8,128)(2,1)}), bf16[128,32,128]{2,1,0:T(8,128)(2,1)S(1)}, u32[]{:S(2)}, u32[]{:S(2)}) %all-to-all-start.2) | async-done | bytes 1048608 | tf_op jit(solution)/shard_map/all_to_all | solution.py:24
  96.5 7.6 %shard_map.121 = (bf16[2048,128]{1,0:T(8,128)(2,1)S(1)}, bf16[2,256,512]{2,1,0:T(8,128)(2,1)}, bf16[2,256,512]{2,1,0:T(8,128)(2,1)}, f32[2,256,512]{2,1,0:T(8,128)}) custom-call(bf16[4096,128]{1,0:T(8,128)(2,1)S(1)} %bitcast.25, bf16[2,256,256]{2,1,0:T(8,128)(2,1)} %get-tuple-element.55.refs_1_, bf16[2,256,512]{2,1,0:T(8,128)(2,1)} %get-tuple-element.56.refs_2_, ...), custom_call_target="tpu_custom_call" | custom-call | flops 100000000 | bytes 6819840 | tf_op jit(solution)/shard_map/pallas_call | solution.py:116
  104.1 18.1 %all_to_all.71 = bf16[128,16,128]{2,1,0:T(8,128)(2,1)S(1)} all-to-all(bf16[128,16,128]{2,1,0:T(8,128)(2,1)S(1)} %bitcast.31), channel_id=1, replica_groups=mesh['segment'=2,'seq'=32,'mp'=2] {'seq','segment','mp'}, dimensions={0} | all-to-all | bytes 1048576 | tf_op jit(solution)/shard_map/all_to_all | solution.py:24
  122.3 3.0 %shard_map.122 = (bf16[2048,128]{1,0:T(8,128)(2,1)}, bf16[2,256,512]{2,1,0:T(8,128)(2,1)}) custom-call(bf16[2048,128]{1,0:T(8,128)(2,1)S(1)} %bitcast.34, bf16[2,256,256]{2,1,0:T(8,128)(2,1)} %get-tuple-element.63.refs_1_, f32[2,512]{1,0:T(2,128)} %get-tuple-element.47.refs_3_.refs_2_), custom_call_target="tpu_custom_call" | custom-call | flops 100000000 | bytes 1839104 | tf_op jit(solution)/shard_map/pallas_call | solution.py:116
  125.3 5.3 %all-to-all-start.4 = ((bf16[128,16,128]{2,1,0:T(8,128)(2,1)}), bf16[128,16,128]{2,1,0:T(8,128)(2,1)S(1)}, u32[]{:S(2)}, u32[]{:S(2)}) async-start(bf16[128,16,128]{2,1,0:T(8,128)(2,1)} %bitcast.16), calls=%async_computation.4 | async-start | bytes 1048576 | tf_op jit(solution)/shard_map/all_to_all | solution.py:24
  130.6 2.3 %shard_map.123.refs_3_.refs_2_ = bf16[2,2,128,256]{3,2,1,0:T(8,128)(2,1)} custom-call(bf16[2,256,512]{2,1,0:T(8,128)(2,1)} %get-tuple-element.67.refs_0_, bf16[2,256,512]{2,1,0:T(8,128)(2,1)} %get-tuple-element.68.refs_1_, bf16[2048,128]{1,0:T(8,128)(2,1)S(1)} %get-tuple-element.62.refs_2_), custom_call_target="tpu_custom_call" | custom-call | flops 100000000 | bytes 1310720 | tf_op jit(solution)/shard_map/pallas_call | solution.py:116
  133.0 0.9 copy-done.3
  133.9 4.1 %shard_map.124.refs_4_.refs_10_ = bf16[2,4,256,512]{3,2,1,0:T(8,128)(2,1)} custom-call(bf16[2,256,512]{2,1,0:T(8,128)(2,1)} %get-tuple-element.66.refs_0_, bf16[512,512]{1,0:T(8,128)(2,1)} %get-tuple-element.48.refs_4_.refs_1_.refs_6_, bf16[4,128,512]{2,1,0:T(8,128)(2,1)} %get-tuple-element.49.refs_5_.refs_2_, bf16[2,2,128,256]{3,2,1,0:T(8,128)(2,1)S(1)} %copy-done.3), custom_call_target="tpu_custom_call" | custom-call | flops 100000000 | bytes 3670016 | tf_op jit(solution)/shard_map/pallas_call | solution.py:116
  138.1 5.4 %all-to-all-done.4 = bf16[128,16,128]{2,1,0:T(8,128)(2,1)S(1)} async-done(((bf16[128,16,128]{2,1,0:T(8,128)(2,1)}), bf16[128,16,128]{2,1,0:T(8,128)(2,1)S(1)}, u32[]{:S(2)}, u32[]{:S(2)}) %all-to-all-start.4) | async-done | bytes 524320 | tf_op jit(solution)/shard_map/all_to_all | solution.py:24
  143.5 6.4 %shard_map.125 = (bf16[2048,128]{1,0:T(8,128)(2,1)}, bf16[2,256,512]{2,1,0:T(8,128)(2,1)}) custom-call(bf16[2048,128]{1,0:T(8,128)(2,1)S(1)} %bitcast.30, f32[2,256,512]{2,1,0:T(8,128)} %get-tuple-element.65.refs_1_.refs_9_, bf16[512,512]{1,0:T(8,128)(2,1)} %get-tuple-element.51.refs_7_.refs_2_, bf16[4,512,128]{2,1,0:T(8,128)(2,1)} %get-tuple-element.50.refs_6_.refs_3_, ...), custom_call_target="tpu_custom_call" | custom-call | flops 100000000 | bytes 7606272 | tf_op jit(solution)/shard_map/pallas_call | solution.py:116
  149.9 5.3 %all-to-all-start.5 = ((bf16[128,16,128]{2,1,0:T(8,128)(2,1)}), bf16[128,16,128]{2,1,0:T(8,128)(2,1)S(1)}, u32[]{:S(2)}, u32[]{:S(2)}) async-start(bf16[128,16,128]{2,1,0:T(8,128)(2,1)} %bitcast.18), calls=%async_computation.5 | async-start | bytes 1048576 | tf_op jit(solution)/shard_map/all_to_all | solution.py:24
  155.2 2.3 %shard_map.126.refs_1_.refs_4_ = bf16[2,2,128,256]{3,2,1,0:T(8,128)(2,1)} custom-call(bf16[2,256,512]{2,1,0:T(8,128)(2,1)} %get-tuple-element.72.refs_0_, bf16[2,256,512]{2,1,0:T(8,128)(2,1)} %get-tuple-element.73.refs_1_, bf16[2048,128]{1,0:T(8,128)(2,1)} %get-tuple-element.64.refs_2_), custom_call_target="tpu_custom_call" | custom-call | flops 100000000 | bytes 1310720 | tf_op jit(solution)/shard_map/pallas_call | solution.py:116
  157.6 0.9 copy-done.2
  158.5 1.7 shard_map.127
  160.3 3.3 %collective-permute-start.12 = (bf16[2,256,256]{2,1,0:T(8,128)(2,1)}, bf16[2,256,256]{2,1,0:T(8,128)(2,1)S(1)}, u32[]{:S(2)}, u32[]{:S(2)}) collective-permute-start(bf16[2,256,256]{2,1,0:T(8,128)(2,1)} %shard_map.127), channel_id=1, source_target_pairs={{0,1},{1,0},{2,3},{3,2},{4,5},{5,4},{6,7},{7,6},{8,9},{9,8},{10,11... | collective-permute-start | bytes 786440 | tf_op jit(solution)/shard_map/ppermute | solution.py:28
  163.6 9.1 %collective-permute-done.12.refs_2_ = bf16[2,256,256]{2,1,0:T(8,128)(2,1)S(1)} collective-permute-done((bf16[2,256,256]{2,1,0:T(8,128)(2,1)}, bf16[2,256,256]{2,1,0:T(8,128)(2,1)S(1)}, u32[]{:S(2)}, u32[]{:S(2)}) %collective-permute-start.12) | collective-permute-done | bytes 262176 | tf_op jit(solution)/shard_map/ppermute | solution.py:28
  172.7 0.7 copy-done.12
  173.4 2.5 %shard_map.128.refs_4_ = bf16[4,2,128,256]{3,2,1,0:T(8,128)(2,1)} custom-call(bf16[2048,128]{1,0:T(8,128)(2,1)S(1)} %bitcast.32, bf16[8,256,256]{2,1,0:T(8,128)(2,1)} %bitcast.37, bf16[2,256,256]{2,1,0:T(8,128)(2,1)} %copy-done.12, f32[2,512]{1,0:T(2,128)} %get-tuple-element.46.refs_2_.refs_8_.refs_3_, bf16[2,2,128,256]{3,2,1,0:T(8,128)(2,1)} %shard_map.126.refs_1_.refs_4_), custom_call_target="tpu_custom_call" | custom-call | flops 100000000 | bytes 1839104 | tf_op jit(solution)/shard_map/pallas_call | solution.py:116
  175.8 4.2 %all-to-all-start.6 = ((bf16[4,2,128,256]{3,2,1,0:T(8,128)(2,1)}), bf16[4,2,128,256]{3,2,1,0:T(8,128)(2,1)S(1)}, u32[]{:S(2)}, u32[]{:S(2)}) async-start(bf16[4,2,128,256]{3,2,1,0:T(8,128)(2,1)} %shard_map.128.refs_4_), calls=%async_computation.6 | async-start | bytes 1048576 | tf_op jit(solution)/shard_map/all_to_all | solution.py:658
  180.0 2.0 shard_map.129
  182.0 0.6 copy-done.5
  182.7 0.0 collective-permute-start.13
  182.7 3.2 %collective-permute-start.14 = (bf16[2,128,256]{2,1,0:T(8,128)(2,1)S(1)}, bf16[2,128,256]{2,1,0:T(8,128)(2,1)S(1)}, u32[]{:S(2)}, u32[]{:S(2)}) collective-permute-start(bf16[2,128,256]{2,1,0:T(8,128)(2,1)S(1)} %get-tuple-element.78), channel_id=1, source_target_pairs={{0,1},{1,0},{2,3},{3,2},{4,5},{5,4},{6,7},{7,6},{8,9},{9,8},{10,11... | collective-permute-start | bytes 393224 | tf_op jit(solution)/shard_map/ppermute | solution.py:28
  185.9 0.4 collective-permute-start.15
  186.3 5.9 %collective-permute-done.14.refs_2_ = bf16[2,128,256]{2,1,0:T(8,128)(2,1)S(1)} collective-permute-done((bf16[2,128,256]{2,1,0:T(8,128)(2,1)S(1)}, bf16[2,128,256]{2,1,0:T(8,128)(2,1)S(1)}, u32[]{:S(2)}, u32[]{:S(2)}) %collective-permute-start.14) | collective-permute-done | bytes 131104 | tf_op jit(solution)/shard_map/ppermute | solution.py:28
  192.2 3.1 %collective-permute-done.15.refs_3_ = bf16[2,128,256]{2,1,0:T(8,128)(2,1)S(1)} collective-permute-done((bf16[2,128,256]{2,1,0:T(8,128)(2,1)S(1)}, bf16[2,128,256]{2,1,0:T(8,128)(2,1)S(1)}, u32[]{:S(2)}, u32[]{:S(2)}) %collective-permute-start.15) | collective-permute-done | bytes 131104 | tf_op jit(solution)/shard_map/ppermute | solution.py:649
  195.3 0.7 copy-done.15
  195.9 2.0 shard_map.130
  197.9 1.1 bitcast_convert_fusion
  (38 shorter events, 0.1 us)
Async XLA Ops:
  0.6 12.6 %copy-start = (bf16[1,8,256,256]{3,2,1,0:T(8,128)(2,1)S(1)}, bf16[1,8,256,256]{3,2,1,0:T(8,128)(2,1)}, u32[]{:S(2)}) copy-start(bf16[1,8,256,256]{3,2,1,0:T(8,128)(2,1)} %param.14) | copy-start | bytes 3145732
  0.6 12.6 %collective-permute-start.1 = (bf16[8,256,256]{2,1,0:T(8,128)(2,1)}, bf16[8,256,256]{2,1,0:T(8,128)(2,1)S(1)}, u32[]{:S(2)}, u32[]{:S(2)}) collective-permute-start(bf16[8,256,256]{2,1,0:T(8,128)(2,1)} %bitcast.27), channel_id=1, source_target_pairs={{0,64},{64,0},{1,65},{65,1},{2,66},{66,2},{3,67},{67,3},{4,68},{68... | collective-permute-start | bytes 3145736 | tf_op jit(solution)/shard_map/ppermute | solution.py:28
  4.4 23.5 %copy-start.6 = (f32[2,256]{1,0:T(2,128)}, f32[2,256]{1,0:T(2,128)S(1)}, u32[]{:S(2)}) copy-start(f32[2,256]{1,0:T(2,128)S(1)} %get-tuple-element.43.refs_2_.refs_6_) | copy-start | bytes 6148
  4.4 18.9 %collective-permute-start.2 = (bf16[2560,128]{1,0:T(8,128)(2,1)}, bf16[2560,128]{1,0:T(8,128)(2,1)}, u32[]{:S(2)}, u32[]{:S(2)}) collective-permute-start(bf16[2560,128]{1,0:T(8,128)(2,1)} %get-tuple-element.44.refs_0_), channel_id=1, source_target_pairs={{0,33},{1,32},{2,35},{3,34},{4,37},{5,36},{6,39},{7,38},{8,41},{9,... | collective-permute-start | bytes 1966088 | tf_op jit(solution)/shard_map/ppermute | solution.py:503
  5.9 25.9 %collective-permute-start.5 = (bf16[8,256,256]{2,1,0:T(8,128)(2,1)}, bf16[8,256,256]{2,1,0:T(8,128)(2,1)}, u32[]{:S(2)}, u32[]{:S(2)}) collective-permute-start(bf16[8,256,256]{2,1,0:T(8,128)(2,1)} %bitcast.38), channel_id=1, source_target_pairs={{0,64},{64,0},{1,65},{65,1},{2,66},{66,2},{3,67},{67,3},{4,68},{68... | collective-permute-start | bytes 3145736 | tf_op jit(solution)/shard_map/ppermute | solution.py:28
  10.6 2.6 %collective-permute-start = (f32[1,256]{1,0:T(1,128)}, f32[1,256]{1,0:T(1,128)S(1)}, u32[]{:S(2)}, u32[]{:S(2)}) collective-permute-start(f32[1,256]{1,0:T(1,128)} %refs_6_.1), channel_id=1, source_target_pairs={{0,64},{64,0},{1,65},{65,1},{2,66},{66,2},{3,67},{67,3},{4,68},{68... | collective-permute-start | bytes 3080 | tf_op jit(solution)/shard_map/ppermute | solution.py:28
  13.3 1.8 copy-start.1
  15.1 26.1 %all-to-all-start = ((bf16[128,32,128]{2,1,0:T(8,128)(2,1)}), bf16[128,32,128]{2,1,0:T(8,128)(2,1)S(1)}, u32[]{:S(2)}, u32[]{:S(2)}) async-start(bf16[128,32,128]{2,1,0:T(8,128)(2,1)} %bitcast.6), calls=%async_computation | async-start | bytes 2097152 | tf_op jit(solution)/shard_map/all_to_all | solution.py:24
  22.0 9.8 %collective-permute-start.3 = (bf16[2560,128]{1,0:T(8,128)(2,1)}, bf16[2560,128]{1,0:T(8,128)(2,1)S(1)}, u32[]{:S(2)}, u32[]{:S(2)}) collective-permute-start(bf16[2560,128]{1,0:T(8,128)(2,1)} %get-tuple-element.44.refs_0_), channel_id=1, source_target_pairs={{0,64},{1,65},{2,66},{3,67},{4,68},{5,69},{6,70},{7,71},{8,72},{9,... | collective-permute-start | bytes 1966088 | tf_op jit(solution)/shard_map/ppermute | solution.py:506
  23.3 8.5 %collective-permute-start.4 = (bf16[2560,128]{1,0:T(8,128)(2,1)}, bf16[2560,128]{1,0:T(8,128)(2,1)S(1)}, u32[]{:S(2)}, u32[]{:S(2)}) collective-permute-start(bf16[2560,128]{1,0:T(8,128)(2,1)} %collective-permute-done.2.refs_1_), channel_id=1, source_target_pairs={{0,64},{1,65},{2,66},{3,67},{4,68},{5,69},{6,70},{7,71},{8,72},{9,... | collective-permute-start | bytes 1966088 | tf_op jit(solution)/shard_map/ppermute | solution.py:506
  24.6 5.1 %collective-permute-start.6 = (f32[2,256]{1,0:T(2,128)S(1)}, f32[2,256]{1,0:T(2,128)S(1)}, u32[]{:S(2)}, u32[]{:S(2)}) collective-permute-start(f32[2,256]{1,0:T(2,128)S(1)} %get-tuple-element.43.refs_2_.refs_6_), channel_id=1, source_target_pairs={{0,33},{1,32},{2,35},{3,34},{4,37},{5,36},{6,39},{7,38},{8,41},{9,... | collective-permute-start | bytes 6152 | tf_op jit(solution)/shard_map/ppermute | solution.py:503
  27.9 3.1 %collective-permute-start.7 = (f32[2,256]{1,0:T(2,128)S(1)}, f32[2,256]{1,0:T(2,128)S(1)}, u32[]{:S(2)}, u32[]{:S(2)}) collective-permute-start(f32[2,256]{1,0:T(2,128)S(1)} %get-tuple-element.43.refs_2_.refs_6_), channel_id=1, source_target_pairs={{0,64},{64,0},{1,65},{65,1},{2,66},{66,2},{3,67},{67,3},{4,68},{68... | collective-permute-start | bytes 6152 | tf_op jit(solution)/shard_map/ppermute | solution.py:28
  29.7 2.2 %copy-start.16 = (f32[2,256]{1,0:T(2,128)}, f32[2,256]{1,0:T(2,128)S(1)}, u32[]{:S(2)}) copy-start(f32[2,256]{1,0:T(2,128)S(1)} %collective-permute-done.6.refs_7_) | copy-start | bytes 6148
  29.7 2.2 %collective-permute-start.8 = (f32[2,256]{1,0:T(2,128)S(1)}, f32[2,256]{1,0:T(2,128)S(1)}, u32[]{:S(2)}, u32[]{:S(2)}) collective-permute-start(f32[2,256]{1,0:T(2,128)S(1)} %collective-permute-done.6.refs_7_), channel_id=1, source_target_pairs={{0,64},{64,0},{1,65},{65,1},{2,66},{66,2},{3,67},{67,3},{4,68},{68... | collective-permute-start | bytes 6152 | tf_op jit(solution)/shard_map/ppermute | solution.py:28
  31.0 0.9 copy-start.17
  31.8 0.6 copy-start.18
  31.8 0.8 copy-start.8
  32.7 0.8 copy-start.9
  48.0 21.8 %all-to-all-start.1 = ((bf16[128,16,128]{2,1,0:T(8,128)(2,1)}), bf16[128,16,128]{2,1,0:T(8,128)(2,1)S(1)}, u32[]{:S(2)}, u32[]{:S(2)}) async-start(bf16[128,16,128]{2,1,0:T(8,128)(2,1)} %bitcast.9), calls=%async_computation.1 | async-start | bytes 1048576 | tf_op jit(solution)/shard_map/all_to_all | solution.py:24
  57.0 24.4 %collective-permute-start.9 = (bf16[2560,128]{1,0:T(8,128)(2,1)}, bf16[2560,128]{1,0:T(8,128)(2,1)S(1)}, u32[]{:S(2)}, u32[]{:S(2)}) collective-permute-start(bf16[2560,128]{1,0:T(8,128)(2,1)} %get-tuple-element.44.refs_0_), channel_id=1, source_target_pairs={{64,97},{65,96},{66,99},{67,98},{68,101},{69,100},{70,103},{71,102... | collective-permute-start | bytes 1966088 | tf_op jit(solution)/shard_map/ppermute | solution.py:503
  64.9 1.0 copy-start.4
  73.1 23.5 %all-to-all-start.2 = ((bf16[128,32,128]{2,1,0:T(8,128)(2,1)}), bf16[128,32,128]{2,1,0:T(8,128)(2,1)S(1)}, u32[]{:S(2)}, u32[]{:S(2)}) async-start(bf16[128,32,128]{2,1,0:T(8,128)(2,1)} %bitcast.12), calls=%async_computation.2 | async-start | bytes 2097152 | tf_op jit(solution)/shard_map/all_to_all | solution.py:24
  78.4 4.9 %collective-permute-start.10 = (bf16[2560,128]{1,0:T(8,128)(2,1)}, bf16[2560,128]{1,0:T(8,128)(2,1)S(1)}, u32[]{:S(2)}, u32[]{:S(2)}) collective-permute-start(bf16[2560,128]{1,0:T(8,128)(2,1)} %get-tuple-element.44.refs_0_), channel_id=1, source_target_pairs={{64,0},{65,1},{66,2},{67,3},{68,4},{69,5},{70,6},{71,7},{72,8},{73... | collective-permute-start | bytes 1966088 | tf_op jit(solution)/shard_map/ppermute | solution.py:506
  81.4 3.0 %copy-start.7 = (bf16[2560,128]{1,0:T(8,128)(2,1)}, bf16[2560,128]{1,0:T(8,128)(2,1)S(1)}, u32[]{:S(2)}) copy-start(bf16[2560,128]{1,0:T(8,128)(2,1)S(1)} %collective-permute-done.9.refs_1_) | copy-start | bytes 1966084
  81.4 3.0 %collective-permute-start.11 = (bf16[2560,128]{1,0:T(8,128)(2,1)S(1)}, bf16[2560,128]{1,0:T(8,128)(2,1)S(1)}, u32[]{:S(2)}, u32[]{:S(2)}) collective-permute-start(bf16[2560,128]{1,0:T(8,128)(2,1)S(1)} %collective-permute-done.9.refs_1_), channel_id=1, source_target_pairs={{64,0},{65,1},{66,2},{67,3},{68,4},{69,5},{70,6},{71,7},{72,8},{73... | collective-permute-start | bytes 1966088 | tf_op jit(solution)/shard_map/ppermute | solution.py:506
  83.3 1.2 copy-start.10
  84.4 0.8 copy-start.11
  125.3 18.2 %all-to-all-start.4 = ((bf16[128,16,128]{2,1,0:T(8,128)(2,1)}), bf16[128,16,128]{2,1,0:T(8,128)(2,1)S(1)}, u32[]{:S(2)}, u32[]{:S(2)}) async-start(bf16[128,16,128]{2,1,0:T(8,128)(2,1)} %bitcast.16), calls=%async_computation.4 | async-start | bytes 1048576 | tf_op jit(solution)/shard_map/all_to_all | solution.py:24
  133.0 1.0 copy-start.3
  149.9 22.7 %all-to-all-start.5 = ((bf16[128,16,128]{2,1,0:T(8,128)(2,1)}), bf16[128,16,128]{2,1,0:T(8,128)(2,1)S(1)}, u32[]{:S(2)}, u32[]{:S(2)}) async-start(bf16[128,16,128]{2,1,0:T(8,128)(2,1)} %bitcast.18), calls=%async_computation.5 | async-start | bytes 1048576 | tf_op jit(solution)/shard_map/all_to_all | solution.py:24
  157.6 1.0 copy-start.2
  160.3 12.4 %collective-permute-start.12 = (bf16[2,256,256]{2,1,0:T(8,128)(2,1)}, bf16[2,256,256]{2,1,0:T(8,128)(2,1)S(1)}, u32[]{:S(2)}, u32[]{:S(2)}) collective-permute-start(bf16[2,256,256]{2,1,0:T(8,128)(2,1)} %shard_map.127), channel_id=1, source_target_pairs={{0,1},{1,0},{2,3},{3,2},{4,5},{5,4},{6,7},{7,6},{8,9},{9,8},{10,11... | collective-permute-start | bytes 786440 | tf_op jit(solution)/shard_map/ppermute | solution.py:28
  172.7 0.7 copy-start.12
  175.8 22.1 %all-to-all-start.6 = ((bf16[4,2,128,256]{3,2,1,0:T(8,128)(2,1)}), bf16[4,2,128,256]{3,2,1,0:T(8,128)(2,1)S(1)}, u32[]{:S(2)}, u32[]{:S(2)}) async-start(bf16[4,2,128,256]{3,2,1,0:T(8,128)(2,1)} %shard_map.128.refs_4_), calls=%async_computation.6 | async-start | bytes 1048576 | tf_op jit(solution)/shard_map/all_to_all | solution.py:658
  182.0 0.7 copy-start.5
  182.7 3.6 %collective-permute-start.13 = (bf16[2,128,256]{2,1,0:T(8,128)(2,1)S(1)}, bf16[2,128,256]{2,1,0:T(8,128)(2,1)S(1)}, u32[]{:S(2)}, u32[]{:S(2)}) collective-permute-start(bf16[2,128,256]{2,1,0:T(8,128)(2,1)S(1)} %get-tuple-element.77), channel_id=1, source_target_pairs={{0,64},{64,0},{1,65},{65,1},{2,66},{66,2},{3,67},{67,3},{4,68},{68... | collective-permute-start | bytes 393224 | tf_op jit(solution)/shard_map/ppermute | solution.py:28
  182.7 9.5 %collective-permute-start.14 = (bf16[2,128,256]{2,1,0:T(8,128)(2,1)S(1)}, bf16[2,128,256]{2,1,0:T(8,128)(2,1)S(1)}, u32[]{:S(2)}, u32[]{:S(2)}) collective-permute-start(bf16[2,128,256]{2,1,0:T(8,128)(2,1)S(1)} %get-tuple-element.78), channel_id=1, source_target_pairs={{0,1},{1,0},{2,3},{3,2},{4,5},{5,4},{6,7},{7,6},{8,9},{9,8},{10,11... | collective-permute-start | bytes 393224 | tf_op jit(solution)/shard_map/ppermute | solution.py:28
  185.9 9.4 %collective-permute-start.15 = (bf16[2,128,256]{2,1,0:T(8,128)(2,1)S(1)}, bf16[2,128,256]{2,1,0:T(8,128)(2,1)S(1)}, u32[]{:S(2)}, u32[]{:S(2)}) collective-permute-start(bf16[2,128,256]{2,1,0:T(8,128)(2,1)S(1)} %get-tuple-element.79), channel_id=1, source_target_pairs={{0,65},{1,64},{64,1},{65,0},{2,67},{3,66},{66,3},{67,2},{4,69},{5,... | collective-permute-start | bytes 393224 | tf_op jit(solution)/shard_map/ppermute | solution.py:649
  186.3 9.0 %copy-start.13 = (bf16[2,128,256]{2,1,0:T(8,128)(2,1)}, bf16[2,128,256]{2,1,0:T(8,128)(2,1)S(1)}, u32[]{:S(2)}) copy-start(bf16[2,128,256]{2,1,0:T(8,128)(2,1)S(1)} %collective-permute-done.13.refs_1_) | copy-start | bytes 393220
  192.2 3.1 %copy-start.14 = (bf16[2,128,256]{2,1,0:T(8,128)(2,1)}, bf16[2,128,256]{2,1,0:T(8,128)(2,1)S(1)}, u32[]{:S(2)}) copy-start(bf16[2,128,256]{2,1,0:T(8,128)(2,1)S(1)} %collective-permute-done.14.refs_2_) | copy-start | bytes 393220
  195.3 0.7 copy-start.15
